TPU v7x, 128 devices: a whole 4x4x4 slice. The times are simulated.
128 devices in a mesh: tm: 8 (over x, core), tile: 16 (over y, z).
Axes of the slice: x: 4, y: 4, z: 4, core: 2. Of those that a mesh axis runs over, the one named last changes fastest.
Arguments:
- movie_frames: bfloat16 [1024, 32, 4096], P(('tm', 'tile')), may hold values from -6 to 6
- baseline: float32 [32, 4096], replicated, may hold values from -3 to 3
- footprints: bfloat16 [64, 32, 4096], P(None, 'tile'), as said below
- traces: float32 [640, 1024], P('tile', 'tm'), may hold values from 0 to 1
- intersection: int32 [32, 64], P('tile'), may hold values from 0 to 639, as said below
- counts: int32 [32], P('tile'), may hold values from 20 to 64
- offsets: int32 [8, 2], replicated, may hold values from -12 to 12, as said below
- cycle_coef: float32 [8], replicated, may hold values from 0.05 to 0.2
- decay_rate: float32 [640], P('tile'), may hold values from 0.9 to 0.9985
- rise_rate: float32 [640], P('tile'), may hold values from 0.1 to 0.6
- penalty: float32 [640], P('tile'), may hold values from 0.05 to 0.3
Outputs:
- neuron_traces: float32 [640, 1024], P('tile', 'tm')
- neuron_shapes: bfloat16 [64, 32, 4096], P(None, 'tile')
- backdrop: bfloat16 [1024, 32, 4096], P(('tm', 'tile'))
Inputs may be any that keep to these rules, and one draw needn't show every extreme that they name: `intersection`: slot s < 20 of tile t names neuron (t // 2) * 40 + s * 2 + t % 2; other slots may name any neuron, repeats allowed. |offsets[r, 0]| + |offsets[r, 1]| = 12 for every r. `footprints`: every entry is positive.
All inputs are finite; a program needn't handle non-finite values.
Results may differ from a plain program's by a relative error of at most 0.0034.
Values may be sent and summed in bfloat16 or wider, within the bound.
No kernel may reach another device: no remote copies, remote signals or barrier semaphores. Data moves between devices by JAX's collectives and lax.ppermute only.
A program may use at most 128 MiB of HBM per device.

v0:
```python
import math

import jax
import jax.numpy as jnp
from jax import lax
from jax.sharding import PartitionSpec as P

TSIDE = 64
GRID_W = 8
RAD = 12
ITERS = 2


EPSILON = 1e-06
PRECISE = lax.Precision.HIGHEST


def passed_along(value, axis, steps):
    count = lax.axis_size(axis)
    initial, last = (max(0, -steps), min(count, count - steps))
    return lax.ppermute(value, axis, [(source, source + steps) for source in range(initial, last)])


def from_everyone(x, axis):
    copies = jnp.broadcast_to(x, (lax.axis_size(axis), *x.shape))
    return lax.all_to_all(copies, axis, split_axis=0, concat_axis=0, tiled=True)


def gathered_once(x, axis):
    leaves = jax.tree.leaves(x)
    order = sorted(range(len(leaves)), key=lambda k: -leaves[k].size)
    width = (1, *leaves[order[0]].shape)[-1]
    lines = [
        jnp.pad(leaves[k].reshape(-1), (0, -leaves[k].size % width)).reshape(-1, width)
        for k in order
    ]
    both, at, found = (from_everyone(jnp.concatenate(lines), axis), 0, {})
    for k, line in zip(order, lines):
        slab = both[:, at : at + len(line)].reshape(len(both), -1)
        found[k] = slab[:, : leaves[k].size].reshape(-1, *leaves[k].shape)
        at += len(line)
    numbers = iter(range(len(leaves)))
    return jax.tree.map(lambda _: found[next(numbers)], x)


def gathered_by_type(x, axis):
    leaves, found = (jax.tree.leaves(x), {})
    for initial, a in enumerate(leaves):
        if initial not in found:
            alike = [k for k, b in enumerate(leaves) if b.dtype == a.dtype]
            got = (
                gathered_once([leaves[k] for k in alike], axis)
                if len(alike) > 1
                else [from_everyone(a, axis)]
            )
            for k, b in zip(alike, got):
                found[k] = b
    numbers = iter(range(len(leaves)))
    return jax.tree.map(lambda _: found[next(numbers)], x)


def combined_pairwise(pieces, combine):
    while len(jax.tree.leaves(pieces)[0]) > 1:
        pieces = jax.vmap(combine)(
            *(jax.tree.map(lambda part: part[side::2], pieces) for side in (0, 1))
        )
    return jax.tree.map(lambda part: part[0], pieces)


def entering_2(x, axis, combine, identity):
    count, mine = (lax.axis_size(axis), lax.axis_index(axis))
    passed = jnp.arange(count) < mine

    def kept(part, zero, own):
        part = jnp.where(
            passed.reshape(-1, *(1 for _ in own.shape)), part, jnp.asarray(zero, own.dtype)
        )
        return part

    pieces = gathered_by_type(x, axis)
    return combined_pairwise(jax.tree.map(kept, pieces, identity, x), combine)


def laid_out(blocks, dim):
    dims = list(blocks.shape[1:])
    dims[dim] *= blocks.shape[0]
    return jnp.moveaxis(blocks, 0, dim).reshape(dims)


def gathered_copies(x, axis, dim):
    return laid_out(from_everyone(x, axis), dim)


def cut_along(x, dim, count):
    dims = x.shape
    blocks = x.reshape(*dims[:dim], count, dims[dim] // count, *dims[dim + 1 :])
    return jnp.moveaxis(blocks, dim, 0)


def sent_and_summed(x, axis, dim):
    blocks = cut_along(x, dim, lax.axis_size(axis))
    arrived = lax.all_to_all(blocks, axis, split_axis=0, concat_axis=0, tiled=True)
    return arrived.sum(axis=0)


def in_one_piece(arrays, axis, dim, along):
    widths = [math.prod(a.shape[along:]) for a in arrays]
    both = jnp.concatenate(
        [a.reshape(*a.shape[:along], w) for a, w in zip(arrays, widths)], axis=along
    )
    result = sent_and_summed(both, axis, dim)
    blocks = jnp.split(result, [sum(widths[:k]) for k in range(1, len(widths))], axis=along)
    return tuple(
        (b.reshape(*result.shape[:along], *a.shape[along:]) for a, b in zip(arrays, blocks))
    )


def of_everyone(x, axis):
    return from_everyone(x, axis).sum(axis=0)


def cycle_sum(padded, shape, offsets, cycle_coef):
    summed = jnp.zeros(shape, jnp.float32)
    anchor = jnp.zeros((), jnp.int32)
    for cycle_index in range(offsets.shape[0]):
        row_start = offsets[cycle_index, 0] + RAD
        col_start = offsets[cycle_index, 1] + RAD
        shifted = lax.dynamic_slice(padded, (anchor, row_start, col_start), shape)
        summed = summed + cycle_coef[cycle_index] * shifted.astype(jnp.float32)
    return summed


def neighbour(piece, by, keep):
    moved = passed_along(piece, "tile", by)
    return moved * keep


def rim_background(leftover, offsets, cycle_coef):
    frame_count, tile_dev, pixels = leftover.shape
    across = GRID_W // tile_dev
    column = lax.axis_index("tile") % across
    keep_left = jnp.where(column > 0, 1.0, 0.0).astype(jnp.bfloat16)
    keep_right = jnp.where(column < across - 1, 1.0, 0.0).astype(jnp.bfloat16)
    keep_all = jnp.ones((), jnp.bfloat16)
    picture = leftover.reshape(frame_count, tile_dev, TSIDE, TSIDE).transpose(0, 2, 1, 3)
    picture = picture.reshape(frame_count, TSIDE, tile_dev * TSIDE)
    upper_left = neighbour(picture[:, -RAD:, -RAD:], across + 1, keep_left)
    upper = neighbour(picture[:, -RAD:, :], across, keep_all)
    upper_right = neighbour(picture[:, -RAD:, :RAD], across - 1, keep_right)
    left_side = neighbour(picture[:, :, -RAD:], 1, keep_left)
    right_side = neighbour(picture[:, :, :RAD], -1, keep_right)
    lower_left = neighbour(picture[:, :RAD, -RAD:], -(across - 1), keep_left)
    lower = neighbour(picture[:, :RAD, :], -across, keep_all)
    lower_right = neighbour(picture[:, :RAD, :RAD], -(across + 1), keep_right)
    top_band = jnp.concatenate([upper_left, upper, upper_right], axis=2)
    mid_band = jnp.concatenate([left_side, picture, right_side], axis=2)
    low_band = jnp.concatenate([lower_left, lower, lower_right], axis=2)
    padded = jnp.concatenate([top_band, mid_band, low_band], axis=1)
    summed = cycle_sum(padded, picture.shape, offsets, cycle_coef)
    summed = summed.reshape(frame_count, TSIDE, tile_dev, TSIDE).transpose(0, 2, 1, 3)
    return summed.reshape(frame_count, tile_dev, pixels)


def response(decay_rate, rise_rate, delays):
    extra_dims = (1,) * delays.ndim
    decay_wide = decay_rate.reshape(decay_rate.shape + extra_dims)
    rise_wide = rise_rate.reshape(rise_rate.shape + extra_dims)
    powers = (delays + 1).astype(jnp.float32)[None]
    result = (jnp.exp(powers * jnp.log(decay_wide)) - jnp.exp(powers * jnp.log(rise_wide))) / (
        decay_wide - rise_wide
    )
    return jnp.where(delays[None] >= 0, result, 0.0)


def combine_maps(before_map, after_map):
    before_mat, before_vec = before_map
    after_mat, after_vec = after_map
    top_left = after_mat[0] * before_mat[0] + after_mat[1] * before_mat[2]
    top_right = after_mat[0] * before_mat[1] + after_mat[1] * before_mat[3]
    low_left = after_mat[2] * before_mat[0] + after_mat[3] * before_mat[2]
    low_right = after_mat[2] * before_mat[1] + after_mat[3] * before_mat[3]
    out_upper = after_mat[0] * before_vec[0] + after_mat[1] * before_vec[1] + after_vec[0]
    out_lower = after_mat[2] * before_vec[0] + after_mat[3] * before_vec[1] + after_vec[1]
    return (
        jnp.stack([top_left, top_right, low_left, low_right]),
        jnp.stack([out_upper, out_lower]),
    )


def calcium_filter(rectified, decay_rate, rise_rate):
    length = rectified.shape[1]
    delays = jnp.arange(length, dtype=jnp.int32)
    coef_one = decay_rate + rise_rate
    coef_two = -decay_rate * rise_rate
    unit_gain = (1.0 - decay_rate) * (1.0 - rise_rate)
    kernel = response(decay_rate, rise_rate, delays[:, None] - delays[None, :])
    forced = jnp.einsum(
        "ktu,ku->kt", kernel * unit_gain[:, None, None], rectified, precision=PRECISE
    )
    current = response(decay_rate, rise_rate, delays)
    earlier = response(decay_rate, rise_rate, delays - 1)
    matrices = jnp.stack(
        [
            current[:, -1] * coef_one + current[:, -2] * coef_two,
            current[:, -1] * coef_two,
            current[:, -2] * coef_one + current[:, -3] * coef_two,
            current[:, -2] * coef_two,
        ]
    )
    vector = jnp.stack([forced[:, -1], forced[:, -2]])
    ones_row = jnp.ones_like(decay_rate)
    zeros_row = jnp.zeros_like(decay_rate)
    identity = (jnp.stack([ones_row, zeros_row, zeros_row, ones_row]), jnp.zeros_like(vector))
    _, entering = entering_2((matrices, vector), "tm", combine_maps, identity)
    leading = coef_one * entering[0] + coef_two * entering[1]
    return forced + current * leading[:, None] + earlier * (coef_two * entering[0])[:, None]


def collect(traces, selector):
    rounded = traces.astype(jnp.bfloat16)
    summed = jnp.einsum(
        "tsk,kf->tsf",
        selector,
        gathered_copies(rounded, "tile", 0),
        preferred_element_type=jnp.float32,
    )
    return summed.astype(jnp.bfloat16)


def body(
    movie_frames,
    baseline,
    footprints,
    traces,
    intersection,
    counts,
    offsets,
    cycle_coef,
    decay_rate,
    rise_rate,
    penalty,
):
    slot_count, tile_dev, pixels = footprints.shape
    neurons = traces.shape[0] * lax.axis_size("tile")
    first_tile = lax.axis_index("tile") * tile_dev
    baseline_here = lax.dynamic_slice_in_dim(baseline, first_tile, tile_dev, 0)
    occupied = jnp.arange(slot_count, dtype=jnp.int32)[None, :] < counts[:, None]
    chosen = (
        intersection[:, :, None] == jnp.arange(neurons, dtype=jnp.int32)[None, None, :]
    ) & occupied[:, :, None]
    selector = chosen.astype(jnp.bfloat16)
    picker = chosen.astype(jnp.float32)
    occupied_rows = occupied.T.astype(jnp.float32)[:, :, None]
    footprint = footprints * occupied_rows.astype(jnp.bfloat16)
    local_movie = lax.all_to_all(movie_frames, "tile", split_axis=1, concat_axis=0, tiled=True)
    slot_rows = collect(traces, selector)
    backdrop_tiles = jnp.zeros(local_movie.shape, jnp.bfloat16)
    for iteration in range(ITERS):
        rebuilt = jnp.einsum(
            "tsf,stp->ftp", slot_rows, footprint, preferred_element_type=jnp.float32
        )
        leftover = (local_movie.astype(jnp.float32) - baseline_here[None] - rebuilt).astype(
            jnp.bfloat16
        )
        backdrop_tiles = rim_background(leftover, offsets, cycle_coef).astype(jnp.bfloat16)
        clean = (
            local_movie.astype(jnp.float32)
            - baseline_here[None]
            - backdrop_tiles.astype(jnp.float32)
        )
        misfit = (clean - rebuilt).astype(jnp.bfloat16)
        shapes_float = footprint.astype(jnp.float32)
        spread = jnp.sum(shapes_float, axis=0)
        projection = jnp.einsum(
            "stp,ftp->tsf", footprint, misfit, preferred_element_type=jnp.float32
        )
        majorizer = jnp.einsum("stp,tp->ts", shapes_float, spread, precision=PRECISE)
        neuron_terms = jnp.einsum("tsk,tsf->kf", picker, projection, precision=PRECISE)
        neuron_scale = jnp.einsum("tsk,ts->k", picker, majorizer, precision=PRECISE)
        gradient, curvature = in_one_piece((neuron_terms, neuron_scale), "tile", 0, 1)
        stepped = traces + gradient / (curvature + EPSILON)[:, None]
        rectified = jnp.maximum(stepped - penalty[:, None], 0.0)
        traces = calcium_filter(rectified, decay_rate, rise_rate)
        slot_rows = collect(traces, selector)
        rebuilt = jnp.einsum(
            "tsf,stp->ftp", slot_rows, footprint, preferred_element_type=jnp.float32
        )
        misfit = (clean - rebuilt).astype(jnp.bfloat16)
        slot_float = slot_rows.astype(jnp.float32)
        cluster = jnp.sum(slot_float, axis=1)
        weight_part = jnp.einsum("tsf,tf->ts", slot_float, cluster, precision=PRECISE)
        share = slot_count // lax.axis_size("tm")
        numerator = sent_and_summed(
            jnp.einsum("tsf,ftp->stp", slot_rows, misfit, preferred_element_type=jnp.float32),
            "tm",
            0,
        )
        weight = of_everyone(weight_part, "tm")
        first_slot = lax.axis_index("tm") * share
        divisor = jnp.maximum(
            lax.dynamic_slice_in_dim(weight.T, first_slot, share, 0), jnp.float32(1.0)
        )
        current_rows = lax.dynamic_slice_in_dim(shapes_float, first_slot, share, 0)
        mask_rows = lax.dynamic_slice_in_dim(occupied_rows, first_slot, share, 0)
        updated = (
            jnp.maximum(current_rows + numerator / divisor[:, :, None], 0.0) * mask_rows
        ).astype(jnp.bfloat16)
        footprint = gathered_copies(updated, "tm", 0)
    backdrop = lax.all_to_all(backdrop_tiles, "tile", split_axis=0, concat_axis=1, tiled=True)
    return (traces, footprint, backdrop)


def solution(mesh):
    in_specs = (
        P(("tm", "tile"), None, None),
        P(),
        P(None, "tile", None),
        P("tile", "tm"),
        P("tile", None),
        P("tile"),
        P(),
        P(),
        P("tile"),
        P("tile"),
        P("tile"),
    )
    out_specs = (P("tile", "tm"), P(None, "tile", None), P(("tm", "tile"), None, None))
    return jax.shard_map(body, mesh=mesh, in_specs=in_specs, out_specs=out_specs, check_vma=False)
```

profile of v0, /device:TPU:1, one launch (start us, length us, event | category | flops | bytes accessed | tf_op | source)
XLA Modules:
  0.0 490.8 jit_solution(16160625242558441274)
XLA Ops:
  0.7 4.2 copy.111
  4.9 8.8 %all-to-all-start = ((bf16[8,32,4096]{2,0,1:T(8,128)(2,1)}), bf16[8,32,4096]{2,0,1:T(8,128)(2,1)}, u32[]{:S(2)}, u32[]{:S(2)}) async-start(bf16[8,32,4096]{2,0,1:T(8,128)(2,1)} %copy.111), calls=%async_computation | async-start | bytes 4194304 | tf_op jit(solution)/shard_map/all_to_all | solution.py:255
  38.6 3.2 all-to-all-done
  42.6 3.7 all-to-all-start.1
  46.2 4.1 copy_bitcast_fusion
  50.3 5.6 %copy.113 = f32[128,2,4096]{0,2,1:T(8,128)} copy(f32[128,2,4096]{2,0,1:T(8,128)} %copy_bitcast_fusion) | data formatting | bytes 8388608 | tf_op jit(solution)/shard_map/convert_element_type | solution.py:267
  56.0 6.0 %subtract_convert_fusion.3 = (bf16[128,2,4096]{0,2,1:T(8,128)(2,1)}, f32[128,2,4096]{0,2,1:T(8,128)}) fusion(f32[128,2,4096]{0,2,1:T(8,128)} %copy.113, f32[2,4096]{1,0:T(2,128)S(1)} %constant_dynamic-slice_fusion.3, bf16[640,128,1]{1,0,2:T(8,128)(2,1)S(1)} %bitcast.299, s32[2,64]{1,0:T(2,128)S(1)} %copy-done.13, pred[2,64]{1,0:T(4,128)(4,1)S(1)} %iota_compare_fusion.1, ...), kind=kOutput, calls=%fused_computation.20 | convolution fusion | flops 159039488 | bytes 11731840 | tf_op jit(solution)/shard_map/tsf,stp->ftp/dot_general | solution.py:259
  65.2 6.0 %collective-permute-start = (bf16[128,12,12]{0,2,1:T(8,128)(2,1)S(1)}, bf16[128,12,12]{0,2,1:T(8,128)(2,1)S(1)}, u32[]{:S(2)}, u32[]{:S(2)}) collective-permute-start(bf16[128,12,12]{0,2,1:T(8,128)(2,1)S(1)} %get-tuple-element.42), channel_id=1, source_target_pairs={{0,5},{1,6},{2,7},{3,8},{4,9},{5,10},{6,11},{7,12},{8,13},{9,14},{... | collective-permute-start | bytes 110600 | tf_op jit(solution)/shard_map/ppermute | solution.py:21
  72.5 4.9 collective-permute-start.2
  78.7 4.0 collective-permute-start.3
  82.7 4.6 collective-permute-start.1
  92.1 3.9 collective-permute-done.6
  95.9 21.6 %maximum_maximum_fusion = bf16[128,88,152]{0,2,1:T(8,128)(2,1)S(1)} fusion(bf16[128,12,12]{0,2,1:T(8,128)(2,1)S(1)} %broadcast_multiply_fusion.6, bf16[128,12,128]{0,2,1:T(8,128)(2,1)S(1)} %collective-permute-done.6, bf16[128,12,12]{0,2,1:T(8,128)(2,1)S(1)} %broadcast_multiply_fusion.10, bf16[128,64,12]{0,2,1:T(8,128)(2,1)S(1)} %broadcast_multiply_fusion.1, ...), kind=kLoop, calls=%fused_computation.21 | loop fusion | flops 30818304 | bytes 6848512 | tf_op jit(solution)/shard_map/concatenate | solution.py:158
  117.5 14.6 %add_convert_fusion.1 = bf16[128,64,128]{0,2,1:T(8,128)(2,1)S(1)} fusion(bf16[128,88,152]{0,2,1:T(8,128)(2,1)S(1)} %maximum_maximum_fusion, s32[]{:T(128)S(6)} %select_n.138, s32[]{:T(128)S(6)} %select_n.139, f32[]{:T(128)} %bitcast.45, s32[]{:T(128)S(6)} %select_n.136, s32[]{:T(128)S(6)} %select_n.137, f32[]{:T(128)} %bitcast.40, s32[]{:T(128)S(6)} %select_n.134, ...), kind=kLoop, calls=%fused_computation.19 | loop fusion | flops 25165824 | bytes 18874464 | tf_op jit(solution)/shard_map/convert_element_type | solution.py:265
  140.1 4.8 all-to-all-start.2
  144.9 9.6 %all-to-all-done.2 = f32[16,40,129]{2,1,0:T(8,128)S(1)} async-done(((f32[16,40,129]{2,1,0:T(8,128)}), f32[16,40,129]{2,1,0:T(8,128)S(1)}, u32[]{:S(2)}, u32[]{:S(2)}) %all-to-all-start.2) | async-done | bytes 330272 | tf_op jit(solution)/shard_map/all_to_all | solution.py:102
  154.8 4.9 fusion.8
  160.7 11.8 %all-to-all-start.3 = ((f32[8,1,240]{2,1,0:T(1,128)}), f32[8,1,240]{2,1,0:T(1,128)S(1)}, u32[]{:S(2)}, u32[]{:S(2)}) async-start(f32[8,1,240]{2,1,0:T(1,128)} %reshape.1445), calls=%async_computation.3 | async-start | bytes 16384 | tf_op jit(solution)/shard_map/all_to_all | solution.py:26
  172.5 4.6 all-to-all-done.3
  179.1 9.9 %all_to_all.92 = bf16[16,40,128]{2,1,0:T(8,128)(2,1)S(1)} all-to-all(bf16[16,40,128]{2,1,0:T(8,128)(2,1)S(1)} %broadcast_in_dim.146), channel_id=1, replica_groups=mesh['tm'=8,'tile'=16] {'tile'}, dimensions={0} | all-to-all | bytes 327680 | tf_op jit(solution)/shard_map/all_to_all | solution.py:26
  190.1 5.2 %all-to-all-start.6 = ((f32[8,1,128]{2,1,0:T(1,128)}), f32[8,1,128]{2,1,0:T(1,128)S(1)}, u32[]{:S(2)}, u32[]{:S(2)}) async-start(f32[8,1,128]{2,1,0:T(1,128)} %reshape.1447), calls=%async_computation.6 | async-start | bytes 8192 | tf_op jit(solution)/shard_map/all_to_all | solution.py:26
  195.3 5.3 %convolution_bitcast_fusion.5 = f32[8,8,2,4096]{3,1,0,2:T(8,128)} fusion(bf16[2,64,128]{2,1,0:T(8,128)(2,1)S(1)} %get-tuple-element.113, f32[128,2,4096]{0,2,1:T(8,128)} %copy-done.4, bf16[64,2,4096]{2,1,0:T(2,128)(2,1)S(1)} %copy-done.6, bf16[64,2]{0,1:T(2,128)(2,1)S(1)} %get-tuple-element.99), kind=kOutput, calls=%fused_computation.9 | convolution fusion | flops 271056896 | bytes 7373056 | tf_op jit(solution)/shard_map/tsf,ftp->stp/dot_general | solution.py:294
  200.7 3.2 copy.125
  203.8 4.8 all-to-all-start.5
  212.0 22.9 %all-to-all-done.5 = f32[8,8,2,4096]{3,1,2,0:T(8,128)} async-done(((f32[8,8,2,4096]{3,1,2,0:T(8,128)}), f32[8,8,2,4096]{3,1,2,0:T(8,128)}, u32[]{:S(2)}, u32[]{:S(2)}) %all-to-all-start.5) | async-done | bytes 2097184 | tf_op jit(solution)/shard_map/all_to_all | solution.py:102
  237.9 18.3 %all_to_all.93 = bf16[8,8,2,4096]{3,1,2,0:T(8,128)(2,1)S(1)} all-to-all(bf16[8,8,2,4096]{3,1,2,0:T(8,128)(2,1)S(1)} %broadcast_in_dim.148), channel_id=1, replica_groups=mesh['tm'=8,'tile'=16] {'tm'}, dimensions={0} | all-to-all | bytes 2097152 | tf_op jit(solution)/shard_map/all_to_all | solution.py:26
  256.2 4.5 subtract_convert_fusion.1
  264.3 4.8 collective-permute-start.9
  270.4 4.0 collective-permute-start.11
  274.4 5.6 %collective-permute-start.10 = (bf16[128,12,12]{0,2,1:T(8,128)(2,1)S(1)}, bf16[128,12,12]{0,2,1:T(8,128)(2,1)}, u32[]{:S(2)}, u32[]{:S(2)}) collective-permute-start(bf16[128,12,12]{0,2,1:T(8,128)(2,1)S(1)} %get-tuple-element.37), channel_id=1, source_target_pairs={{0,3},{1,4},{2,5},{3,6},{4,7},{5,8},{6,9},{7,10},{8,11},{9,12},{10... | collective-permute-start | bytes 110600 | tf_op jit(solution)/shard_map/ppermute | solution.py:21
  283.7 4.2 collective-permute-done.13
  292.0 6.2 %collective-permute-done.15 = bf16[128,12,12]{0,2,1:T(8,128)(2,1)S(1)} collective-permute-done((bf16[128,12,12]{0,2,1:T(8,128)(2,1)}, bf16[128,12,12]{0,2,1:T(8,128)(2,1)S(1)}, u32[]{:S(2)}, u32[]{:S(2)}) %collective-permute-start.15) | collective-permute-done | bytes 36896 | tf_op jit(solution)/shard_map/ppermute | solution.py:21
  298.4 19.0 %maximum_maximum_fusion.1 = bf16[128,88,152]{0,2,1:T(8,128)(2,1)S(1)} fusion(bf16[128,12,12]{0,2,1:T(8,128)(2,1)S(1)} %broadcast_multiply_fusion.4, bf16[128,12,128]{0,2,1:T(8,128)(2,1)S(1)} %collective-permute-done.14, bf16[128,12,12]{0,2,1:T(8,128)(2,1)S(1)} %broadcast_multiply_fusion.8, bf16[128,64,12]{0,2,1:T(8,128)(2,1)S(1)} %broadcast_multiply_fusion, ...), kind=kLoop, calls=%fused_computation.22 | loop fusion | flops 30818304 | bytes 6848512 | tf_op jit(solution)/shard_map/concatenate | solution.py:158
  317.4 14.8 %add_convert_fusion = bf16[128,64,128]{0,2,1:T(8,128)(2,1)S(1)} fusion(bf16[128,88,152]{0,2,1:T(8,128)(2,1)S(1)} %maximum_maximum_fusion.1, s32[]{:T(128)S(6)} %select_n.138, s32[]{:T(128)S(6)} %select_n.139, s32[]{:T(128)S(6)} %select_n.136, s32[]{:T(128)S(6)} %select_n.137, s32[]{:T(128)S(6)} %select_n.134, s32[]{:T(128)S(6)} %select_n.135, ...), kind=kLoop, calls=%fused_computation.16 | loop fusion | flops 25165824 | bytes 18874464 | tf_op jit(solution)/shard_map/convert_element_type | solution.py:265
  337.8 17.2 %all_to_all.94 = f32[16,40,129]{2,1,0:T(8,128)S(1)} all-to-all(f32[16,40,129]{2,1,0:T(8,128)S(1)} %pad_maximum_fusion.1), channel_id=1, replica_groups=mesh['tm'=8,'tile'=16] {'tile'}, dimensions={0} | all-to-all | bytes 660480 | tf_op jit(solution)/shard_map/all_to_all | solution.py:102
  355.4 4.9 fusion.7
  360.7 13.5 %all_to_all.95 = f32[8,1,240]{2,1,0:T(1,128)S(1)} all-to-all(f32[8,1,240]{2,1,0:T(1,128)S(1)} %reshape.1449), channel_id=1, replica_groups=mesh['tm'=8,'tile'=16] {'tm'}, dimensions={0} | all-to-all | bytes 15360 | tf_op jit(solution)/shard_map/all_to_all | solution.py:26
  376.2 10.1 %all_to_all.96 = bf16[16,40,128]{2,1,0:T(8,128)(2,1)S(1)} all-to-all(bf16[16,40,128]{2,1,0:T(8,128)(2,1)S(1)} %broadcast_in_dim.150), channel_id=1, replica_groups=mesh['tm'=8,'tile'=16] {'tile'}, dimensions={0} | all-to-all | bytes 327680 | tf_op jit(solution)/shard_map/all_to_all | solution.py:26
  387.4 5.2 %all-to-all-start.12 = ((f32[8,1,128]{2,1,0:T(1,128)}), f32[8,1,128]{2,1,0:T(1,128)S(1)}, u32[]{:S(2)}, u32[]{:S(2)}) async-start(f32[8,1,128]{2,1,0:T(1,128)} %reshape.1451), calls=%async_computation.12 | async-start | bytes 8192 | tf_op jit(solution)/shard_map/all_to_all | solution.py:26
  392.6 6.2 %convolution_bitcast_fusion.4 = f32[8,8,2,4096]{3,1,0,2:T(8,128)} fusion(bf16[2,64,128]{2,1,0:T(8,128)(2,1)S(1)} %get-tuple-element.117, bf16[128,2,4096]{0,2,1:T(8,128)(2,1)} %bitcast.279, f32[128,2,4096]{0,2,1:T(8,128)} %copy.113, f32[2,4096]{1,0:T(2,128)S(1)} %constant_dynamic-slice_fusion.3, bf16[8,8,2,4096]{3,1,2,0:T(8,128)(2,1)S(1)} %all_to_all.93), kind=kOutput, calls=%fused_computation.8 | convolution fusion | flops 273678336 | bytes 9502720 | tf_op jit(solution)/shard_map/tsf,ftp->stp/dot_general | solution.py:294
  398.7 3.2 copy.135
  401.9 4.8 all-to-all-start.11
  406.7 6.2 %copy.138 = bf16[128,2,4096]{2,1,0:T(2,128)(2,1)} copy(bf16[128,2,4096]{0,2,1:T(8,128)(2,1)} %bitcast.280) | data formatting | bytes 4194304 | tf_op jit(solution)/shard_map/convert_element_type | solution.py:265
  412.9 20.1 %all-to-all-done.11 = f32[8,8,2,4096]{3,1,2,0:T(8,128)} async-done(((f32[8,8,2,4096]{3,1,2,0:T(8,128)}), f32[8,8,2,4096]{3,1,2,0:T(8,128)}, u32[]{:S(2)}, u32[]{:S(2)}) %all-to-all-start.11) | async-done | bytes 2097184 | tf_op jit(solution)/shard_map/all_to_all | solution.py:102
  433.0 4.5 all-to-all-start.14
  440.4 25.2 %all-to-all-done.14 = bf16[128,2,4096]{2,1,0:T(2,128)(2,1)} async-done(((bf16[128,2,4096]{2,1,0:T(2,128)(2,1)}), bf16[128,2,4096]{2,1,0:T(2,128)(2,1)}, u32[]{:S(2)}, u32[]{:S(2)}) %all-to-all-start.14) | async-done | bytes 2097184 | tf_op jit(solution)/shard_map/all_to_all | solution.py:309
  467.6 6.9 %all-to-all-start.13 = ((bf16[8,8,2,4096]{3,2,1,0:T(2,128)(2,1)}), bf16[8,8,2,4096]{3,2,1,0:T(2,128)(2,1)S(1)}, u32[]{:S(2)}, u32[]{:S(2)}) async-start(bf16[8,8,2,4096]{3,2,1,0:T(2,128)(2,1)} %broadcast_in_dim.152), calls=%async_computation.13 | async-start | bytes 2097152 | tf_op jit(solution)/shard_map/all_to_all | solution.py:26
  480.2 9.3 %all-to-all-done.13 = bf16[8,8,2,4096]{3,2,1,0:T(2,128)(2,1)S(1)} async-done(((bf16[8,8,2,4096]{3,2,1,0:T(2,128)(2,1)}), bf16[8,8,2,4096]{3,2,1,0:T(2,128)(2,1)S(1)}, u32[]{:S(2)}, u32[]{:S(2)}) %all-to-all-start.13) | async-done | bytes 1048608 | tf_op jit(solution)/shard_map/all_to_all | solution.py:26
  (279 shorter events, 67.5 us)
Async XLA Ops:
  0.6 38.0 %copy-start = (f32[32,4096]{1,0:T(8,128)S(1)}, f32[32,4096]{1,0:T(8,128)}, u32[]{:S(2)}) copy-start(f32[32,4096]{1,0:T(8,128)} %param.12) | copy-start | bytes 1572868
  4.8 32.1 %copy-start.10 = (f32[40,128]{1,0:T(8,128)S(1)}, f32[40,128]{1,0:T(8,128)}, u32[]{:S(2)}) copy-start(f32[40,128]{1,0:T(8,128)} %param.14) | copy-start | bytes 61444
  4.8 32.6 %copy-start.12 = (f32[8]{0:T(128)S(1)}, f32[8]{0:T(128)}, u32[]{:S(2)}) copy-start(f32[8]{0:T(128)} %param.18) | copy-start | bytes 100
  4.9 33.3 %copy-start.39 = (f32[40]{0:T(128)S(1)}, f32[40]{0:T(128)}, u32[]{:S(2)}) copy-start(f32[40]{0:T(128)} %param.20) | copy-start | bytes 484
  4.9 33.3 %copy-start.40 = (f32[40]{0:T(128)S(1)}, f32[40]{0:T(128)}, u32[]{:S(2)}) copy-start(f32[40]{0:T(128)} %param.19) | copy-start | bytes 484
  4.9 37.0 %all-to-all-start = ((bf16[8,32,4096]{2,0,1:T(8,128)(2,1)}), bf16[8,32,4096]{2,0,1:T(8,128)(2,1)}, u32[]{:S(2)}, u32[]{:S(2)}) async-start(bf16[8,32,4096]{2,0,1:T(8,128)(2,1)} %copy.111), calls=%async_computation | async-start | bytes 4194304 | tf_op jit(solution)/shard_map/all_to_all | solution.py:255
  13.8 175.2 %copy-start.26 = (pred[2,64]{1,0:T(4,128)(4,1)}, pred[2,64]{1,0:T(4,128)(4,1)S(1)}, u32[]{:S(2)}) copy-start(pred[2,64]{1,0:T(4,128)(4,1)S(1)} %iota_compare_fusion.1) | copy-start | bytes 388
  37.4 141.4 %copy-start.29 = (f32[128]{0:T(128)}, f32[128]{0:T(128)S(1)}, u32[]{:S(2)}) copy-start(f32[128]{0:T(128)S(1)} %get-tuple-element.119) | copy-start | bytes 1540
  37.4 141.4 %copy-start.43 = (f32[128]{0:T(128)}, f32[128]{0:T(128)S(1)}, u32[]{:S(2)}) copy-start(f32[128]{0:T(128)S(1)} %get-tuple-element.118) | copy-start | bytes 1540
  38.2 116.6 %copy-start.48 = (f32[40]{0:T(128)}, f32[40]{0:T(128)S(1)}, u32[]{:S(2)}) copy-start(f32[40]{0:T(128)S(1)} %get-tuple-element.78) | copy-start | bytes 484
  38.2 140.7 %copy-start.16 = (f32[40]{0:T(128)}, f32[40]{0:T(128)S(1)}, u32[]{:S(2)}) copy-start(f32[40]{0:T(128)S(1)} %get-tuple-element.79) | copy-start | bytes 484
  38.2 140.7 %copy-start.18 = (f32[40]{0:T(128)}, f32[40]{0:T(128)S(1)}, u32[]{:S(2)}) copy-start(f32[40]{0:T(128)S(1)} %get-tuple-element.100) | copy-start | bytes 484
  38.2 140.7 %copy-start.20 = (f32[40]{0:T(128)}, f32[40]{0:T(128)S(1)}, u32[]{:S(2)}) copy-start(f32[40]{0:T(128)S(1)} %get-tuple-element.101) | copy-start | bytes 484
  38.6 121.4 %copy-start.31 = (f32[1,40]{1,0:T(1,128)}, f32[1,40]{1,0:T(1,128)S(1)}, u32[]{:S(2)}) copy-start(f32[1,40]{1,0:T(1,128)S(1)} %get-tuple-element.30) | copy-start | bytes 484
  38.6 121.3 %copy-start.33 = (f32[1,40]{1,0:T(1,128)}, f32[1,40]{1,0:T(1,128)S(1)}, u32[]{:S(2)}) copy-start(f32[1,40]{1,0:T(1,128)S(1)} %get-tuple-element.32) | copy-start | bytes 484
  38.6 140.2 %copy-start.24 = (f32[40]{0:T(128)}, f32[40]{0:T(128)S(1)}, u32[]{:S(2)}) copy-start(f32[40]{0:T(128)S(1)} %get-tuple-element.33) | copy-start | bytes 484
  42.6 13.4 %all-to-all-start.1 = ((bf16[16,40,128]{2,1,0:T(8,128)(2,1)}), bf16[16,40,128]{2,1,0:T(8,128)(2,1)S(1)}, u32[]{:S(2)}, u32[]{:S(2)}) async-start(bf16[16,40,128]{2,1,0:T(8,128)(2,1)} %broadcast_in_dim.139), calls=%async_computation.1 | async-start | bytes 327680 | tf_op jit(solution)/shard_map/all_to_all | solution.py:26
  63.8 14.9 %collective-permute-start.5 = (bf16[128,12,12]{0,2,1:T(8,128)(2,1)S(1)}, bf16[128,12,12]{0,2,1:T(8,128)(2,1)S(1)}, u32[]{:S(2)}, u32[]{:S(2)}) collective-permute-start(bf16[128,12,12]{0,2,1:T(8,128)(2,1)S(1)} %get-tuple-element.44), channel_id=1, source_target_pairs={{3,0},{4,1},{5,2},{6,3},{7,4},{8,5},{9,6},{10,7},{11,8},{12,9},{13... | collective-permute-start | bytes 110600 | tf_op jit(solution)/shard_map/ppermute | solution.py:21
  65.2 17.5 %collective-permute-start = (bf16[128,12,12]{0,2,1:T(8,128)(2,1)S(1)}, bf16[128,12,12]{0,2,1:T(8,128)(2,1)S(1)}, u32[]{:S(2)}, u32[]{:S(2)}) collective-permute-start(bf16[128,12,12]{0,2,1:T(8,128)(2,1)S(1)} %get-tuple-element.42), channel_id=1, source_target_pairs={{0,5},{1,6},{2,7},{3,8},{4,9},{5,10},{6,11},{7,12},{8,13},{9,14},{... | collective-permute-start | bytes 110600 | tf_op jit(solution)/shard_map/ppermute | solution.py:21
  71.2 16.2 %collective-permute-start.7 = (bf16[128,12,12]{0,2,1:T(8,128)(2,1)S(1)}, bf16[128,12,12]{0,2,1:T(8,128)(2,1)S(1)}, u32[]{:S(2)}, u32[]{:S(2)}) collective-permute-start(bf16[128,12,12]{0,2,1:T(8,128)(2,1)S(1)} %get-tuple-element.43), channel_id=1, source_target_pairs={{5,0},{6,1},{7,2},{8,3},{9,4},{10,5},{11,6},{12,7},{13,8},{14,9},{... | collective-permute-start | bytes 110600 | tf_op jit(solution)/shard_map/ppermute | solution.py:21
  72.5 16.4 %collective-permute-start.2 = (bf16[128,12,12]{0,2,1:T(8,128)(2,1)S(1)}, bf16[128,12,12]{0,2,1:T(8,128)(2,1)S(1)}, u32[]{:S(2)}, u32[]{:S(2)}) collective-permute-start(bf16[128,12,12]{0,2,1:T(8,128)(2,1)S(1)} %get-tuple-element.45), channel_id=1, source_target_pairs={{0,3},{1,4},{2,5},{3,6},{4,7},{5,8},{6,9},{7,10},{8,11},{9,12},{10... | collective-permute-start | bytes 110600 | tf_op jit(solution)/shard_map/ppermute | solution.py:21
  77.4 11.5 %collective-permute-start.4 = (bf16[128,64,12]{0,2,1:T(8,128)(2,1)S(1)}, bf16[128,64,12]{0,2,1:T(8,128)(2,1)S(1)}, u32[]{:S(2)}, u32[]{:S(2)}) collective-permute-start(bf16[128,64,12]{0,2,1:T(8,128)(2,1)S(1)} %get-tuple-element.49), channel_id=1, source_target_pairs={{1,0},{2,1},{3,2},{4,3},{5,4},{6,5},{7,6},{8,7},{9,8},{10,9},{11,1... | collective-permute-start | bytes 589832 | tf_op jit(solution)/shard_map/ppermute | solution.py:21
  78.7 10.3 %collective-permute-start.3 = (bf16[128,64,12]{0,2,1:T(8,128)(2,1)S(1)}, bf16[128,64,12]{0,2,1:T(8,128)(2,1)S(1)}, u32[]{:S(2)}, u32[]{:S(2)}) collective-permute-start(bf16[128,64,12]{0,2,1:T(8,128)(2,1)S(1)} %get-tuple-element.48), channel_id=1, source_target_pairs={{0,1},{1,2},{2,3},{3,4},{4,5},{5,6},{6,7},{7,8},{8,9},{9,10},{10,1... | collective-permute-start | bytes 589832 | tf_op jit(solution)/shard_map/ppermute | solution.py:21
  82.7 9.3 %collective-permute-start.1 = (bf16[128,12,128]{0,2,1:T(8,128)(2,1)S(1)}, bf16[128,12,128]{0,2,1:T(8,128)(2,1)S(1)}, u32[]{:S(2)}, u32[]{:S(2)}) collective-permute-start(bf16[128,12,128]{0,2,1:T(8,128)(2,1)S(1)} %get-tuple-element.46), channel_id=1, source_target_pairs={{0,4},{1,5},{2,6},{3,7},{4,8},{5,9},{6,10},{7,11},{8,12},{9,13},{1... | collective-permute-start | bytes 1179656 | tf_op jit(solution)/shard_map/ppermute | solution.py:21
  87.4 8.5 %collective-permute-start.6 = (bf16[128,12,128]{0,2,1:T(8,128)(2,1)S(1)}, bf16[128,12,128]{0,2,1:T(8,128)(2,1)S(1)}, u32[]{:S(2)}, u32[]{:S(2)}) collective-permute-start(bf16[128,12,128]{0,2,1:T(8,128)(2,1)S(1)} %get-tuple-element.47), channel_id=1, source_target_pairs={{4,0},{5,1},{6,2},{7,3},{8,4},{9,5},{10,6},{11,7},{12,8},{13,9},{1... | collective-permute-start | bytes 1179656 | tf_op jit(solution)/shard_map/ppermute | solution.py:21
  140.1 14.4 %all-to-all-start.2 = ((f32[16,40,129]{2,1,0:T(8,128)}), f32[16,40,129]{2,1,0:T(8,128)S(1)}, u32[]{:S(2)}, u32[]{:S(2)}) async-start(f32[16,40,129]{2,1,0:T(8,128)} %pad_maximum_fusion), calls=%async_computation.2 | async-start | bytes 1310720 | tf_op jit(solution)/shard_map/all_to_all | solution.py:102
  144.9 34.0 %copy-start.45 = (pred[128]{0:T(512)(128)(4,1)}, pred[128]{0:T(512)(128)(4,1)S(1)}, u32[]{:S(2)}) copy-start(pred[128]{0:T(512)(128)(4,1)S(1)} %add_compare_fusion) | copy-start | bytes 388
  154.8 23.6 %copy-start.22 = (f32[4,40]{1,0:T(4,128)S(1)}, f32[4,40]{1,0:T(4,128)}, u32[]{:S(2)}) copy-start(f32[4,40]{1,0:T(4,128)} %constant.106.clone.1) | copy-start | bytes 1924
  160.7 16.4 %all-to-all-start.3 = ((f32[8,1,240]{2,1,0:T(1,128)}), f32[8,1,240]{2,1,0:T(1,128)S(1)}, u32[]{:S(2)}, u32[]{:S(2)}) async-start(f32[8,1,240]{2,1,0:T(1,128)} %reshape.1445), calls=%async_computation.3 | async-start | bytes 16384 | tf_op jit(solution)/shard_map/all_to_all | solution.py:26
  172.5 28.1 %copy-start.14 = (pred[8]{0:T(512)(128)(4,1)}, pred[8]{0:T(512)(128)(4,1)S(1)}, u32[]{:S(2)}) copy-start(pred[8]{0:T(512)(128)(4,1)S(1)} %iota_compare_fusion.2) | copy-start | bytes 28
  190.1 13.7 %all-to-all-start.6 = ((f32[8,1,128]{2,1,0:T(1,128)}), f32[8,1,128]{2,1,0:T(1,128)S(1)}, u32[]{:S(2)}, u32[]{:S(2)}) async-start(f32[8,1,128]{2,1,0:T(1,128)} %reshape.1447), calls=%async_computation.6 | async-start | bytes 8192 | tf_op jit(solution)/shard_map/all_to_all | solution.py:26
  203.8 31.1 %all-to-all-start.5 = ((f32[8,8,2,4096]{3,1,2,0:T(8,128)}), f32[8,8,2,4096]{3,1,2,0:T(8,128)}, u32[]{:S(2)}, u32[]{:S(2)}) async-start(f32[8,8,2,4096]{3,1,2,0:T(8,128)} %copy.125), calls=%async_computation.5 | async-start | bytes 4194304 | tf_op jit(solution)/shard_map/all_to_all | solution.py:102
  260.7 20.3 %copy-start.27 = (pred[2,64]{1,0:T(4,128)(4,1)S(1)}, pred[2,64]{1,0:T(4,128)(4,1)}, u32[]{:S(2)}) copy-start(pred[2,64]{1,0:T(4,128)(4,1)} %copy-done.26) | copy-start | bytes 388
  263.0 35.3 %collective-permute-start.14 = (bf16[128,12,128]{0,2,1:T(8,128)(2,1)S(1)}, bf16[128,12,128]{0,2,1:T(8,128)(2,1)S(1)}, u32[]{:S(2)}, u32[]{:S(2)}) collective-permute-start(bf16[128,12,128]{0,2,1:T(8,128)(2,1)S(1)} %get-tuple-element.39), channel_id=1, source_target_pairs={{4,0},{5,1},{6,2},{7,3},{8,4},{9,5},{10,6},{11,7},{12,8},{13,9},{1... | collective-permute-start | bytes 1179656 | tf_op jit(solution)/shard_map/ppermute | solution.py:21
  264.3 34.1 %collective-permute-start.9 = (bf16[128,12,128]{0,2,1:T(8,128)(2,1)S(1)}, bf16[128,12,128]{0,2,1:T(8,128)(2,1)}, u32[]{:S(2)}, u32[]{:S(2)}) collective-permute-start(bf16[128,12,128]{0,2,1:T(8,128)(2,1)S(1)} %get-tuple-element.38), channel_id=1, source_target_pairs={{0,4},{1,5},{2,6},{3,7},{4,8},{5,9},{6,10},{7,11},{8,12},{9,13},{1... | collective-permute-start | bytes 1179656 | tf_op jit(solution)/shard_map/ppermute | solution.py:21
  269.1 29.2 %collective-permute-start.12 = (bf16[128,64,12]{0,2,1:T(8,128)(2,1)S(1)}, bf16[128,64,12]{0,2,1:T(8,128)(2,1)S(1)}, u32[]{:S(2)}, u32[]{:S(2)}) collective-permute-start(bf16[128,64,12]{0,2,1:T(8,128)(2,1)S(1)} %get-tuple-element.41), channel_id=1, source_target_pairs={{1,0},{2,1},{3,2},{4,3},{5,4},{6,5},{7,6},{8,7},{9,8},{10,9},{11,1... | collective-permute-start | bytes 589832 | tf_op jit(solution)/shard_map/ppermute | solution.py:21
  270.4 27.9 %collective-permute-start.11 = (bf16[128,64,12]{0,2,1:T(8,128)(2,1)}, bf16[128,64,12]{0,2,1:T(8,128)(2,1)S(1)}, u32[]{:S(2)}, u32[]{:S(2)}) collective-permute-start(bf16[128,64,12]{0,2,1:T(8,128)(2,1)} %get-tuple-element.40), channel_id=1, source_target_pairs={{0,1},{1,2},{2,3},{3,4},{4,5},{5,6},{6,7},{7,8},{8,9},{9,10},{10,1... | collective-permute-start | bytes 589832 | tf_op jit(solution)/shard_map/ppermute | solution.py:21
  274.4 7.3 %collective-permute-start.10 = (bf16[128,12,12]{0,2,1:T(8,128)(2,1)S(1)}, bf16[128,12,12]{0,2,1:T(8,128)(2,1)}, u32[]{:S(2)}, u32[]{:S(2)}) collective-permute-start(bf16[128,12,12]{0,2,1:T(8,128)(2,1)S(1)} %get-tuple-element.37), channel_id=1, source_target_pairs={{0,3},{1,4},{2,5},{3,6},{4,7},{5,8},{6,9},{7,10},{8,11},{9,12},{10... | collective-permute-start | bytes 110600 | tf_op jit(solution)/shard_map/ppermute | solution.py:21
  281.6 6.3 %collective-permute-start.13 = (bf16[128,12,12]{0,2,1:T(8,128)(2,1)}, bf16[128,12,12]{0,2,1:T(8,128)(2,1)S(1)}, u32[]{:S(2)}, u32[]{:S(2)}) collective-permute-start(bf16[128,12,12]{0,2,1:T(8,128)(2,1)} %get-tuple-element.36), channel_id=1, source_target_pairs={{3,0},{4,1},{5,2},{6,3},{7,4},{8,5},{9,6},{10,7},{11,8},{12,9},{13... | collective-permute-start | bytes 110600 | tf_op jit(solution)/shard_map/ppermute | solution.py:21
  287.9 2.8 collective-permute-start.8
  290.7 7.5 %collective-permute-start.15 = (bf16[128,12,12]{0,2,1:T(8,128)(2,1)}, bf16[128,12,12]{0,2,1:T(8,128)(2,1)S(1)}, u32[]{:S(2)}, u32[]{:S(2)}) collective-permute-start(bf16[128,12,12]{0,2,1:T(8,128)(2,1)} %get-tuple-element.35), channel_id=1, source_target_pairs={{5,0},{6,1},{7,2},{8,3},{9,4},{10,5},{11,6},{12,7},{13,8},{14,9},{... | collective-permute-start | bytes 110600 | tf_op jit(solution)/shard_map/ppermute | solution.py:21
  335.2 20.1 %copy-start.21 = (f32[40]{0:T(128)S(1)}, f32[40]{0:T(128)}, u32[]{:S(2)}) copy-start(f32[40]{0:T(128)} %copy-done.20) | copy-start | bytes 484
  335.2 20.1 %copy-start.49 = (f32[40]{0:T(128)S(1)}, f32[40]{0:T(128)}, u32[]{:S(2)}) copy-start(f32[40]{0:T(128)} %copy-done.48) | copy-start | bytes 484
  355.4 30.8 %copy-start.28 = (pred[2,64]{1,0:T(4,128)(4,1)S(1)}, pred[2,64]{1,0:T(4,128)(4,1)}, u32[]{:S(2)}) copy-start(pred[2,64]{1,0:T(4,128)(4,1)} %copy-done.26) | copy-start | bytes 388
  387.4 14.5 %all-to-all-start.12 = ((f32[8,1,128]{2,1,0:T(1,128)}), f32[8,1,128]{2,1,0:T(1,128)S(1)}, u32[]{:S(2)}, u32[]{:S(2)}) async-start(f32[8,1,128]{2,1,0:T(1,128)} %reshape.1451), calls=%async_computation.12 | async-start | bytes 8192 | tf_op jit(solution)/shard_map/all_to_all | solution.py:26
  401.9 31.1 %all-to-all-start.11 = ((f32[8,8,2,4096]{3,1,2,0:T(8,128)}), f32[8,8,2,4096]{3,1,2,0:T(8,128)}, u32[]{:S(2)}, u32[]{:S(2)}) async-start(f32[8,8,2,4096]{3,1,2,0:T(8,128)} %copy.135), calls=%async_computation.11 | async-start | bytes 4194304 | tf_op jit(solution)/shard_map/all_to_all | solution.py:102
  433.0 32.6 %all-to-all-start.14 = ((bf16[128,2,4096]{2,1,0:T(2,128)(2,1)}), bf16[128,2,4096]{2,1,0:T(2,128)(2,1)}, u32[]{:S(2)}, u32[]{:S(2)}) async-start(bf16[128,2,4096]{2,1,0:T(2,128)(2,1)} %copy.138), calls=%async_computation.14 | async-start | bytes 4194304 | tf_op jit(solution)/shard_map/all_to_all | solution.py:309
  467.6 21.9 %all-to-all-start.13 = ((bf16[8,8,2,4096]{3,2,1,0:T(2,128)(2,1)}), bf16[8,8,2,4096]{3,2,1,0:T(2,128)(2,1)S(1)}, u32[]{:S(2)}, u32[]{:S(2)}) async-start(bf16[8,8,2,4096]{3,2,1,0:T(2,128)(2,1)} %broadcast_in_dim.152), calls=%async_computation.13 | async-start | bytes 2097152 | tf_op jit(solution)/shard_map/all_to_all | solution.py:26
  (28 other events, 340.5 us)
where the time goes:
time: 499 us; the launch traced here: 491 us
  waiting for transfers between devices  114 us (23%)
  starting transfers between devices  106 us (21%)
  other arithmetic  91.4 us (18%)
  blocking collectives  69 us (14%)
  local copies, waits for them, and re-layouts  47.8 us (10%)
  matrix products  40.2 us (8%)
  between operations  22.4 us (4%)
    all_to_all x3, waiting for transfers between devices, sent_and_summed(): lax.all_to_all(blocks, axis, split_axis=0, concat_axis=0, tiled=True)  52.6 us
    all_to_all x4, blocking collectives, from_everyone(): return lax.all_to_all(copies, axis, split_axis=0, concat_axis=0, tiled=True)  51.8 us
    ppermute x16, starting transfers between devices, passed_along(): lax.ppermute(value, axis, [(source, source + steps) for source in range(i...  45.6 us
    concatenate x2, other arithmetic, rim_background(): padded = jnp.concatenate([top_band, mid_band, low_band], axis=1)  40.6 us
    all_to_all x5, starting transfers between devices, from_everyone(): return lax.all_to_all(copies, axis, split_axis=0, concat_axis=0, tiled=True)  32.8 us
    convert_element_type x2, other arithmetic, body(): rim_background(leftover, offsets, cycle_coef).astype(jnp.bfloat16)  29.4 us
    all_to_all x1, waiting for transfers between devices, body(): lax.all_to_all(backdrop_tiles, 'tile', split_axis=0, concat_axis=1, tiled...  25.2 us
    ppermute x16, waiting for transfers between devices, passed_along(): lax.ppermute(value, axis, [(source, source + steps) for source in range(i...  18.8 us
  transfers between devices with their start and end apart: 26, of which 12 were waited for; matrix products, arithmetic and copies ran while one was open for 11% of the time, Pallas kernels for 0%

commit v1 on v0

v1 whole, which is shorter than its diff:
```python
import functools

import jax
import jax.numpy as jnp
from jax import lax
from jax.experimental import pallas as pl
from jax.experimental.pallas import tpu as pltpu
from jax.sharding import PartitionSpec as P

SIDE = 64
WIDE = 128
RAD = 12
STRIP = 16
GRID_W = 8
ITERS = 2
SLOTS = 64
CYCLE = 8
NEUR = 40
NPAD = 48
EPSILON = 1e-06
F32 = jnp.float32
BF16 = jnp.bfloat16


def nt(a, b):
    return lax.dot_general(a, b, (((1,), (1,)), ((), ())), preferred_element_type=F32)


def nn(a, b):
    return lax.dot_general(a, b, (((1,), (0,)), ((), ())), preferred_element_type=F32)


def eye(n):
    return (
        lax.broadcasted_iota(jnp.int32, (n, n), 0) == lax.broadcasted_iota(jnp.int32, (n, n), 1)
    ).astype(BF16)


def three(x):
    high = x.astype(BF16)
    rest = x - high.astype(F32)
    mid = rest.astype(BF16)
    low = (rest - mid.astype(F32)).astype(BF16)
    return high, mid, low


def lane(shape):
    return lax.broadcasted_iota(jnp.int32, shape, len(shape) - 1)


def row(shape):
    return lax.broadcasted_iota(jnp.int32, shape, len(shape) - 2)


def call(body, outs, args, smem=0, scratch=(), name=None):
    spaces = [pl.BlockSpec(memory_space=pltpu.SMEM)] * smem
    spaces += [pl.BlockSpec(memory_space=pltpu.VMEM)] * (len(args) - smem)
    return pl.pallas_call(
        body,
        out_shape=[jax.ShapeDtypeStruct(s, d) for s, d in outs],
        in_specs=spaces,
        out_specs=[pl.BlockSpec(memory_space=pltpu.VMEM)] * len(outs),
        scratch_shapes=list(scratch),
        name=name,
    )(*args)


def doubled(block):
    wide = block.astype(F32)
    first = (lane(wide.shape) & (WIDE - 1)) < SIDE
    upper = jnp.where(first, wide, 0.0)
    return jnp.concatenate([upper, wide - upper], axis=0).astype(BF16)


def baseline_body(base_ref, out_ref):
    unit = eye(256)

    def step(j, carry):
        for t in range(2):
            line = base_ref[t, 0:1, pl.ds(pl.multiple_of(j * 256, 256), 256)]
            parts = three(jnp.broadcast_to(line, (WIDE, 256)))
            col = nt(unit, parts[0]) + nt(unit, parts[1]) + nt(unit, parts[2])
            out_ref[pl.ds(j * 4, 4), t * SIDE : (t + 1) * SIDE, :] = col.reshape(4, SIDE, WIDE)
        return carry

    lax.fori_loop(0, 16, step, 0)


def merge_body(count_ref, fp_ref, out_ref):
    first = lane((SLOTS, WIDE)) < SIDE
    slot = row((SLOTS, WIDE))
    live = slot < jnp.where(first, count_ref[0], count_ref[1])
    for j in range(32):
        a = fp_ref[0, :, j * WIDE : (j + 1) * WIDE].astype(F32)
        b = fp_ref[1, :, j * WIDE : (j + 1) * WIDE].astype(F32)
        even = jnp.where(first, a, pltpu.roll(b, SIDE, 1))
        odd = jnp.where(first, pltpu.roll(a, SIDE, 1), b)
        at = (2 * j) % 8 * WIDE
        out_ref[j // 4, :, at : at + WIDE] = jnp.where(live, even, 0.0).astype(BF16)
        out_ref[j // 4, :, at + WIDE : at + 2 * WIDE] = jnp.where(live, odd, 0.0).astype(BF16)


def split_body(fb_ref, out_ref):
    first = lane((SLOTS, WIDE)) < SIDE
    for j in range(32):
        at = (2 * j) % 8 * WIDE
        even = fb_ref[j // 4, :, at : at + WIDE].astype(F32)
        odd = fb_ref[j // 4, :, at + WIDE : at + 2 * WIDE].astype(F32)
        a = jnp.where(first, even, pltpu.roll(odd, SIDE, 1))
        b = jnp.where(first, pltpu.roll(even, SIDE, 1), odd)
        out_ref[0, :, j * WIDE : (j + 1) * WIDE] = a.astype(BF16)
        out_ref[1, :, j * WIDE : (j + 1) * WIDE] = b.astype(BF16)


def expand_body(fb_ref, out_ref):
    unit = eye(256)

    def step(j, carry):
        both = doubled(fb_ref[j])
        for k in range(4):
            out_ref[j, k * 256 : (k + 1) * 256, :] = nt(
                unit, both[:, k * 256 : (k + 1) * 256]
            ).astype(BF16)
        return carry

    lax.fori_loop(0, 8, step, 0)


def major_body(fb_ref, out_ref):
    def step(j, total):
        for k in range(8):
            block = fb_ref[j, :, k * WIDE : (k + 1) * WIDE].astype(F32)
            total = total + block * jnp.sum(block, axis=0, keepdims=True)
        return total

    total = lax.fori_loop(0, 8, step, jnp.zeros((SLOTS, WIDE), F32))
    first = lane((SLOTS, WIDE)) < SIDE
    upper = jnp.sum(jnp.where(first, total, 0.0), axis=1, keepdims=True)
    lower = jnp.sum(jnp.where(first, 0.0, total), axis=1, keepdims=True)
    out_ref[...] = jnp.broadcast_to(jnp.concatenate([upper, lower], axis=0), (WIDE, WIDE))


def collect_body(g_ref, pick_ref, out_ref):
    keys = g_ref.shape[0] * g_ref.shape[1]
    chosen = (pick_ref[...] == lane((WIDE, keys))).astype(F32).astype(BF16)
    out_ref[...] = nn(chosen, g_ref[...].reshape(keys, WIDE)).astype(BF16)


def rims(left_ref, rim_refs):
    top, bottom, west, east, nw, ne, sw, se = rim_refs
    top[...] = left_ref[:RAD]
    bottom[...] = left_ref[SIDE - RAD :]
    west[...] = left_ref[:, :STRIP]
    east[...] = left_ref[:, WIDE - STRIP :]
    nw[...] = left_ref[:RAD, :STRIP]
    ne[...] = left_ref[:RAD, WIDE - STRIP :]
    sw[...] = left_ref[SIDE - RAD :, :STRIP]
    se[...] = left_ref[SIDE - RAD :, WIDE - STRIP :]


def first_left_body(x_ref, base_ref, ft_ref, s_ref, d_ref, resid_ref, left_ref, *rim_refs):
    unit = eye(256)
    slots = s_ref[...]

    def step(j, carry):
        halves = []
        for t in range(2):
            part = x_ref[:, t, :, pl.ds(pl.multiple_of(j * 256, 256), 256)].astype(F32)
            part = part.reshape(WIDE, 256).astype(BF16)
            halves.append(nt(unit, part).reshape(4, SIDE, WIDE))
        rows = pl.ds(j * 4, 4)
        clean = jnp.concatenate(halves, axis=1) - base_ref[rows]
        ft = ft_ref[j // 2, pl.ds(pl.multiple_of((j % 2) * 512, 512), 512), :]
        resid = clean - nn(ft, slots).reshape(4, WIDE, WIDE)
        d_ref[rows] = clean
        resid_ref[rows] = resid
        left_ref[rows] = resid.astype(BF16)
        return carry

    lax.fori_loop(0, 16, step, 0)
    rims(left_ref, rim_refs)


def next_left_body(fb_ref, d_ref, s_ref, ft_ref, resid_ref, left_ref, *rim_refs):
    unit = eye(256)
    slots = s_ref[...]

    def step(j, carry):
        both = doubled(fb_ref[j])
        for k in range(4):
            ft = nt(unit, both[:, k * 256 : (k + 1) * 256]).astype(BF16)
            ft_ref[j, k * 256 : (k + 1) * 256, :] = ft
            rows = pl.ds(j * 8 + k * 2, 2)
            resid = d_ref[rows] - nn(ft, slots).reshape(2, WIDE, WIDE)
            resid_ref[rows] = resid
            left_ref[rows] = resid.astype(BF16)
        return carry

    lax.fori_loop(0, 8, step, 0)
    rims(left_ref, rim_refs)


def stencil_body(
    off_ref, coef_ref, left_ref, top, bottom, west, east, nw, ne, sw, se,
    resid_ref, fb_ref, major_ref, pick_ref, drop_ref, out_ref, pad_ref, mis_ref,
):
    first, last = RAD, RAD + SIDE
    inner, outer = STRIP, STRIP + WIDE

    def fill(r, carry):
        pad_ref[first + r, inner:outer, :] = left_ref[r].astype(F32)
        pad_ref[first + r, :inner, :] = west[r].astype(F32)
        pad_ref[first + r, outer:, :] = east[r].astype(F32)
        return carry

    lax.fori_loop(0, SIDE, fill, 0)

    def ends(r, carry):
        pad_ref[r, inner:outer, :] = top[r].astype(F32)
        pad_ref[r, :inner, :] = nw[r].astype(F32)
        pad_ref[r, outer:, :] = ne[r].astype(F32)
        pad_ref[last + r, inner:outer, :] = bottom[r].astype(F32)
        pad_ref[last + r, :inner, :] = sw[r].astype(F32)
        pad_ref[last + r, outer:, :] = se[r].astype(F32)
        return carry

    lax.fori_loop(0, RAD, ends, 0)

    def step(r, carry):
        total = jnp.zeros((WIDE, WIDE), F32)
        for i in range(CYCLE):
            source = pad_ref[r + RAD + off_ref[i, 0], pl.ds(STRIP + off_ref[i, 1], WIDE), :]
            total = total + coef_ref[i] * source
        drop = total.astype(BF16)
        drop_ref[r] = drop
        mis_ref[r] = (resid_ref[r] - drop.astype(F32)).astype(BF16)
        return carry

    lax.fori_loop(0, SIDE, step, 0)

    total = jnp.zeros((WIDE, WIDE), F32)
    for j in range(8):
        total = total + nn(
            doubled(fb_ref[j]), mis_ref[j * 8 : (j + 1) * 8].reshape(8 * WIDE, WIDE)
        )
    keys = out_ref.shape[0] * NPAD
    chosen = (pick_ref[...] == row((keys, WIDE))).astype(F32).astype(BF16)
    both = jnp.concatenate([total, major_ref[...]], axis=1)
    high, mid, low = three(both)
    found = nn(chosen, high) + nn(chosen, mid) + nn(chosen, low)
    diagonal = row((NPAD, WIDE)) == lane((NPAD, WIDE))
    for b in range(out_ref.shape[0]):
        out_ref[b] = found[b * NPAD : (b + 1) * NPAD, :WIDE]
        spread = jnp.where(diagonal, found[b * NPAD : (b + 1) * NPAD, WIDE:], 0.0)
        out_ref[b, NEUR:NPAD, :] = jnp.broadcast_to(
            jnp.sum(spread, axis=0, keepdims=True), (NPAD - NEUR, WIDE)
        )


def first_order(x, rate):
    at = lane(x.shape)
    power = rate
    for k in range(7):
        x = x + power * jnp.where(at >= (1 << k), pltpu.roll(x, 1 << k, 1), 0.0)
        power = power * power
    return x


def filter_body(sum_ref, traces_ref, decay_ref, rise_ref, penalty_ref, a_ref, b_ref, out_ref):
    total = jnp.sum(sum_ref[...], axis=0)
    gradient = total[:NEUR]
    diagonal = row((NEUR, WIDE)) == lane((NEUR, WIDE))
    spread = jnp.where(diagonal, jnp.broadcast_to(total[NEUR : NEUR + 1], (NEUR, WIDE)), 0.0)
    curvature = jnp.sum(spread, axis=1, keepdims=True)
    decay, rise = decay_ref[...], rise_ref[...]
    stepped = traces_ref[...] + gradient / (curvature + EPSILON)
    rectified = jnp.maximum(stepped - penalty_ref[...], 0.0)
    driven = (1.0 - decay) * (1.0 - rise) * rectified
    a = first_order(driven, decay)
    b = first_order(driven, rise)
    a_ref[...] = a
    b_ref[...] = b
    ends = []
    for x in (a, b):
        at_end = jnp.broadcast_to(x[:, WIDE - 1 :], (NEUR, WIDE))
        ends.append(jnp.sum(jnp.where(diagonal, at_end, 0.0), axis=0, keepdims=True))
    ends.append(jnp.zeros((6, WIDE), F32))
    block = jnp.concatenate(ends, axis=0)
    for k in range(out_ref.shape[0]):
        out_ref[k] = block


def entering_body(
    here_ref, ends_ref, rates_ref, a_ref, b_ref, decay_ref, rise_ref, out_ref, copies_ref
):
    here = here_ref[0]
    rates = rates_ref[...]
    for _ in range(7):
        rates = rates * rates
    held = jnp.zeros((8, WIDE), F32)
    for k in range(ends_ref.shape[0]):
        held = jnp.where(k < here, rates * held + ends_ref[k], held)
    diagonal = row((NEUR, WIDE)) == lane((NEUR, WIDE))
    later = lane((NEUR, WIDE)) + 1

    def whole(x, rate, line):
        spread = jnp.where(diagonal, jnp.broadcast_to(line, (NEUR, WIDE)), 0.0)
        entering = jnp.sum(spread, axis=1, keepdims=True)
        powers = jnp.ones((NEUR, WIDE), F32)
        squared = rate
        for k in range(8):
            powers = powers * jnp.where((later >> k) & 1 == 1, squared, 1.0)
            squared = squared * squared
        return x + powers * entering

    decay, rise = decay_ref[...], rise_ref[...]
    a = whole(a_ref[...], decay, held[0:1])
    b = whole(b_ref[...], rise, held[1:2])
    traces = (decay * a - rise * b) / (decay - rise)
    out_ref[...] = traces
    padded = jnp.concatenate([traces, jnp.zeros((NPAD - NEUR, WIDE), F32)], axis=0).astype(BF16)
    for k in range(copies_ref.shape[0]):
        copies_ref[k] = padded


def numer_body(g_ref, pick_ref, d_ref, drop_ref, ft_ref, s_ref, out_ref):
    keys = g_ref.shape[0] * g_ref.shape[1]
    chosen = (pick_ref[...] == lane((WIDE, keys))).astype(F32).astype(BF16)
    slots = nn(chosen, g_ref[...].reshape(keys, WIDE)).astype(BF16)
    s_ref[...] = slots
    wide = slots.astype(F32)
    sums = jnp.concatenate(
        [
            jnp.broadcast_to(jnp.sum(wide[:SLOTS], axis=0, keepdims=True), (SLOTS, WIDE)),
            jnp.broadcast_to(jnp.sum(wide[SLOTS:], axis=0, keepdims=True), (SLOTS, WIDE)),
        ],
        axis=0,
    )
    weight = jnp.sum(wide * sums, axis=1, keepdims=True)
    first = lane((SLOTS, WIDE)) < SIDE
    weights = jnp.where(first, weight[:SLOTS], weight[SLOTS:])
    first = (lane((SLOTS, 8 * WIDE)) & (WIDE - 1)) < SIDE

    def step(j, carry):
        rebuilt = nn(ft_ref[j], slots)
        rows = pl.ds(j * 8, 8)
        clean = d_ref[rows] - drop_ref[rows].astype(F32)
        mis = (clean.reshape(8 * WIDE, WIDE) - rebuilt).astype(BF16)
        both = nt(slots, mis)
        out_ref[j, :, : 8 * WIDE] = jnp.where(first, both[:SLOTS], both[SLOTS:])
        out_ref[j, :, 8 * WIDE :] = weights
        return carry

    lax.fori_loop(0, 8, step, 0)


def update_body(info_ref, parts_ref, fb_ref, out_ref):
    first = lane((SLOTS, WIDE)) < SIDE
    slot = row((SLOTS, WIDE))
    live = slot < jnp.where(first, info_ref[1], info_ref[2])
    here = info_ref[0]
    count = parts_ref.shape[0]

    def total(at):
        part = parts_ref[0, :, at : at + WIDE]
        for k in range(1, count):
            part = part + parts_ref[k, :, at : at + WIDE]
        return part

    divisor = jnp.maximum(total(8 * WIDE), 1.0)
    for j in range(8):
        at = j * WIDE
        current = fb_ref[here, :, at : at + WIDE].astype(F32)
        fresh = jnp.maximum(current + total(at) / divisor, 0.0)
        fresh = jnp.where(live, fresh, 0.0).astype(BF16)
        for k in range(out_ref.shape[0]):
            out_ref[k, :, at : at + WIDE] = fresh


def frames_body(drop_ref, out_ref):
    unit = eye(WIDE)

    def step(j, carry):
        for t in range(2):
            part = drop_ref[pl.ds(j * 4, 4), t * SIDE : (t + 1) * SIDE, :].reshape(256, WIDE)
            turned = nt(unit, part).reshape(16, 8, 256)
            out_ref[:, t, :, pl.ds(pl.multiple_of(j * 256, 256), 256)] = turned.astype(BF16)
        return carry

    lax.fori_loop(0, 16, step, 0)


def swapped(x, axis):
    return lax.all_to_all(x, axis, split_axis=0, concat_axis=0, tiled=True)


def rim_exchange(rims_here, across):
    top, bottom, west, east, nw, ne, sw, se = rims_here
    count = lax.axis_size("tile")

    def moved(piece, down, right):
        pairs = []
        for source in range(count):
            y, x = source // across + down, source % across + right
            if 0 <= y < count // across and 0 <= x < across:
                pairs.append((source, y * across + x))
        return lax.ppermute(piece, "tile", pairs)

    return (
        moved(bottom, 1, 0),
        moved(top, -1, 0),
        moved(east, 0, 1),
        moved(west, 0, -1),
        moved(se, 1, 1),
        moved(sw, 1, -1),
        moved(ne, -1, 1),
        moved(nw, -1, -1),
    )


def body(
    movie_frames,
    baseline,
    footprints,
    traces,
    intersection,
    counts,
    offsets,
    cycle_coef,
    decay_rate,
    rise_rate,
    penalty,
):
    tiles, frames = lax.axis_size("tile"), lax.axis_size("tm")
    frames_dev = movie_frames.shape[0]
    pixels = SIDE * SIDE
    here = lax.axis_index("tile")
    block = lax.axis_index("tm").astype(jnp.int32)
    picture = (SIDE, WIDE, WIDE)

    ready = movie_frames.reshape(frames_dev, tiles, 2, pixels).transpose(1, 2, 0, 3)
    local_movie = swapped(ready, "tile")

    base = lax.dynamic_slice_in_dim(baseline, here * 2, 2, 0).reshape(2, 1, pixels)
    occupied = jnp.arange(SLOTS, dtype=jnp.int32)[None, :] < counts[:, None]
    owner = intersection // NEUR
    pick = jnp.where(occupied, owner * NPAD + (intersection - owner * NEUR), -1).reshape(-1)
    pick_row, pick_col = pick.reshape(1, WIDE), pick.reshape(WIDE, 1)
    decay, rise, cost = (v.reshape(NEUR, 1) for v in (decay_rate, rise_rate, penalty))
    rates = jnp.zeros((8, WIDE), F32).at[0, :NEUR].set(decay_rate).at[1, :NEUR].set(rise_rate)
    info = jnp.concatenate([block.reshape(1), counts])

    padded = jnp.pad(traces, ((0, NPAD - NEUR), (0, 0))).astype(BF16)
    gathered = swapped(jnp.broadcast_to(padded, (tiles, NPAD, WIDE)), "tile")
    (base_cols,) = call(baseline_body, [(picture, F32)], (base,), name="base")
    (shapes,) = call(
        merge_body,
        [((8, SLOTS, 8 * WIDE), BF16)],
        (counts, footprints.transpose(1, 0, 2)),
        smem=1,
        name="merge",
    )
    (turned,) = call(expand_body, [((8, 8 * WIDE, WIDE), BF16)], (shapes,), name="expand")
    (slots,) = call(
        collect_body, [((WIDE, WIDE), BF16)], (gathered, pick_col), name="collect"
    )
    rim_shapes = [
        ((RAD, WIDE, WIDE), BF16),
        ((RAD, WIDE, WIDE), BF16),
        ((SIDE, STRIP, WIDE), BF16),
        ((SIDE, STRIP, WIDE), BF16),
    ] + [((RAD, STRIP, WIDE), BF16)] * 4
    drop = None
    clean = None
    for iteration in range(ITERS):
        (major,) = call(major_body, [((WIDE, WIDE), F32)], (shapes,), name="major")
        if iteration == 0:
            clean, resid, left, *rim = call(
                first_left_body,
                [(picture, F32), (picture, F32), (picture, BF16)] + rim_shapes,
                (local_movie, base_cols, turned, slots),
                name="left0",
            )
        else:
            turned, resid, left, *rim = call(
                next_left_body,
                [((8, 8 * WIDE, WIDE), BF16), (picture, F32), (picture, BF16)] + rim_shapes,
                (shapes, clean, slots),
                name="left1",
            )
        around = rim_exchange(rim, GRID_W // 2)
        up, down, left_side, right_side, nw, ne, sw, se = around
        drop, terms = call(
            stencil_body,
            [(picture, BF16), ((tiles, NPAD, WIDE), F32)],
            (offsets, cycle_coef, left, up, down, left_side, right_side, nw, ne, sw, se,
             resid, shapes, major, pick_row),
            smem=2,
            scratch=[
                pltpu.VMEM((SIDE + 2 * RAD, WIDE + 2 * STRIP, WIDE), F32),
                pltpu.VMEM(picture, BF16),
            ],
            name="stencil",
        )
        arrived = swapped(terms, "tile")
        a, b, ends = call(
            filter_body,
            [((NEUR, WIDE), F32), ((NEUR, WIDE), F32), ((frames, 8, WIDE), F32)],
            (arrived, traces, decay, rise, cost),
            name="filter",
        )
        ends = swapped(ends, "tm")
        traces, copies = call(
            entering_body,
            [((NEUR, WIDE), F32), ((tiles, NPAD, WIDE), BF16)],
            (block.reshape(1), ends, rates, a, b, decay, rise),
            smem=1,
            name="entering",
        )
        gathered = swapped(copies, "tile")
        slots, numer = call(
            numer_body,
            [((WIDE, WIDE), BF16), ((frames, SLOTS, 9 * WIDE), F32)],
            (gathered, pick_col, clean, drop, turned),
            name="numer",
        )
        parts = swapped(numer, "tm")
        (fresh,) = call(
            update_body,
            [((frames, SLOTS, 8 * WIDE), BF16)],
            (info, parts, shapes),
            smem=1,
            name="update",
        )
        shapes = swapped(fresh, "tm")
    (by_frame,) = call(frames_body, [((tiles, 2, frames_dev, pixels), BF16)], (drop,), name="turn")
    backdrop = swapped(by_frame, "tile").transpose(2, 0, 1, 3).reshape(movie_frames.shape)
    (out_shapes,) = call(split_body, [((2, SLOTS, pixels), BF16)], (shapes,), name="split")
    return (traces, out_shapes.transpose(1, 0, 2), backdrop)


def solution(mesh):
    in_specs = (
        P(("tm", "tile"), None, None),
        P(),
        P(None, "tile", None),
        P("tile", "tm"),
        P("tile", None),
        P("tile"),
        P(),
        P(),
        P("tile"),
        P("tile"),
        P("tile"),
    )
    out_specs = (P("tile", "tm"), P(None, "tile", None), P(("tm", "tile"), None, None))
    return jax.shard_map(body, mesh=mesh, in_specs=in_specs, out_specs=out_specs, check_vma=False)
```

time: 499 us -> 432 us (0.87); the launches traced: 491 us -> 430 us
  Pallas kernels: 0 us -> 107 us
  other arithmetic: 91.4 us -> 1.52 us
  matrix products: 40.2 us -> 0 us
  between operations: 22.4 us -> 1.09 us
  starting transfers between devices: 106 us -> 85.9 us
  local copies, waits for them, and re-layouts: 47.8 us -> 29 us
  waiting for transfers between devices: 114 us -> 132 us
    pallas_call x0 -> x20, Pallas kernels: none -> 107 us  [call(): pl.pallas_call(body, out_shape=[jax.ShapeDtypeStruct(s, d) for s, d in ou...]
    concatenate x4 -> x1, other arithmetic: 41.5 us -> 0.66 us  [body(): info = jnp.concatenate([block.reshape(1), counts])]
    dot_general x18 -> x0, matrix products: 40.2 us -> none  [the longest x2 11.5 us: body(): jnp.einsum('tsf,ftp->stp', slot_rows, misfit, preferred_element_type=jnp....]
    convert_element_type x13 -> x0, other arithmetic: 38.6 us -> none  [the longest x2 29.4 us: body(): rim_background(leftover, offsets, cycle_coef).astype(jnp.bfloat16)]
    ppermute x16, starting transfers between devices: 45.6 us -> 32 us  [moved(): return lax.ppermute(piece, 'tile', pairs)]
    convert_element_type x5 -> x0, local copies, waits for them, and re-layouts: 12.4 us -> none  [the longest x2 6.4 us: body(): rim_background(leftover, offsets, cycle_coef).astype(jnp.bfloat16)]
    all_to_all x10 -> x8, waiting for transfers between devices: 95.1 us -> 104 us  [swapped(): return lax.all_to_all(x, axis, split_axis=0, concat_axis=0, tiled=True)]
    ppermute x16, waiting for transfers between devices: 18.8 us -> 27.7 us  [moved(): return lax.ppermute(piece, 'tile', pairs)]
  transfers between devices with their start and end apart: 26 -> 24, of which waited for: 12 -> 12; matrix products, arithmetic and copies ran while one was open for 11% -> 4% of each run, Pallas kernels for 0% -> 8%
where the time goes in v1:
time: 432 us; the launch traced here: 430 us
  waiting for transfers between devices  132 us (31%)
  Pallas kernels  107 us (25%)
  starting transfers between devices  85.9 us (20%)
  blocking collectives  73.6 us (17%)
  local copies, waits for them, and re-layouts  29 us (7%)
    pallas_call x20, Pallas kernels, call(): pl.pallas_call(body, out_shape=[jax.ShapeDtypeStruct(s, d) for s, d in ou...  107 us
    all_to_all x8, waiting for transfers between devices, swapped(): return lax.all_to_all(x, axis, split_axis=0, concat_axis=0, tiled=True)  104 us
    all_to_all x5, blocking collectives, swapped(): return lax.all_to_all(x, axis, split_axis=0, concat_axis=0, tiled=True)  73.6 us
    all_to_all x8, starting transfers between devices, swapped(): return lax.all_to_all(x, axis, split_axis=0, concat_axis=0, tiled=True)  54 us
    ppermute x16, starting transfers between devices, moved(): return lax.ppermute(piece, 'tile', pairs)  32 us
    ppermute x16, waiting for transfers between devices, moved(): return lax.ppermute(piece, 'tile', pairs)  27.7 us
    unnamed x69, local copies, waits for them, and re-layouts  24.1 us
  transfers between devices with their start and end apart: 24, of which 12 were waited for; matrix products, arithmetic and copies ran while one was open for 4% of the time, Pallas kernels for 8%

profile of v1, /device:TPU:1, one launch (start us, length us, event | category | flops | bytes accessed | tf_op | source)
XLA Modules:
  0.0 430.2 jit_solution(6775889280581186811)
XLA Ops:
  2.1 8.6 %all-to-all-start.1 = ((bf16[16,48,128]{2,1,0:T(8,128)(2,1)}), bf16[16,48,128]{2,1,0:T(8,128)(2,1)S(1)}, u32[]{:S(2)}, u32[]{:S(2)}) async-start(bf16[16,48,128]{2,1,0:T(8,128)(2,1)} %broadcast_in_dim.3), calls=%async_computation.1 | async-start | bytes 393216 | tf_op jit(solution)/shard_map/all_to_all | solution.py:394
  10.7 4.1 copy.14
  14.8 3.1 all-to-all-done.1.g_ref
  18.6 3.7 all-to-all-start
  23.0 8.8 %base.1.base_ref = f32[64,128,128]{2,1,0:T(8,128)} custom-call(f32[2,1,4096]{2,1,0:T(1,128)} %reshape.91.base_ref), custom_call_target="tpu_custom_call" | custom-call | tf_op jit(solution)/shard_map/base/pallas_call | solution.py:58
  31.7 2.8 copy.34
  34.5 2.7 merge.1.fb_ref
  37.3 5.0 %expand.1.ft_ref = bf16[8,1024,128]{2,1,0:T(8,128)(2,1)} custom-call(bf16[8,64,1024]{2,1,0:T(8,128)(2,1)} %merge.1.fb_ref), custom_call_target="tpu_custom_call" | custom-call | tf_op jit(solution)/shard_map/expand/pallas_call | solution.py:58
  44.9 3.3 all-to-all-done.x_ref
  49.5 12.2 %left0.1 = (f32[64,128,128]{2,1,0:T(8,128)}, f32[64,128,128]{2,1,0:T(8,128)}, bf16[64,128,128]{2,1,0:T(8,128)(2,1)}, bf16[12,128,128]{2,1,0:T(8,128)(2,1)}, bf16...) custom-call(bf16[16,2,8,4096]{3,2,1,0:T(8,128)(2,1)} %copy-done.4, ...), custom_call_target="tpu_custom_call" | custom-call | tf_op jit(solution)/shard_map/left0/pallas_call | solution.py:58
  64.6 2.2 collective-permute-start.2
  68.1 8.0 %collective-permute-start.4 = (bf16[12,16,128]{2,1,0:T(8,128)(2,1)}, bf16[12,16,128]{2,1,0:T(8,128)(2,1)S(1)}, u32[]{:S(2)}, u32[]{:S(2)}) collective-permute-start(bf16[12,16,128]{2,1,0:T(8,128)(2,1)} %get-tuple-element.71), channel_id=1, source_target_pairs={{0,5},{1,6},{2,7},{4,9},{5,10},{6,11},{8,13},{9,14},{10,15},{16,21... | collective-permute-start | bytes 147464 | tf_op jit(solution)/shard_map/ppermute | solution.py:407
  80.3 2.4 major.2.major_ref
  84.0 11.8 %collective-permute-done.7.se = bf16[12,16,128]{2,1,0:T(8,128)(2,1)S(1)} collective-permute-done((bf16[12,16,128]{2,1,0:T(8,128)(2,1)}, bf16[12,16,128]{2,1,0:T(8,128)(2,1)S(1)}, u32[]{:S(2)}, u32[]{:S(2)}) %collective-permute-start.7) | collective-permute-done | bytes 49184 | tf_op jit(solution)/shard_map/ppermute | solution.py:407
  96.8 9.5 %stencil.2 = (bf16[64,128,128]{2,1,0:T(8,128)(2,1)}, f32[16,48,128]{2,1,0:T(8,128)}) custom-call(s32[8,2]{1,0:T(8,128)} %copy.24.off_ref, f32[8]{0:T(128)} %coef_ref.3, bf16[64,128,128]{2,1,0:T(8,128)(2,1)} %get-tuple-element.66.left_ref, bf16[12,128,128]{2,1,0:T(8,128)(2,1)} %copy-done.8, bf16[12,128,128]{2,1,0:T(8,128)(2,1)} %copy-done.10, ...), custom_call_target="tpu_custom_call" | custom-call | tf_op jit(solution)/shard_map/stencil/pallas_call | solution.py:58
  106.3 6.8 %all-to-all-start.2 = ((f32[16,48,128]{2,1,0:T(8,128)}), f32[16,48,128]{2,1,0:T(8,128)S(1)}, u32[]{:S(2)}, u32[]{:S(2)}) async-start(f32[16,48,128]{2,1,0:T(8,128)} %get-tuple-element.76), calls=%async_computation.2 | async-start | bytes 786432 | tf_op jit(solution)/shard_map/all_to_all | solution.py:394
  115.2 5.9 %all-to-all-done.2.sum_ref = f32[16,48,128]{2,1,0:T(8,128)S(1)} async-done(((f32[16,48,128]{2,1,0:T(8,128)}), f32[16,48,128]{2,1,0:T(8,128)S(1)}, u32[]{:S(2)}, u32[]{:S(2)}) %all-to-all-start.2) | async-done | bytes 393248 | tf_op jit(solution)/shard_map/all_to_all | solution.py:394
  121.8 2.3 filter.2
  124.2 13.1 %all-to-all-start.3 = ((f32[8,8,128]{2,1,0:T(8,128)}), f32[8,8,128]{2,1,0:T(8,128)S(1)}, u32[]{:S(2)}, u32[]{:S(2)}) async-start(f32[8,8,128]{2,1,0:T(8,128)} %get-tuple-element.77), calls=%async_computation.3 | async-start | bytes 65536 | tf_op jit(solution)/shard_map/all_to_all | solution.py:394
  137.5 4.5 %all-to-all-done.3.ends_ref = f32[8,8,128]{2,1,0:T(8,128)S(1)} async-done(((f32[8,8,128]{2,1,0:T(8,128)}), f32[8,8,128]{2,1,0:T(8,128)S(1)}, u32[]{:S(2)}, u32[]{:S(2)}) %all-to-all-start.3) | async-done | bytes 32800 | tf_op jit(solution)/shard_map/all_to_all | solution.py:394
  144.3 11.3 %all_to_all.65.g_ref = bf16[16,48,128]{2,1,0:T(8,128)(2,1)} all-to-all(bf16[16,48,128]{2,1,0:T(8,128)(2,1)} %get-tuple-element.80), channel_id=1, replica_groups=mesh['tm'=8,'tile'=16] {'tile'}, dimensions={0} | all-to-all | bytes 393216 | tf_op jit(solution)/shard_map/all_to_all | solution.py:394
  155.6 8.7 %numer.2 = (bf16[128,128]{1,0:T(8,128)(2,1)}, f32[8,64,1152]{2,1,0:T(8,128)}) custom-call(bf16[16,48,128]{2,1,0:T(8,128)(2,1)} %all_to_all.65.g_ref, s32[128,1]{1,0:T(8,128)} %reshape_reshape.8.pick_ref, f32[64,128,128]{2,1,0:T(8,128)} %get-tuple-element.81.d_ref, bf16[64,128,128]{2,1,0:T(8,128)(2,1)} %get-tuple-element.82.drop_ref, ...), custom_call_target="tpu_custom_call" | custom-call | tf_op jit(solution)/shard_map/numer/pallas_call | solution.py:58
  164.3 5.3 %all-to-all-start.5 = ((f32[8,64,1152]{2,1,0:T(8,128)}), f32[8,64,1152]{2,1,0:T(8,128)S(1)}, u32[]{:S(2)}, u32[]{:S(2)}) async-start(f32[8,64,1152]{2,1,0:T(8,128)} %get-tuple-element.83), calls=%async_computation.5 | async-start | bytes 4718592 | tf_op jit(solution)/shard_map/all_to_all | solution.py:394
  170.3 28.4 %all-to-all-done.5.parts_ref = f32[8,64,1152]{2,1,0:T(8,128)S(1)} async-done(((f32[8,64,1152]{2,1,0:T(8,128)}), f32[8,64,1152]{2,1,0:T(8,128)S(1)}, u32[]{:S(2)}, u32[]{:S(2)}) %all-to-all-start.5) | async-done | bytes 2359328 | tf_op jit(solution)/shard_map/all_to_all | solution.py:394
  200.1 3.2 update.2
  203.3 20.1 %all_to_all.66.fb_ref = bf16[8,64,1024]{2,1,0:T(8,128)(2,1)} all-to-all(bf16[8,64,1024]{2,1,0:T(8,128)(2,1)} %update.2), channel_id=1, replica_groups=mesh['tm'=8,'tile'=16] {'tm'}, dimensions={0} | all-to-all | bytes 2097152 | tf_op jit(solution)/shard_map/all_to_all | solution.py:394
  223.5 12.4 %left1.1 = (bf16[8,1024,128]{2,1,0:T(8,128)(2,1)}, f32[64,128,128]{2,1,0:T(8,128)}, bf16[64,128,128]{2,1,0:T(8,128)(2,1)}, bf16[12,128,128]{2,1,0:T(8,128)(2,1)}...) custom-call(bf16[8,64,1024]{2,1,0:T(8,128)(2,1)} %all_to_all.66.fb_r, ...), custom_call_target="tpu_custom_call" | custom-call | tf_op jit(solution)/shard_map/left1/pallas_call | solution.py:58
  239.1 2.0 collective-permute-start.10
  242.5 5.8 %collective-permute-start.12 = (bf16[12,16,128]{2,1,0:T(8,128)(2,1)}, bf16[12,16,128]{2,1,0:T(8,128)(2,1)S(1)}, u32[]{:S(2)}, u32[]{:S(2)}) collective-permute-start(bf16[12,16,128]{2,1,0:T(8,128)(2,1)} %get-tuple-element.90), channel_id=1, source_target_pairs={{0,5},{1,6},{2,7},{4,9},{5,10},{6,11},{8,13},{9,14},{10,15},{16,21... | collective-permute-start | bytes 147464 | tf_op jit(solution)/shard_map/ppermute | solution.py:407
  252.4 2.4 major.3.major_ref
  254.8 12.9 %collective-permute-done.15.se = bf16[12,16,128]{2,1,0:T(8,128)(2,1)S(1)} collective-permute-done((bf16[12,16,128]{2,1,0:T(8,128)(2,1)}, bf16[12,16,128]{2,1,0:T(8,128)(2,1)S(1)}, u32[]{:S(2)}, u32[]{:S(2)}) %collective-permute-start.15) | collective-permute-done | bytes 49184 | tf_op jit(solution)/shard_map/ppermute | solution.py:407
  268.8 9.5 %stencil.3 = (bf16[64,128,128]{2,1,0:T(8,128)(2,1)}, f32[16,48,128]{2,1,0:T(8,128)}) custom-call(s32[8,2]{1,0:T(8,128)} %copy.24.off_ref, f32[8]{0:T(128)} %coef_ref.3, bf16[64,128,128]{2,1,0:T(8,128)(2,1)} %get-tuple-element.85.left_ref, bf16[12,128,128]{2,1,0:T(8,128)(2,1)} %copy-done.9, bf16[12,128,128]{2,1,0:T(8,128)(2,1)} %copy-done.11, ...), custom_call_target="tpu_custom_call" | custom-call | tf_op jit(solution)/shard_map/stencil/pallas_call | solution.py:58
  278.3 13.9 %all_to_all.67.sum_ref = f32[16,48,128]{2,1,0:T(8,128)} all-to-all(f32[16,48,128]{2,1,0:T(8,128)} %get-tuple-element.95), channel_id=1, replica_groups=mesh['tm'=8,'tile'=16] {'tile'}, dimensions={0} | all-to-all | bytes 786432 | tf_op jit(solution)/shard_map/all_to_all | solution.py:394
  292.1 2.3 filter.3
  294.5 17.0 %all_to_all.68.ends_ref = f32[8,8,128]{2,1,0:T(8,128)} all-to-all(f32[8,8,128]{2,1,0:T(8,128)} %get-tuple-element.97), channel_id=1, replica_groups=mesh['tm'=8,'tile'=16] {'tm'}, dimensions={0} | all-to-all | bytes 65536 | tf_op jit(solution)/shard_map/all_to_all | solution.py:394
  313.2 11.3 %all_to_all.69.g_ref = bf16[16,48,128]{2,1,0:T(8,128)(2,1)} all-to-all(bf16[16,48,128]{2,1,0:T(8,128)(2,1)} %get-tuple-element.101), channel_id=1, replica_groups=mesh['tm'=8,'tile'=16] {'tile'}, dimensions={0} | all-to-all | bytes 393216 | tf_op jit(solution)/shard_map/all_to_all | solution.py:394
  324.5 8.7 %numer.3 = (bf16[128,128]{1,0:T(8,128)(2,1)}, f32[8,64,1152]{2,1,0:T(8,128)}) custom-call(bf16[16,48,128]{2,1,0:T(8,128)(2,1)} %all_to_all.69.g_ref, s32[128,1]{1,0:T(8,128)} %reshape_reshape.8.pick_ref, f32[64,128,128]{2,1,0:T(8,128)} %get-tuple-element.81.d_ref, bf16[64,128,128]{2,1,0:T(8,128)(2,1)} %get-tuple-element.102.drop_ref, ...), custom_call_target="tpu_custom_call" | custom-call | tf_op jit(solution)/shard_map/numer/pallas_call | solution.py:58
  333.2 5.3 %all-to-all-start.10 = ((f32[8,64,1152]{2,1,0:T(8,128)}), f32[8,64,1152]{2,1,0:T(8,128)S(1)}, u32[]{:S(2)}, u32[]{:S(2)}) async-start(f32[8,64,1152]{2,1,0:T(8,128)} %get-tuple-element.104), calls=%async_computation.10 | async-start | bytes 4718592 | tf_op jit(solution)/shard_map/all_to_all | solution.py:394
  338.6 6.0 %turn.1 = bf16[16,2,8,4096]{3,2,1,0:T(8,128)(2,1)} custom-call(bf16[64,128,128]{2,1,0:T(8,128)(2,1)} %get-tuple-element.102.drop_ref), custom_call_target="tpu_custom_call" | custom-call | tf_op jit(solution)/shard_map/turn/pallas_call | solution.py:58
  344.6 23.0 %all-to-all-done.10.parts_ref = f32[8,64,1152]{2,1,0:T(8,128)S(1)} async-done(((f32[8,64,1152]{2,1,0:T(8,128)}), f32[8,64,1152]{2,1,0:T(8,128)S(1)}, u32[]{:S(2)}, u32[]{:S(2)}) %all-to-all-start.10) | async-done | bytes 2359328 | tf_op jit(solution)/shard_map/all_to_all | solution.py:394
  369.0 4.4 %all-to-all-start.12 = ((bf16[16,2,8,4096]{3,2,1,0:T(8,128)(2,1)}), bf16[16,2,8,4096]{3,2,1,0:T(8,128)(2,1)}, u32[]{:S(2)}, u32[]{:S(2)}) async-start(bf16[16,2,8,4096]{3,2,1,0:T(8,128)(2,1)} %turn.1), calls=%async_computation.12 | async-start | bytes 4194304 | tf_op jit(solution)/shard_map/all_to_all | solution.py:394
  373.4 3.2 update.3
  376.7 25.0 %all-to-all-done.12 = bf16[16,2,8,4096]{3,2,1,0:T(8,128)(2,1)} async-done(((bf16[16,2,8,4096]{3,2,1,0:T(8,128)(2,1)}), bf16[16,2,8,4096]{3,2,1,0:T(8,128)(2,1)}, u32[]{:S(2)}, u32[]{:S(2)}) %all-to-all-start.12) | async-done | bytes 2097184 | tf_op jit(solution)/shard_map/all_to_all | solution.py:394
  401.6 6.6 %all-to-all-start.11 = ((bf16[8,64,1024]{2,1,0:T(8,128)(2,1)}), bf16[8,64,1024]{2,1,0:T(8,128)(2,1)S(1)}, u32[]{:S(2)}, u32[]{:S(2)}) async-start(bf16[8,64,1024]{2,1,0:T(8,128)(2,1)} %update.3), calls=%async_computation.11 | async-start | bytes 2097152 | tf_op jit(solution)/shard_map/all_to_all | solution.py:394
  408.3 4.1 copy.32
  412.4 10.9 %all-to-all-done.11.fb_ref = bf16[8,64,1024]{2,1,0:T(8,128)(2,1)S(1)} async-done(((bf16[8,64,1024]{2,1,0:T(8,128)(2,1)}), bf16[8,64,1024]{2,1,0:T(8,128)(2,1)S(1)}, u32[]{:S(2)}, u32[]{:S(2)}) %all-to-all-start.11) | async-done | bytes 1048608 | tf_op jit(solution)/shard_map/all_to_all | solution.py:394
  424.2 2.7 split.1
  426.9 3.3 copy.31
  (108 shorter events, 38.4 us)
Async XLA Ops:
  0.6 21.7 %copy-start = (f32[32,4096]{1,0:T(8,128)S(1)}, f32[32,4096]{1,0:T(8,128)}, u32[]{:S(2)}) copy-start(f32[32,4096]{1,0:T(8,128)} %param.16) | copy-start | bytes 1572868
  2.1 15.7 %all-to-all-start.1 = ((bf16[16,48,128]{2,1,0:T(8,128)(2,1)}), bf16[16,48,128]{2,1,0:T(8,128)(2,1)S(1)}, u32[]{:S(2)}, u32[]{:S(2)}) async-start(bf16[16,48,128]{2,1,0:T(8,128)(2,1)} %broadcast_in_dim.3), calls=%async_computation.1 | async-start | bytes 393216 | tf_op jit(solution)/shard_map/all_to_all | solution.py:394
  18.6 29.6 %all-to-all-start = ((bf16[16,2,8,4096]{3,2,1,0:T(8,128)(2,1)}), bf16[16,2,8,4096]{3,2,1,0:T(8,128)(2,1)S(1)}, u32[]{:S(2)}, u32[]{:S(2)}) async-start(bf16[16,2,8,4096]{3,2,1,0:T(8,128)(2,1)} %bitcast.2), calls=%async_computation | async-start | bytes 4194304 | tf_op jit(solution)/shard_map/all_to_all | solution.py:394
  37.3 5.0 %copy-start.26 = (s32[2]{0:T(128)S(1)}, s32[2]{0:T(128)}, u32[]{:S(2)}) copy-start(s32[2]{0:T(128)} %count_ref.1) | copy-start | bytes 28
  37.3 5.0 %copy-start.30 = (s32[2,64]{1,0:T(2,128)S(1)}, s32[2,64]{1,0:T(2,128)}, u32[]{:S(2)}) copy-start(s32[2,64]{1,0:T(2,128)} %param.19) | copy-start | bytes 1540
  44.9 38.4 %copy-start.29 = (s32[8,2]{0,1:T(2,128)S(1)}, s32[8,2]{0,1:T(2,128)}, u32[]{:S(2)}) copy-start(s32[8,2]{0,1:T(2,128)} %param.21) | copy-start | bytes 196
  48.2 1.3 copy-start.4
  61.7 34.1 %collective-permute-start = (bf16[12,128,128]{2,1,0:T(8,128)(2,1)}, bf16[12,128,128]{2,1,0:T(8,128)(2,1)S(1)}, u32[]{:S(2)}, u32[]{:S(2)}) collective-permute-start(bf16[12,128,128]{2,1,0:T(8,128)(2,1)} %get-tuple-element.67), channel_id=1, source_target_pairs={{0,4},{1,5},{2,6},{3,7},{4,8},{5,9},{6,10},{7,11},{8,12},{9,13},{1... | collective-permute-start | bytes 1179656 | tf_op jit(solution)/shard_map/ppermute | solution.py:407
  63.3 32.5 %collective-permute-start.1 = (bf16[12,128,128]{2,1,0:T(8,128)(2,1)}, bf16[12,128,128]{2,1,0:T(8,128)(2,1)S(1)}, u32[]{:S(2)}, u32[]{:S(2)}) collective-permute-start(bf16[12,128,128]{2,1,0:T(8,128)(2,1)} %get-tuple-element.68), channel_id=1, source_target_pairs={{4,0},{5,1},{6,2},{7,3},{8,4},{9,5},{10,6},{11,7},{12,8},{13,9},{1... | collective-permute-start | bytes 1179656 | tf_op jit(solution)/shard_map/ppermute | solution.py:407
  64.6 31.2 %collective-permute-start.2 = (bf16[64,16,128]{2,1,0:T(8,128)(2,1)}, bf16[64,16,128]{2,1,0:T(8,128)(2,1)S(1)}, u32[]{:S(2)}, u32[]{:S(2)}) collective-permute-start(bf16[64,16,128]{2,1,0:T(8,128)(2,1)} %get-tuple-element.69), channel_id=1, source_target_pairs={{0,1},{1,2},{2,3},{4,5},{5,6},{6,7},{8,9},{9,10},{10,11},{12,13},{... | collective-permute-start | bytes 786440 | tf_op jit(solution)/shard_map/ppermute | solution.py:407
  66.8 28.9 %collective-permute-start.3 = (bf16[64,16,128]{2,1,0:T(8,128)(2,1)}, bf16[64,16,128]{2,1,0:T(8,128)(2,1)S(1)}, u32[]{:S(2)}, u32[]{:S(2)}) collective-permute-start(bf16[64,16,128]{2,1,0:T(8,128)(2,1)} %get-tuple-element.70), channel_id=1, source_target_pairs={{1,0},{2,1},{3,2},{5,4},{6,5},{7,6},{9,8},{10,9},{11,10},{13,12},{... | collective-permute-start | bytes 786440 | tf_op jit(solution)/shard_map/ppermute | solution.py:407
  68.1 9.5 %collective-permute-start.4 = (bf16[12,16,128]{2,1,0:T(8,128)(2,1)}, bf16[12,16,128]{2,1,0:T(8,128)(2,1)S(1)}, u32[]{:S(2)}, u32[]{:S(2)}) collective-permute-start(bf16[12,16,128]{2,1,0:T(8,128)(2,1)} %get-tuple-element.71), channel_id=1, source_target_pairs={{0,5},{1,6},{2,7},{4,9},{5,10},{6,11},{8,13},{9,14},{10,15},{16,21... | collective-permute-start | bytes 147464 | tf_op jit(solution)/shard_map/ppermute | solution.py:407
  77.6 18.2 %copy-start.17 = (bf16[12,16,128]{2,1,0:T(8,128)(2,1)}, bf16[12,16,128]{2,1,0:T(8,128)(2,1)S(1)}, u32[]{:S(2)}) copy-start(bf16[12,16,128]{2,1,0:T(8,128)(2,1)S(1)} %collective-permute-done.4.nw) | copy-start | bytes 147460
  77.6 0.7 collective-permute-start.5
  78.3 17.6 %copy-start.19 = (bf16[12,16,128]{2,1,0:T(8,128)(2,1)}, bf16[12,16,128]{2,1,0:T(8,128)(2,1)S(1)}, u32[]{:S(2)}) copy-start(bf16[12,16,128]{2,1,0:T(8,128)(2,1)S(1)} %collective-permute-done.5.ne) | copy-start | bytes 147460
  78.3 0.7 collective-permute-start.6
  79.0 16.9 %copy-start.21 = (bf16[12,16,128]{2,1,0:T(8,128)(2,1)}, bf16[12,16,128]{2,1,0:T(8,128)(2,1)S(1)}, u32[]{:S(2)}) copy-start(bf16[12,16,128]{2,1,0:T(8,128)(2,1)S(1)} %collective-permute-done.6.sw) | copy-start | bytes 147460
  79.0 16.8 %collective-permute-start.7 = (bf16[12,16,128]{2,1,0:T(8,128)(2,1)}, bf16[12,16,128]{2,1,0:T(8,128)(2,1)S(1)}, u32[]{:S(2)}, u32[]{:S(2)}) collective-permute-start(bf16[12,16,128]{2,1,0:T(8,128)(2,1)} %get-tuple-element.74), channel_id=1, source_target_pairs={{5,0},{6,1},{7,2},{9,4},{10,5},{11,6},{13,8},{14,9},{15,10},{21,16... | collective-permute-start | bytes 147464 | tf_op jit(solution)/shard_map/ppermute | solution.py:407
  95.8 0.9 copy-start.8
  95.8 1.0 copy-start.10
  96.8 16.3 %copy-start.27 = (f32[40]{0:T(128)S(1)}, f32[40]{0:T(128)}, u32[]{:S(2)}) copy-start(f32[40]{0:T(128)} %param.23) | copy-start | bytes 484
  96.8 17.0 %copy-start.28 = (f32[40]{0:T(128)S(1)}, f32[40]{0:T(128)}, u32[]{:S(2)}) copy-start(f32[40]{0:T(128)} %param.24) | copy-start | bytes 484
  96.8 17.7 %copy-start.31 = (f32[40]{0:T(128)S(1)}, f32[40]{0:T(128)}, u32[]{:S(2)}) copy-start(f32[40]{0:T(128)} %param.25) | copy-start | bytes 484
  106.3 14.8 %all-to-all-start.2 = ((f32[16,48,128]{2,1,0:T(8,128)}), f32[16,48,128]{2,1,0:T(8,128)S(1)}, u32[]{:S(2)}, u32[]{:S(2)}) async-start(f32[16,48,128]{2,1,0:T(8,128)} %get-tuple-element.76), calls=%async_computation.2 | async-start | bytes 786432 | tf_op jit(solution)/shard_map/all_to_all | solution.py:394
  124.2 17.8 %all-to-all-start.3 = ((f32[8,8,128]{2,1,0:T(8,128)}), f32[8,8,128]{2,1,0:T(8,128)S(1)}, u32[]{:S(2)}, u32[]{:S(2)}) async-start(f32[8,8,128]{2,1,0:T(8,128)} %get-tuple-element.77), calls=%async_computation.3 | async-start | bytes 65536 | tf_op jit(solution)/shard_map/all_to_all | solution.py:394
  137.5 4.5 %copy-start.25 = (f32[8,128]{1,0:T(8,128)}, f32[8,128]{1,0:T(8,128)S(1)}, u32[]{:S(2)}) copy-start(f32[8,128]{1,0:T(8,128)S(1)} %scatter.9.rates_ref) | copy-start | bytes 12292
  164.3 34.4 %all-to-all-start.5 = ((f32[8,64,1152]{2,1,0:T(8,128)}), f32[8,64,1152]{2,1,0:T(8,128)S(1)}, u32[]{:S(2)}, u32[]{:S(2)}) async-start(f32[8,64,1152]{2,1,0:T(8,128)} %get-tuple-element.83), calls=%async_computation.5 | async-start | bytes 4718592 | tf_op jit(solution)/shard_map/all_to_all | solution.py:394
  198.7 1.4 copy-start.3
  235.8 31.9 %collective-permute-start.8 = (bf16[12,128,128]{2,1,0:T(8,128)(2,1)}, bf16[12,128,128]{2,1,0:T(8,128)(2,1)S(1)}, u32[]{:S(2)}, u32[]{:S(2)}) collective-permute-start(bf16[12,128,128]{2,1,0:T(8,128)(2,1)} %get-tuple-element.86), channel_id=1, source_target_pairs={{0,4},{1,5},{2,6},{3,7},{4,8},{5,9},{6,10},{7,11},{8,12},{9,13},{1... | collective-permute-start | bytes 1179656 | tf_op jit(solution)/shard_map/ppermute | solution.py:407
  237.8 29.9 %collective-permute-start.9 = (bf16[12,128,128]{2,1,0:T(8,128)(2,1)}, bf16[12,128,128]{2,1,0:T(8,128)(2,1)S(1)}, u32[]{:S(2)}, u32[]{:S(2)}) collective-permute-start(bf16[12,128,128]{2,1,0:T(8,128)(2,1)} %get-tuple-element.87), channel_id=1, source_target_pairs={{4,0},{5,1},{6,2},{7,3},{8,4},{9,5},{10,6},{11,7},{12,8},{13,9},{1... | collective-permute-start | bytes 1179656 | tf_op jit(solution)/shard_map/ppermute | solution.py:407
  239.1 28.6 %collective-permute-start.10 = (bf16[64,16,128]{2,1,0:T(8,128)(2,1)}, bf16[64,16,128]{2,1,0:T(8,128)(2,1)S(1)}, u32[]{:S(2)}, u32[]{:S(2)}) collective-permute-start(bf16[64,16,128]{2,1,0:T(8,128)(2,1)} %get-tuple-element.88), channel_id=1, source_target_pairs={{0,1},{1,2},{2,3},{4,5},{5,6},{6,7},{8,9},{9,10},{10,11},{12,13},{... | collective-permute-start | bytes 786440 | tf_op jit(solution)/shard_map/ppermute | solution.py:407
  241.2 26.6 %collective-permute-start.11 = (bf16[64,16,128]{2,1,0:T(8,128)(2,1)}, bf16[64,16,128]{2,1,0:T(8,128)(2,1)S(1)}, u32[]{:S(2)}, u32[]{:S(2)}) collective-permute-start(bf16[64,16,128]{2,1,0:T(8,128)(2,1)} %get-tuple-element.89), channel_id=1, source_target_pairs={{1,0},{2,1},{3,2},{5,4},{6,5},{7,6},{9,8},{10,9},{11,10},{13,12},{... | collective-permute-start | bytes 786440 | tf_op jit(solution)/shard_map/ppermute | solution.py:407
  242.5 7.3 %collective-permute-start.12 = (bf16[12,16,128]{2,1,0:T(8,128)(2,1)}, bf16[12,16,128]{2,1,0:T(8,128)(2,1)S(1)}, u32[]{:S(2)}, u32[]{:S(2)}) collective-permute-start(bf16[12,16,128]{2,1,0:T(8,128)(2,1)} %get-tuple-element.90), channel_id=1, source_target_pairs={{0,5},{1,6},{2,7},{4,9},{5,10},{6,11},{8,13},{9,14},{10,15},{16,21... | collective-permute-start | bytes 147464 | tf_op jit(solution)/shard_map/ppermute | solution.py:407
  249.7 18.1 %copy-start.18 = (bf16[12,16,128]{2,1,0:T(8,128)(2,1)}, bf16[12,16,128]{2,1,0:T(8,128)(2,1)S(1)}, u32[]{:S(2)}) copy-start(bf16[12,16,128]{2,1,0:T(8,128)(2,1)S(1)} %collective-permute-done.12.nw) | copy-start | bytes 147460
  249.7 0.7 collective-permute-start.13
  250.4 17.4 %copy-start.20 = (bf16[12,16,128]{2,1,0:T(8,128)(2,1)}, bf16[12,16,128]{2,1,0:T(8,128)(2,1)S(1)}, u32[]{:S(2)}) copy-start(bf16[12,16,128]{2,1,0:T(8,128)(2,1)S(1)} %collective-permute-done.13.ne) | copy-start | bytes 147460
  250.4 0.7 collective-permute-start.14
  251.1 16.7 %copy-start.22 = (bf16[12,16,128]{2,1,0:T(8,128)(2,1)}, bf16[12,16,128]{2,1,0:T(8,128)(2,1)S(1)}, u32[]{:S(2)}) copy-start(bf16[12,16,128]{2,1,0:T(8,128)(2,1)S(1)} %collective-permute-done.14.sw) | copy-start | bytes 147460
  251.1 16.6 %collective-permute-start.15 = (bf16[12,16,128]{2,1,0:T(8,128)(2,1)}, bf16[12,16,128]{2,1,0:T(8,128)(2,1)S(1)}, u32[]{:S(2)}, u32[]{:S(2)}) collective-permute-start(bf16[12,16,128]{2,1,0:T(8,128)(2,1)} %get-tuple-element.93), channel_id=1, source_target_pairs={{5,0},{6,1},{7,2},{9,4},{10,5},{11,6},{13,8},{14,9},{15,10},{21,16... | collective-permute-start | bytes 147464 | tf_op jit(solution)/shard_map/ppermute | solution.py:407
  267.7 0.8 copy-start.15
  267.8 0.9 copy-start.9
  267.8 1.0 copy-start.11
  333.2 34.4 %all-to-all-start.10 = ((f32[8,64,1152]{2,1,0:T(8,128)}), f32[8,64,1152]{2,1,0:T(8,128)S(1)}, u32[]{:S(2)}, u32[]{:S(2)}) async-start(f32[8,64,1152]{2,1,0:T(8,128)} %get-tuple-element.104), calls=%async_computation.10 | async-start | bytes 4718592 | tf_op jit(solution)/shard_map/all_to_all | solution.py:394
  367.6 1.4 copy-start.2
  369.0 32.6 %all-to-all-start.12 = ((bf16[16,2,8,4096]{3,2,1,0:T(8,128)(2,1)}), bf16[16,2,8,4096]{3,2,1,0:T(8,128)(2,1)}, u32[]{:S(2)}, u32[]{:S(2)}) async-start(bf16[16,2,8,4096]{3,2,1,0:T(8,128)(2,1)} %turn.1), calls=%async_computation.12 | async-start | bytes 4194304 | tf_op jit(solution)/shard_map/all_to_all | solution.py:394
  401.6 21.6 %all-to-all-start.11 = ((bf16[8,64,1024]{2,1,0:T(8,128)(2,1)}), bf16[8,64,1024]{2,1,0:T(8,128)(2,1)S(1)}, u32[]{:S(2)}, u32[]{:S(2)}) async-start(bf16[8,64,1024]{2,1,0:T(8,128)(2,1)} %update.3), calls=%async_computation.11 | async-start | bytes 2097152 | tf_op jit(solution)/shard_map/all_to_all | solution.py:394
  408.3 21.9 %copy-start.1 = (f32[32,4096]{1,0:T(8,128)S(1)}, f32[32,4096]{1,0:T(8,128)}, u32[]{:S(2)}) copy-start(f32[32,4096]{1,0:T(8,128)} %param.16) | copy-start | bytes 1572868
  423.3 1.0 copy-start.5
  (8 other events, 5.5 us)

commit v2 on v1

v2 whole, which is shorter than its diff:
```python
import functools

import jax
import jax.numpy as jnp
from jax import lax
from jax.experimental import pallas as pl
from jax.experimental.pallas import tpu as pltpu
from jax.sharding import PartitionSpec as P

SIDE = 64
WIDE = 128
RAD = 12
STRIP = 16
GRID_W = 8
ITERS = 2
SLOTS = 64
CYCLE = 8
NEUR = 40
NPAD = 48
EPSILON = 1e-06
F32 = jnp.float32
BF16 = jnp.bfloat16


def nt(a, b):
    return lax.dot_general(a, b, (((1,), (1,)), ((), ())), preferred_element_type=F32)


def nn(a, b):
    return lax.dot_general(a, b, (((1,), (0,)), ((), ())), preferred_element_type=F32)


def eye(n):
    return (
        lax.broadcasted_iota(jnp.int32, (n, n), 0) == lax.broadcasted_iota(jnp.int32, (n, n), 1)
    ).astype(BF16)


def three(x):
    high = x.astype(BF16)
    rest = x - high.astype(F32)
    mid = rest.astype(BF16)
    low = (rest - mid.astype(F32)).astype(BF16)
    return high, mid, low


def lane(shape):
    return lax.broadcasted_iota(jnp.int32, shape, len(shape) - 1)


def row(shape):
    return lax.broadcasted_iota(jnp.int32, shape, len(shape) - 2)


def call(body, outs, args, smem=0, scratch=(), name=None, room=6, aliases=None):
    spaces = [pl.BlockSpec(memory_space=pltpu.SMEM)] * smem
    spaces += [pl.BlockSpec(memory_space=pltpu.VMEM)] * (len(args) - smem)
    held = [pltpu.with_memory_space_constraint(a, pltpu.VMEM) for a in args[smem:]]
    return pl.pallas_call(
        body,
        out_shape=[pltpu.VMEM(s, d) for s, d in outs],
        in_specs=spaces,
        out_specs=[pl.BlockSpec(memory_space=pltpu.VMEM)] * len(outs),
        scratch_shapes=list(scratch),
        input_output_aliases=aliases or {},
        compiler_params=pltpu.CompilerParams(vmem_limit_bytes=room << 20),
        name=name,
    )(*args[:smem], *held)


def column(line, rows):
    diagonal = row((rows, WIDE)) == lane((rows, WIDE))
    spread = jnp.where(diagonal, jnp.broadcast_to(line, (rows, WIDE)), 0.0)
    return jnp.sum(spread, axis=1, keepdims=True)


def picked(g_ref, pick_ref):
    keys = g_ref.shape[0] * g_ref.shape[1]
    wanted = column(pick_ref[0:1], WIDE).astype(jnp.int32)
    chosen = (wanted == lane((WIDE, keys))).astype(F32).astype(BF16)
    return nn(chosen, g_ref[...].reshape(keys, WIDE)).astype(BF16)


def doubled(block):
    wide = block.astype(F32)
    first = (lane(wide.shape) & (WIDE - 1)) < SIDE
    upper = jnp.where(first, wide, 0.0)
    return jnp.concatenate([upper, wide - upper], axis=0).astype(BF16)


def baseline_body(base_ref, out_ref):
    unit = eye(256)

    def step(j, carry):
        for t in range(2):
            line = base_ref[t, 0:1, pl.ds(pl.multiple_of(j * 256, 256), 256)]
            parts = three(jnp.broadcast_to(line, (WIDE, 256)))
            col = nt(unit, parts[0]) + nt(unit, parts[1]) + nt(unit, parts[2])
            out_ref[pl.ds(j * 4, 4), t * SIDE : (t + 1) * SIDE, :] = col.reshape(4, SIDE, WIDE)
        return carry

    lax.fori_loop(0, 16, step, 0)


def merge_body(info_ref, fp_ref, out_ref):
    first = lane((SLOTS, WIDE)) < SIDE
    slot = row((SLOTS, WIDE))
    live = slot < jnp.where(first, info_ref[1], info_ref[2])
    for j in range(32):
        a = fp_ref[0, :, j * WIDE : (j + 1) * WIDE].astype(F32)
        b = fp_ref[1, :, j * WIDE : (j + 1) * WIDE].astype(F32)
        even = jnp.where(first, a, pltpu.roll(b, SIDE, 1))
        odd = jnp.where(first, pltpu.roll(a, SIDE, 1), b)
        at = (2 * j) % 8 * WIDE
        out_ref[j // 4, :, at : at + WIDE] = jnp.where(live, even, 0.0).astype(BF16)
        out_ref[j // 4, :, at + WIDE : at + 2 * WIDE] = jnp.where(live, odd, 0.0).astype(BF16)


def split_body(info_ref, *refs):
    blocks, out_ref = refs[:-1], refs[-1]
    first = lane((SLOTS, WIDE)) < SIDE
    for block_ref, j in zip(blocks, owners(info_ref)):
        for k in range(4):
            at = 2 * k * WIDE
            even = block_ref[:, at : at + WIDE].astype(F32)
            odd = block_ref[:, at + WIDE : at + 2 * WIDE].astype(F32)
            a = jnp.where(first, even, pltpu.roll(odd, SIDE, 1))
            b = jnp.where(first, pltpu.roll(even, SIDE, 1), odd)
            to = pl.ds(pl.multiple_of((j * 4 + k) * WIDE, WIDE), WIDE)
            out_ref[0, :, to] = a.astype(BF16)
            out_ref[1, :, to] = b.astype(BF16)


def expand_body(fb_ref, out_ref):
    unit = eye(256)

    def step(j, carry):
        both = doubled(fb_ref[j])
        for k in range(4):
            out_ref[j, k * 256 : (k + 1) * 256, :] = nt(
                unit, both[:, k * 256 : (k + 1) * 256]
            ).astype(BF16)
        return carry

    lax.fori_loop(0, 8, step, 0)


def major_body(fb_ref, out_ref):
    def step(j, total):
        for k in range(8):
            block = fb_ref[j, :, k * WIDE : (k + 1) * WIDE].astype(F32)
            total = total + block * jnp.sum(block, axis=0, keepdims=True)
        return total

    total = lax.fori_loop(0, 8, step, jnp.zeros((SLOTS, WIDE), F32))
    first = lane((SLOTS, WIDE)) < SIDE
    upper = jnp.sum(jnp.where(first, total, 0.0), axis=1, keepdims=True)
    lower = jnp.sum(jnp.where(first, 0.0, total), axis=1, keepdims=True)
    out_ref[...] = jnp.broadcast_to(jnp.concatenate([upper, lower], axis=0), (WIDE, WIDE))


def collect_body(g_ref, lines_ref, out_ref):
    out_ref[...] = picked(g_ref, lines_ref)


def sides(left_ref, west, east):
    west[...] = left_ref[:, :STRIP]
    east[...] = left_ref[:, WIDE - STRIP :]


def first_left_body(x_ref, base_ref, ft_ref, s_ref, d_ref, resid_ref, left_ref, west, east):
    unit = eye(256)
    slots = s_ref[...]

    def step(j, carry):
        halves = []
        for t in range(2):
            part = x_ref[:, t, :, pl.ds(pl.multiple_of(j * 256, 256), 256)].astype(F32)
            part = part.reshape(WIDE, 256).astype(BF16)
            halves.append(nt(unit, part).reshape(4, SIDE, WIDE))
        rows = pl.ds(j * 4, 4)
        clean = jnp.concatenate(halves, axis=1) - base_ref[rows]
        ft = ft_ref[j // 2, pl.ds(pl.multiple_of((j % 2) * 512, 512), 512), :]
        resid = clean - nn(ft, slots).reshape(4, WIDE, WIDE)
        d_ref[rows] = clean
        resid_ref[rows] = resid
        left_ref[rows] = resid.astype(BF16)
        return carry

    lax.fori_loop(0, 16, step, 0)
    sides(left_ref, west, east)


def owners(info_ref):
    x, core = info_ref[0] // 2, info_ref[0] % 2
    found = []
    for side in (core, 1 - core):
        for away in (0, -1, 1, 2):
            found.append(lax.rem(x + away + 4, 4) * 2 + side)
    return found


def next_left_body(info_ref, *refs):
    blocks, (d_ref, s_ref, fb_ref, ft_ref, resid_ref, left_ref, west, east) = refs[:8], refs[8:]
    unit = eye(256)
    slots = s_ref[...]
    for block_ref, j in zip(blocks, owners(info_ref)):
        fb_ref[j] = block_ref[...]
        both = doubled(block_ref[...])
        for k in range(4):
            ft = nt(unit, both[:, k * 256 : (k + 1) * 256]).astype(BF16)
            ft_ref[j, k * 256 : (k + 1) * 256, :] = ft
            rows = pl.ds(j * 8 + k * 2, 2)
            resid = d_ref[rows] - nn(ft, slots).reshape(2, WIDE, WIDE)
            resid_ref[rows] = resid
            left_ref[rows] = resid.astype(BF16)
    sides(left_ref, west, east)


def shelf_body(left_ref, west, east, top, bottom):
    for at, out in ((0, top), (SIDE - RAD, bottom)):
        rows = slice(at, at + RAD)
        out[:, :STRIP] = west[rows]
        out[:, STRIP : STRIP + WIDE] = left_ref[rows]
        out[:, STRIP + WIDE :] = east[rows]


def drops(first, last, info_ref, coef_ref, pad_ref, resid_ref, drop_ref, mis_ref):
    def step(r, carry):
        total = jnp.zeros((WIDE, WIDE), F32)
        for i in range(CYCLE):
            down, right = info_ref[3 + 2 * i], info_ref[4 + 2 * i]
            total = total + coef_ref[i] * pad_ref[r + RAD + down, pl.ds(STRIP + right, WIDE), :]
        drop = total.astype(BF16)
        drop_ref[r] = drop
        mis_ref[r] = (resid_ref[r] - drop.astype(F32)).astype(BF16)
        return carry

    lax.fori_loop(first, last, step, 0)


def projected(blocks, fb_ref, mis_ref):
    total = jnp.zeros((WIDE, WIDE), F32)
    for j in blocks:
        total = total + nn(
            doubled(fb_ref[j]), mis_ref[j * 8 : (j + 1) * 8].reshape(8 * WIDE, WIDE)
        )
    return total


def inner_body(
    info_ref, coef_ref, left_ref, west, east, resid_ref, fb_ref, pad_ref, drop_ref, mis_ref, out_ref
):
    def fill(r, carry):
        pad_ref[RAD + r, STRIP : STRIP + WIDE, :] = left_ref[r].astype(F32)
        pad_ref[RAD + r, :STRIP, :] = west[r].astype(F32)
        pad_ref[RAD + r, STRIP + WIDE :, :] = east[r].astype(F32)
        return carry

    lax.fori_loop(0, SIDE, fill, 0)
    drops(RAD, SIDE - RAD, info_ref, coef_ref, pad_ref, resid_ref, drop_ref, mis_ref)
    out_ref[...] = projected(range(2, 6), fb_ref, mis_ref)


def outer_body(
    info_ref, coef_ref, top, bottom, resid_ref, fb_ref, major_ref, lines_ref, part_ref,
    pad_in, drop_in, mis_in, pad_ref, drop_ref, mis_ref, out_ref,
):
    def fill(r, carry):
        pad_ref[r] = top[r].astype(F32)
        pad_ref[RAD + SIDE + r] = bottom[r].astype(F32)
        return carry

    lax.fori_loop(0, RAD, fill, 0)
    drops(0, RAD, info_ref, coef_ref, pad_ref, resid_ref, drop_ref, mis_ref)
    drops(SIDE - RAD, SIDE, info_ref, coef_ref, pad_ref, resid_ref, drop_ref, mis_ref)
    total = part_ref[...] + projected((0, 1, 6, 7), fb_ref, mis_ref)
    keys = out_ref.shape[0] * NPAD
    chosen = (lines_ref[0:1].astype(jnp.int32) == row((keys, WIDE))).astype(F32).astype(BF16)
    both = jnp.concatenate([total, major_ref[...]], axis=1)
    high, mid, low = three(both)
    found = nn(chosen, high) + nn(chosen, mid) + nn(chosen, low)
    diagonal = row((NPAD, WIDE)) == lane((NPAD, WIDE))
    for b in range(out_ref.shape[0]):
        out_ref[b, :NEUR] = found[b * NPAD : b * NPAD + NEUR, :WIDE]
        spread = jnp.where(diagonal, found[b * NPAD : (b + 1) * NPAD, WIDE:], 0.0)
        out_ref[b, NEUR:NPAD, :] = jnp.broadcast_to(
            jnp.sum(spread, axis=0, keepdims=True), (NPAD - NEUR, WIDE)
        )


def first_order(x, rate):
    at = lane(x.shape)
    power = rate
    for k in range(7):
        x = x + power * jnp.where(at >= (1 << k), pltpu.roll(x, 1 << k, 1), 0.0)
        power = power * power
    return x


def filter_body(sum_ref, traces_ref, lines_ref, a_ref, b_ref, out_ref):
    total = jnp.sum(sum_ref[...], axis=0)
    gradient = total[:NEUR]
    diagonal = row((NEUR, WIDE)) == lane((NEUR, WIDE))
    curvature = column(total[NEUR : NEUR + 1], NEUR)
    decay, rise, cost = (column(lines_ref[k : k + 1], NEUR) for k in (1, 2, 3))
    stepped = traces_ref[...] + gradient / (curvature + EPSILON)
    rectified = jnp.maximum(stepped - cost, 0.0)
    driven = (1.0 - decay) * (1.0 - rise) * rectified
    a = first_order(driven, decay)
    b = first_order(driven, rise)
    a_ref[...] = a
    b_ref[...] = b
    ends = []
    for x in (a, b):
        at_end = jnp.broadcast_to(x[:, WIDE - 1 :], (NEUR, WIDE))
        ends.append(jnp.sum(jnp.where(diagonal, at_end, 0.0), axis=0, keepdims=True))
    ends.append(jnp.zeros((6, WIDE), F32))
    block = jnp.concatenate(ends, axis=0)
    for k in range(out_ref.shape[0]):
        out_ref[k] = block


def entering_body(info_ref, ends_ref, lines_ref, a_ref, b_ref, out_ref, copies_ref):
    here = info_ref[0]
    rates = lines_ref[1:3]
    for _ in range(7):
        rates = rates * rates
    held = jnp.zeros((2, WIDE), F32)
    for k in range(ends_ref.shape[0]):
        held = jnp.where(k < here, rates * held + ends_ref[k, :2], held)
    later = lane((NEUR, WIDE)) + 1

    def whole(x, rate, line):
        powers = jnp.ones((NEUR, WIDE), F32)
        squared = rate
        for k in range(8):
            powers = powers * jnp.where((later >> k) & 1 == 1, squared, 1.0)
            squared = squared * squared
        return x + powers * column(line, NEUR)

    decay, rise = (column(lines_ref[k : k + 1], NEUR) for k in (1, 2))
    a = whole(a_ref[...], decay, held[0:1])
    b = whole(b_ref[...], rise, held[1:2])
    traces = (decay * a - rise * b) / (decay - rise)
    out_ref[...] = traces
    padded = jnp.concatenate([traces, jnp.zeros((NPAD - NEUR, WIDE), F32)], axis=0).astype(BF16)
    for k in range(copies_ref.shape[0]):
        copies_ref[k] = padded


def numer_body(info_ref, g_ref, lines_ref, d_ref, drop_ref, ft_ref, s_ref, keep_ref, send_ref):
    slots = picked(g_ref, lines_ref)
    s_ref[...] = slots
    wide = slots.astype(F32)
    sums = jnp.concatenate(
        [
            jnp.broadcast_to(jnp.sum(wide[:SLOTS], axis=0, keepdims=True), (SLOTS, WIDE)),
            jnp.broadcast_to(jnp.sum(wide[SLOTS:], axis=0, keepdims=True), (SLOTS, WIDE)),
        ],
        axis=0,
    )
    weight = jnp.sum(wide * sums, axis=1, keepdims=True)
    first = lane((SLOTS, WIDE)) < SIDE
    weights = jnp.where(first, weight[:SLOTS], weight[SLOTS:])
    first = (lane((SLOTS, 8 * WIDE)) & (WIDE - 1)) < SIDE
    core = info_ref[0] % 2
    for out_ref, side in ((send_ref, 1 - core), (keep_ref, core)):

        def step(x, carry):
            j = 2 * x + side
            rebuilt = nn(ft_ref[j], slots)
            rows = pl.ds(j * 8, 8)
            clean = d_ref[rows] - drop_ref[rows].astype(F32)
            mis = (clean.reshape(8 * WIDE, WIDE) - rebuilt).astype(BF16)
            both = nt(slots, mis)
            out_ref[x, :, : 8 * WIDE] = jnp.where(first, both[:SLOTS], both[SLOTS:])
            out_ref[x, :, 8 * WIDE :] = weights
            return carry

        lax.fori_loop(0, 4, step, 0)


def fold_body(info_ref, keep_ref, got_ref, own_ref, *out_refs):
    x = info_ref[0] // 2
    own_ref[...] = keep_ref[x] + got_ref[x]
    for away, out_ref in zip((1, -1, 2), out_refs):
        there = lax.rem(x + away + 4, 4)
        out_ref[:, : 8 * WIDE] = (
            keep_ref[there, :, : 8 * WIDE] + got_ref[there, :, : 8 * WIDE]
        ).astype(BF16)
        weights = keep_ref[there, :, 8 * WIDE :] + got_ref[there, :, 8 * WIDE :]
        high = weights.astype(BF16)
        out_ref[:, 8 * WIDE : 9 * WIDE] = high
        out_ref[:, 9 * WIDE :] = (weights - high.astype(F32)).astype(BF16)


def update_body(info_ref, own_ref, one, two, far, fb_ref, out_ref):
    first = lane((SLOTS, WIDE)) < SIDE
    live = row((SLOTS, WIDE)) < jnp.where(first, info_ref[1], info_ref[2])
    here = info_ref[0]
    others = (one, two, far)
    total = own_ref[:, 8 * WIDE :]
    for part in others:
        total = total + (
            part[:, 8 * WIDE : 9 * WIDE].astype(F32) + part[:, 9 * WIDE :].astype(F32)
        )
    divisor = jnp.maximum(total, 1.0)
    for j in range(8):
        lanes = slice(j * WIDE, (j + 1) * WIDE)
        total = own_ref[:, lanes]
        for part in others:
            total = total + part[:, lanes].astype(F32)
        fresh = jnp.maximum(fb_ref[here, :, lanes].astype(F32) + total / divisor, 0.0)
        out_ref[:, lanes] = jnp.where(live, fresh, 0.0).astype(BF16)


def frames_body(drop_ref, out_ref):
    unit = eye(WIDE)

    def step(j, carry):
        for t in range(2):
            part = drop_ref[pl.ds(j * 4, 4), t * SIDE : (t + 1) * SIDE, :].reshape(256, WIDE)
            turned = nt(unit, part).reshape(16, 8, 256)
            out_ref[:, t, :, pl.ds(pl.multiple_of(j * 256, 256), 256)] = turned.astype(BF16)
        return carry

    lax.fori_loop(0, 16, step, 0)


def swapped(x, axis):
    return lax.all_to_all(x, axis, split_axis=0, concat_axis=0, tiled=True)


def moved(piece, down, right):
    count, across = lax.axis_size("tile"), GRID_W // 2
    pairs = []
    for source in range(count):
        y, x = source // across + down, source % across + right
        if 0 <= y < count // across and 0 <= x < across:
            pairs.append((source, y * across + x))
    return lax.ppermute(piece, "tile", pairs)


def along(piece, away):
    return lax.ppermute(piece, "tm", [(k, (k + 2 * away) % 8) for k in range(8)])


def other_core(piece):
    return lax.ppermute(piece, "tm", [(k, k ^ 1) for k in range(8)])


def body(
    movie_frames,
    baseline,
    footprints,
    traces,
    intersection,
    counts,
    offsets,
    cycle_coef,
    decay_rate,
    rise_rate,
    penalty,
):
    tiles, frames = lax.axis_size("tile"), lax.axis_size("tm")
    frames_dev = movie_frames.shape[0]
    pixels = SIDE * SIDE
    here = lax.axis_index("tile")
    block = lax.axis_index("tm").astype(jnp.int32)
    picture = (SIDE, WIDE, WIDE)
    turned_shape = (8, 8 * WIDE, WIDE)
    shape_block = (SLOTS, 8 * WIDE)

    ready = movie_frames.reshape(frames_dev, tiles, 2, pixels).transpose(1, 2, 0, 3)
    local_movie = swapped(ready, "tile")

    ready, traces_later = lax.optimization_barrier((ready, traces))
    padded = jnp.pad(traces_later, ((0, NPAD - NEUR), (0, 0))).astype(BF16)
    gathered = swapped(jnp.broadcast_to(padded, (tiles, NPAD, WIDE)), "tile")

    base = lax.dynamic_slice_in_dim(baseline, here * 2, 2, 0).reshape(2, 1, pixels)
    occupied = jnp.arange(SLOTS, dtype=jnp.int32)[None, :] < counts[:, None]
    owner = intersection // NEUR
    pick = jnp.where(occupied, owner * NPAD + (intersection - owner * NEUR), -1)
    lines = [pick.reshape(1, WIDE).astype(F32)]
    for rate in (decay_rate, rise_rate, penalty):
        lines.append(jnp.pad(rate, (0, WIDE - NEUR)).reshape(1, WIDE))
    lines = jnp.concatenate(lines + [jnp.zeros((4, WIDE), F32)])
    info = jnp.concatenate([block.reshape(1), counts, offsets.reshape(-1)])

    (base_cols,) = call(baseline_body, [(picture, F32)], (base,), name="base")
    (shapes,) = call(
        merge_body,
        [((8, SLOTS, 8 * WIDE), BF16)],
        (info, footprints.transpose(1, 0, 2)),
        smem=1,
        name="merge",
    )
    (turned,) = call(expand_body, [(turned_shape, BF16)], (shapes,), name="expand")
    (slots,) = call(collect_body, [((WIDE, WIDE), BF16)], (gathered, lines), name="collect")
    side_shapes = [((SIDE, STRIP, WIDE), BF16)] * 2
    shelf_shapes = [((RAD, WIDE + 2 * STRIP, WIDE), BF16)] * 2
    pad_shape = (SIDE + 2 * RAD, WIDE + 2 * STRIP, WIDE)
    blocks = by_frame = clean = None
    for iteration in range(ITERS):
        if iteration == 0:
            clean, resid, left, west, east = call(
                first_left_body,
                [(picture, F32), (picture, F32), (picture, BF16)] + side_shapes,
                (local_movie, base_cols, turned, slots),
                name="left0",
            )
        else:
            shapes, turned, resid, left, west, east = call(
                next_left_body,
                [((8, SLOTS, 8 * WIDE), BF16), (turned_shape, BF16), (picture, F32),
                 (picture, BF16)] + side_shapes,
                (info, *blocks, clean, slots),
                smem=1,
                name="left1",
            )
        (major,) = call(major_body, [((WIDE, WIDE), F32)], (shapes,), name="major")
        from_west, from_east = moved(east, 0, 1), moved(west, 0, -1)
        top, bottom = call(shelf_body, shelf_shapes, (left, from_west, from_east), name="shelf")
        from_top, from_bottom = moved(bottom, 1, 0), moved(top, -1, 0)
        pad, drop, mis, part = call(
            inner_body,
            [(pad_shape, F32), (picture, BF16), (picture, BF16), ((WIDE, WIDE), F32)],
            (info, cycle_coef, left, from_west, from_east, resid, shapes),
            smem=2,
            name="inner",
        )
        _, drop, _, terms = call(
            outer_body,
            [(pad_shape, F32), (picture, BF16), (picture, BF16), ((tiles, NPAD, WIDE), F32)],
            (info, cycle_coef, from_top, from_bottom, resid, shapes, major, lines, part,
             pad, drop, mis),
            smem=2,
            name="outer",
            aliases={9: 0, 10: 1, 11: 2},
        )
        arrived = swapped(terms, "tile")
        if iteration == ITERS - 1:
            (by_frame,) = call(
                frames_body, [((tiles, 2, frames_dev, pixels), BF16)], (drop,), name="turn"
            )
            by_frame, arrived = lax.optimization_barrier((by_frame, arrived))
            by_frame = swapped(by_frame, "tile")
        a, b, ends = call(
            filter_body,
            [((NEUR, WIDE), F32), ((NEUR, WIDE), F32), ((frames, 8, WIDE), F32)],
            (arrived, traces, lines),
            name="filter",
        )
        ends = swapped(ends, "tm")
        traces, copies = call(
            entering_body,
            [((NEUR, WIDE), F32), ((tiles, NPAD, WIDE), BF16)],
            (info, ends, lines, a, b),
            smem=1,
            name="entering",
        )
        gathered = swapped(copies, "tile")
        slots, keep, send = call(
            numer_body,
            [((WIDE, WIDE), BF16), ((4, SLOTS, 9 * WIDE), F32), ((4, SLOTS, 9 * WIDE), F32)],
            (info, gathered, lines, clean, drop, turned),
            smem=1,
            name="numer",
        )
        own, *outward = call(
            fold_body,
            [((SLOTS, 9 * WIDE), F32)] + [((SLOTS, 10 * WIDE), BF16)] * 3,
            (info, keep, other_core(send)),
            smem=1,
            name="fold",
        )
        inward = [along(piece, away) for piece, away in zip(outward, (1, -1, 2))]
        (fresh,) = call(
            update_body, [(shape_block, BF16)], (info, own, *inward, shapes), smem=1, name="update"
        )
        blocks = [fresh] + [along(fresh, away) for away in (1, -1, 2)]
        blocks = blocks + [other_core(piece) for piece in blocks]
    backdrop = by_frame.transpose(2, 0, 1, 3).reshape(movie_frames.shape)
    (out_shapes,) = call(
        split_body, [((2, SLOTS, pixels), BF16)], (info, *blocks), smem=1, name="split"
    )
    return (traces, out_shapes.transpose(1, 0, 2), backdrop)


def solution(mesh):
    in_specs = (
        P(("tm", "tile"), None, None),
        P(),
        P(None, "tile", None),
        P("tile", "tm"),
        P("tile", None),
        P("tile"),
        P(),
        P(),
        P("tile"),
        P("tile"),
        P("tile"),
    )
    out_specs = (P("tile", "tm"), P(None, "tile", None), P(("tm", "tile"), None, None))
    return jax.shard_map(body, mesh=mesh, in_specs=in_specs, out_specs=out_specs, check_vma=False)
```

time: 432 us -> 280 us (0.65)
  waiting for transfers between devices: 132 us -> 63.2 us
  Pallas kernels: 107 us -> 55.1 us
  starting transfers between devices: 85.9 us -> 63.7 us
  local copies, waits for them, and re-layouts: 29 us -> 22 us
    all_to_all x8 -> x3, waiting for transfers between devices: 104 us -> 16.7 us  [swapped(): return lax.all_to_all(x, axis, split_axis=0, concat_axis=0, tiled=True)]
    pallas_call x20 -> x26, Pallas kernels: 107 us -> 55.1 us  [call(): pl.pallas_call(body, out_shape=[pltpu.VMEM(s, d) for s, d in outs], in_sp...]
    all_to_all x8 -> x3, starting transfers between devices: 54 us -> 13.8 us  [swapped(): return lax.all_to_all(x, axis, split_axis=0, concat_axis=0, tiled=True)]
    ppermute x0 -> x22, starting transfers between devices: none -> 34 us  [the longest x10 20.3 us: other_core(): return lax.ppermute(piece, 'tm', [(k, k ^ 1) for k in range(8)])]
    ppermute x0 -> x22, waiting for transfers between devices: none -> 19.2 us  [the longest x12 12.8 us: along(): lax.ppermute(piece, 'tm', [(k, (k + 2 * away) % 8) for k in range(8)])]
    ppermute x16 -> x8, starting transfers between devices: 32 us -> 15.9 us  [moved(): return lax.ppermute(piece, 'tile', pairs)]
    unnamed x69 -> x44, local copies, waits for them, and re-layouts: 24.1 us -> 21.7 us
    ppermute x16 -> x8, waiting for transfers between devices: 27.7 us -> 27.3 us  [moved(): return lax.ppermute(piece, 'tile', pairs)]
  transfers between devices with their start and end apart: 24 -> 33, of which waited for: 12 -> 18; matrix products, arithmetic and copies ran while one was open for 4% -> 1% of each run, Pallas kernels for 8% -> 10%
where the time goes in v2:
time: 280 us; the launch traced here: 279 us
  blocking collectives  73.6 us (26%)
  starting transfers between devices  63.7 us (23%)
  waiting for transfers between devices  63.2 us (23%)
  Pallas kernels  55.1 us (20%)
  local copies, waits for them, and re-layouts  22 us (8%)
    all_to_all x6, blocking collectives, swapped(): return lax.all_to_all(x, axis, split_axis=0, concat_axis=0, tiled=True)  73.6 us
    pallas_call x26, Pallas kernels, call(): pl.pallas_call(body, out_shape=[pltpu.VMEM(s, d) for s, d in outs], in_sp...  55.1 us
    ppermute x8, waiting for transfers between devices, moved(): return lax.ppermute(piece, 'tile', pairs)  27.3 us
    unnamed x44, local copies, waits for them, and re-layouts  21.7 us
    ppermute x10, starting transfers between devices, other_core(): return lax.ppermute(piece, 'tm', [(k, k ^ 1) for k in range(8)])  20.3 us
    all_to_all x3, waiting for transfers between devices, swapped(): return lax.all_to_all(x, axis, split_axis=0, concat_axis=0, tiled=True)  16.7 us
    ppermute x8, starting transfers between devices, moved(): return lax.ppermute(piece, 'tile', pairs)  15.9 us
    all_to_all x3, starting transfers between devices, swapped(): return lax.all_to_all(x, axis, split_axis=0, concat_axis=0, tiled=True)  13.8 us
  transfers between devices with their start and end apart: 33, of which 18 were waited for; matrix products, arithmetic and copies ran while one was open for 1% of the time, Pallas kernels for 10%

profile of v2, /device:TPU:1, one launch (start us, length us, event | category | flops | bytes accessed | tf_op | source)
XLA Modules:
  0.0 278.9 jit_solution(8652681303181132904)
XLA Ops:
  0.7 4.1 %copy.26 = bf16[8,32,4096]{2,0,1:T(8,128)(2,1)} copy(bf16[8,32,4096]{2,1,0:T(8,128)(2,1)} %param.11) | data formatting | bytes 4194304 | tf_op args[0]
  4.8 15.5 %all_to_all.45.g_ref = bf16[16,48,128]{2,1,0:T(8,128)(2,1)S(1)} all-to-all(bf16[16,48,128]{2,1,0:T(8,128)(2,1)S(1)} %broadcast_in_dim.10), channel_id=1, replica_groups=mesh['tm'=8,'tile'=16] {'tile'}, dimensions={0} | all-to-all | bytes 393216 | tf_op jit(solution)/shard_map/all_to_all | solution.py:432
  20.4 4.6 %all-to-all-start = ((bf16[16,2,8,4096]{3,2,1,0:T(8,128)(2,1)}), bf16[16,2,8,4096]{3,2,1,0:T(8,128)(2,1)}, u32[]{:S(2)}, u32[]{:S(2)}) async-start(bf16[16,2,8,4096]{3,2,1,0:T(8,128)(2,1)} %bitcast.2), calls=%async_computation | async-start | bytes 4194304 | tf_op jit(solution)/shard_map/all_to_all | solution.py:432
  27.1 2.4 expand.1.ft_ref
  29.6 5.9 %base.1.base_ref = f32[64,128,128]{2,1,0:T(8,128)S(1)} custom-call(f32[2,1,4096]{2,1,0:T(1,128)S(1)} %reshape.48.base_ref), custom_call_target="tpu_custom_call" | custom-call | tf_op jit(solution)/shard_map/base/pallas_call | solution.py:59
  37.9 13.1 %all-to-all-done.x_ref = bf16[16,2,8,4096]{3,2,1,0:T(8,128)(2,1)} async-done(((bf16[16,2,8,4096]{3,2,1,0:T(8,128)(2,1)}), bf16[16,2,8,4096]{3,2,1,0:T(8,128)(2,1)}, u32[]{:S(2)}, u32[]{:S(2)}) %all-to-all-start) | async-done | bytes 2097184 | tf_op jit(solution)/shard_map/all_to_all | solution.py:432
  50.9 2.2 copy-done.5
  53.1 6.0 %left0.1 = (f32[64,128,128]{2,1,0:T(8,128)S(1)}, f32[64,128,128]{2,1,0:T(8,128)S(1)}, bf16[64,128,128]{2,1,0:T(8,128)(2,1)S(1)}, bf16[64,16,128]{2,1,0:T(8,128)(2,1)S(1)}, bf16[64,16,128]{2,1,0:T(8,128)(2,1)S(1)}) custom-call(bf16[16,2,8,4096]{3,2,1,0:T(8,128)(2,1)} %all-to-all-done.x_ref, f32[64,128,128]{2,1,0:T(8,128)S(1)} %copy-done.5, ...), custom_call_target="tpu_custom_call" | custom-call | tf_op jit(solution)/shard_map/left0/pallas_call | solution.py:59
  59.1 2.4 collective-permute-start
  64.8 3.8 %collective-permute-done.1.east = bf16[64,16,128]{2,1,0:T(8,128)(2,1)S(1)} collective-permute-done((bf16[64,16,128]{2,1,0:T(8,128)(2,1)S(1)}, bf16[64,16,128]{2,1,0:T(8,128)(2,1)S(1)}, u32[]{:S(2)}, u32[]{:S(2)}) %collective-permute-start.1) | collective-permute-done | bytes 262176 | tf_op jit(solution)/shard_map/ppermute | solution.py:442
  68.7 4.3 %collective-permute-start.2 = (bf16[12,160,128]{2,1,0:T(8,128)(2,1)S(1)}, bf16[12,160,128]{2,1,0:T(8,128)(2,1)S(1)}, u32[]{:S(2)}, u32[]{:S(2)}) collective-permute-start(bf16[12,160,128]{2,1,0:T(8,128)(2,1)S(1)} %get-tuple-element.60), channel_id=1, source_target_pairs={{0,4},{1,5},{2,6},{3,7},{4,8},{5,9},{6,10},{7,11},{8,12},{9,13},{1... | collective-permute-start | bytes 1474568 | tf_op jit(solution)/shard_map/ppermute | solution.py:442
  74.9 3.4 %inner.2 = (f32[88,160,128]{2,1,0:T(8,128)S(1)}, bf16[64,128,128]{2,1,0:T(8,128)(2,1)S(1)}, bf16[64,128,128]{2,1,0:T(8,128)(2,1)S(1)}, f32[128,128]{1,0:T(8,128)S(1)}) custom-call(s32[19]{0:T(128)S(1)} %pad_add_fusion.info_ref, f32[8]{0:T(128)S(1)} %copy-done.11, bf16[64,128,128]{2,1,0:T(8,128)(2,1)S(1)} %get-tuple-element.57.left_ref, ...), custom_call_target="tpu_custom_call" | custom-call | tf_op jit(solution)/shard_map/inner/pallas_call | solution.py:59
  78.4 2.3 collective-permute-done.2.top
  80.7 3.9 %collective-permute-done.3.bottom = bf16[12,160,128]{2,1,0:T(8,128)(2,1)S(1)} collective-permute-done((bf16[12,160,128]{2,1,0:T(8,128)(2,1)S(1)}, bf16[12,160,128]{2,1,0:T(8,128)(2,1)S(1)}, u32[]{:S(2)}, u32[]{:S(2)}) %collective-permute-start.3) | collective-permute-done | bytes 491552 | tf_op jit(solution)/shard_map/ppermute | solution.py:442
  84.5 2.8 outer.2
  87.3 12.0 %all_to_all.46.sum_ref = f32[16,48,128]{2,1,0:T(8,128)S(1)} all-to-all(f32[16,48,128]{2,1,0:T(8,128)S(1)} %get-tuple-element.67), channel_id=1, replica_groups=mesh['tm'=8,'tile'=16] {'tile'}, dimensions={0} | all-to-all | bytes 786432 | tf_op jit(solution)/shard_map/all_to_all | solution.py:432
  100.0 14.0 %all_to_all.47.ends_ref = f32[8,8,128]{2,1,0:T(8,128)S(1)} all-to-all(f32[8,8,128]{2,1,0:T(8,128)S(1)} %get-tuple-element.68), channel_id=1, replica_groups=mesh['tm'=8,'tile'=16] {'tm'}, dimensions={0} | all-to-all | bytes 65536 | tf_op jit(solution)/shard_map/all_to_all | solution.py:432
  114.7 10.3 %all_to_all.48.g_ref = bf16[16,48,128]{2,1,0:T(8,128)(2,1)S(1)} all-to-all(bf16[16,48,128]{2,1,0:T(8,128)(2,1)S(1)} %get-tuple-element.71), channel_id=1, replica_groups=mesh['tm'=8,'tile'=16] {'tile'}, dimensions={0} | all-to-all | bytes 393216 | tf_op jit(solution)/shard_map/all_to_all | solution.py:432
  125.0 4.3 %numer.2 = (bf16[128,128]{1,0:T(8,128)(2,1)S(1)}, f32[4,64,1152]{2,1,0:T(8,128)S(1)}, f32[4,64,1152]{2,1,0:T(8,128)S(1)}) custom-call(s32[19]{0:T(128)S(1)} %pad_add_fusion.info_ref, bf16[16,48,128]{2,1,0:T(8,128)(2,1)S(1)} %all_to_all.48.g_ref, f32[8,128]{1,0:T(8,128)S(1)} %concatenate.7.lines_ref, f32[64,128,128]{2,1,0:T(8,128)S(1)} %get-tuple-element.72.d_ref.refs_8_, ...), custom_call_target="tpu_custom_call" | custom-call | tf_op jit(solution)/shard_map/numer/pallas_call | solution.py:59
  129.4 2.2 collective-permute-start.4
  131.6 2.5 collective-permute-done.4.got_ref
  135.1 2.4 collective-permute-start.6
  137.5 3.9 %collective-permute-done.5.one = bf16[64,1280]{1,0:T(8,128)(2,1)S(1)} collective-permute-done((bf16[64,1280]{1,0:T(8,128)(2,1)S(1)}, bf16[64,1280]{1,0:T(8,128)(2,1)S(1)}, u32[]{:S(2)}, u32[]{:S(2)}) %collective-permute-start.5) | collective-permute-done | bytes 163872 | tf_op jit(solution)/shard_map/ppermute | solution.py:446
  141.4 2.5 collective-permute-done.7.far
  146.2 2.4 collective-permute-start.9
  150.7 3.6 %collective-permute-start.14 = (bf16[64,1024]{1,0:T(8,128)(2,1)S(1)}, bf16[64,1024]{1,0:T(8,128)(2,1)S(1)}, u32[]{:S(2)}, u32[]{:S(2)}) collective-permute-start(bf16[64,1024]{1,0:T(8,128)(2,1)S(1)} %collective-permute-done.10.refs_3_), channel_id=1, source_target_pairs={{0,16},{16,0},{32,48},{48,32},{64,80},{80,64},{96,112},{112,96},{1... | collective-permute-start | bytes 393224 | tf_op jit(solution)/shard_map/ppermute | solution.py:450
  157.6 6.5 %left1.1 = (bf16[8,64,1024]{2,1,0:T(8,128)(2,1)S(1)}, bf16[8,1024,128]{2,1,0:T(8,128)(2,1)S(1)}, f32[64,128,128]{2,1,0:T(8,128)S(1)}, bf16[64,128,128]{2,1,0:T(8...) custom-call(s32[19]{0:T(128)S(1)} %pad_add_fusion.info_ref, ...), custom_call_target="tpu_custom_call" | custom-call | tf_op jit(solution)/shard_map/left1/pallas_call | solution.py:59
  167.6 4.0 %collective-permute-done.15.west = bf16[64,16,128]{2,1,0:T(8,128)(2,1)S(1)} collective-permute-done((bf16[64,16,128]{2,1,0:T(8,128)(2,1)S(1)}, bf16[64,16,128]{2,1,0:T(8,128)(2,1)S(1)}, u32[]{:S(2)}, u32[]{:S(2)}) %collective-permute-start.15) | collective-permute-done | bytes 262176 | tf_op jit(solution)/shard_map/ppermute | solution.py:442
  171.5 3.8 %collective-permute-done.16.east = bf16[64,16,128]{2,1,0:T(8,128)(2,1)S(1)} collective-permute-done((bf16[64,16,128]{2,1,0:T(8,128)(2,1)S(1)}, bf16[64,16,128]{2,1,0:T(8,128)(2,1)S(1)}, u32[]{:S(2)}, u32[]{:S(2)}) %collective-permute-start.16) | collective-permute-done | bytes 262176 | tf_op jit(solution)/shard_map/ppermute | solution.py:442
  179.2 3.4 %inner.3 = (f32[88,160,128]{2,1,0:T(8,128)S(1)}, bf16[64,128,128]{2,1,0:T(8,128)(2,1)S(1)}, bf16[64,128,128]{2,1,0:T(8,128)(2,1)S(1)}, f32[128,128]{1,0:T(8,128)S(1)}) custom-call(s32[19]{0:T(128)S(1)} %pad_add_fusion.info_ref, f32[8]{0:T(128)S(1)} %copy-done.11, bf16[64,128,128]{2,1,0:T(8,128)(2,1)S(1)} %get-tuple-element.81.left_ref, ...), custom_call_target="tpu_custom_call" | custom-call | tf_op jit(solution)/shard_map/inner/pallas_call | solution.py:59
  182.7 3.7 %collective-permute-done.17.top = bf16[12,160,128]{2,1,0:T(8,128)(2,1)S(1)} collective-permute-done((bf16[12,160,128]{2,1,0:T(8,128)(2,1)S(1)}, bf16[12,160,128]{2,1,0:T(8,128)(2,1)S(1)}, u32[]{:S(2)}, u32[]{:S(2)}) %collective-permute-start.17) | collective-permute-done | bytes 491552 | tf_op jit(solution)/shard_map/ppermute | solution.py:442
  186.4 3.9 %collective-permute-done.18.bottom = bf16[12,160,128]{2,1,0:T(8,128)(2,1)S(1)} collective-permute-done((bf16[12,160,128]{2,1,0:T(8,128)(2,1)S(1)}, bf16[12,160,128]{2,1,0:T(8,128)(2,1)S(1)}, u32[]{:S(2)}, u32[]{:S(2)}) %collective-permute-start.18) | collective-permute-done | bytes 491552 | tf_op jit(solution)/shard_map/ppermute | solution.py:442
  190.3 2.8 outer.3
  193.8 4.7 %all-to-all-start.5 = ((f32[16,48,128]{2,1,0:T(8,128)}), f32[16,48,128]{2,1,0:T(8,128)}, u32[]{:S(2)}, u32[]{:S(2)}) async-start(f32[16,48,128]{2,1,0:T(8,128)} %copy-done.9), calls=%async_computation.5 | async-start | bytes 786432 | tf_op jit(solution)/shard_map/all_to_all | solution.py:432
  198.6 3.1 %turn.1 = bf16[16,2,8,4096]{3,2,1,0:T(8,128)(2,1)S(1)} custom-call(bf16[64,128,128]{2,1,0:T(8,128)(2,1)S(1)} %get-tuple-element.92.drop_ref), custom_call_target="tpu_custom_call" | custom-call | tf_op jit(solution)/shard_map/turn/pallas_call | solution.py:59
  203.0 3.6 %all-to-all-done.5.sum_ref = f32[16,48,128]{2,1,0:T(8,128)} async-done(((f32[16,48,128]{2,1,0:T(8,128)}), f32[16,48,128]{2,1,0:T(8,128)}, u32[]{:S(2)}, u32[]{:S(2)}) %all-to-all-start.5) | async-done | bytes 393248 | tf_op jit(solution)/shard_map/all_to_all | solution.py:432
  208.3 11.4 %all_to_all.49.ends_ref = f32[8,8,128]{2,1,0:T(8,128)S(1)} all-to-all(f32[8,8,128]{2,1,0:T(8,128)S(1)} %get-tuple-element.96), channel_id=1, replica_groups=mesh['tm'=8,'tile'=16] {'tm'}, dimensions={0} | all-to-all | bytes 65536 | tf_op jit(solution)/shard_map/all_to_all | solution.py:432
  220.4 10.3 %all_to_all.50.g_ref = bf16[16,48,128]{2,1,0:T(8,128)(2,1)S(1)} all-to-all(bf16[16,48,128]{2,1,0:T(8,128)(2,1)S(1)} %get-tuple-element.100), channel_id=1, replica_groups=mesh['tm'=8,'tile'=16] {'tile'}, dimensions={0} | all-to-all | bytes 393216 | tf_op jit(solution)/shard_map/all_to_all | solution.py:432
  230.7 4.4 %all-to-all-start.8 = ((bf16[16,2,8,4096]{3,2,1,0:T(8,128)(2,1)}), bf16[16,2,8,4096]{3,2,1,0:T(8,128)(2,1)}, u32[]{:S(2)}, u32[]{:S(2)}) async-start(bf16[16,2,8,4096]{3,2,1,0:T(8,128)(2,1)} %copy-done.6), calls=%async_computation.8 | async-start | bytes 4194304 | tf_op jit(solution)/shard_map/all_to_all | solution.py:432
  235.2 2.2 copy-done.3
  238.9 4.5 %numer.3 = (bf16[128,128]{1,0:T(8,128)(2,1)}, f32[4,64,1152]{2,1,0:T(8,128)S(1)}, f32[4,64,1152]{2,1,0:T(8,128)S(1)}) custom-call(s32[19]{0:T(128)S(1)} %pad_add_fusion.info_ref, bf16[16,48,128]{2,1,0:T(8,128)(2,1)S(1)} %all_to_all.50.g_ref, f32[8,128]{1,0:T(8,128)S(1)} %concatenate.7.lines_ref, f32[64,128,128]{2,1,0:T(8,128)S(1)} %copy-done.3, ...), custom_call_target="tpu_custom_call" | custom-call | tf_op jit(solution)/shard_map/numer/pallas_call | solution.py:59
  245.6 2.5 collective-permute-done.19.got_ref
  249.1 2.4 collective-permute-start.21
  251.5 4.0 %collective-permute-done.20.one = bf16[64,1280]{1,0:T(8,128)(2,1)S(1)} collective-permute-done((bf16[64,1280]{1,0:T(8,128)(2,1)S(1)}, bf16[64,1280]{1,0:T(8,128)(2,1)S(1)}, u32[]{:S(2)}, u32[]{:S(2)}) %collective-permute-start.20) | collective-permute-done | bytes 163872 | tf_op jit(solution)/shard_map/ppermute | solution.py:446
  255.5 2.4 collective-permute-done.22.far
  260.3 2.4 collective-permute-start.24
  264.7 3.8 %collective-permute-start.29 = (bf16[64,1024]{1,0:T(8,128)(2,1)S(1)}, bf16[64,1024]{1,0:T(8,128)(2,1)S(1)}, u32[]{:S(2)}, u32[]{:S(2)}) collective-permute-start(bf16[64,1024]{1,0:T(8,128)(2,1)S(1)} %collective-permute-done.25.refs_3_), channel_id=1, source_target_pairs={{0,16},{16,0},{32,48},{48,32},{64,80},{80,64},{96,112},{112,96},{1... | collective-permute-start | bytes 393224 | tf_op jit(solution)/shard_map/ppermute | solution.py:450
  274.8 4.1 %copy.29 = bf16[8,32,4096]{2,1,0:T(8,128)(2,1)} copy(bf16[8,32,4096]{2,0,1:T(8,128)(2,1)} %bitcast.10) | data formatting | bytes 4194304
  (107 shorter events, 46.8 us)
Async XLA Ops:
  0.6 24.7 %copy-start = (f32[32,4096]{1,0:T(8,128)S(1)}, f32[32,4096]{1,0:T(8,128)}, u32[]{:S(2)}) copy-start(f32[32,4096]{1,0:T(8,128)} %param.12) | copy-start | bytes 1572868
  0.6 4.1 %copy-start.10 = (f32[40,128]{1,0:T(8,128)S(1)}, f32[40,128]{1,0:T(8,128)}, u32[]{:S(2)}) copy-start(f32[40,128]{1,0:T(8,128)} %traces_ref.1) | copy-start | bytes 61444
  20.4 4.6 %copy-start.13 = (s32[2]{0:T(128)S(1)}, s32[2]{0:T(128)}, u32[]{:S(2)}) copy-start(s32[2]{0:T(128)} %param.16) | copy-start | bytes 28
  20.4 4.6 %copy-start.15 = (s32[2,64]{1,0:T(2,128)S(1)}, s32[2,64]{1,0:T(2,128)}, u32[]{:S(2)}) copy-start(s32[2,64]{1,0:T(2,128)} %param.15) | copy-start | bytes 1540
  20.4 4.8 %copy-start.14 = (s32[8,2]{0,1:T(2,128)S(1)}, s32[8,2]{0,1:T(2,128)}, u32[]{:S(2)}) copy-start(s32[8,2]{0,1:T(2,128)} %param.17) | copy-start | bytes 196
  20.4 5.0 %copy-start.12 = (bf16[64,2,4096]{2,1,0:T(2,128)(2,1)S(1)}, bf16[64,2,4096]{2,1,0:T(2,128)(2,1)}, u32[]{:S(2)}) copy-start(bf16[64,2,4096]{2,1,0:T(2,128)(2,1)} %param.13) | copy-start | bytes 3145732
  20.4 30.6 %all-to-all-start = ((bf16[16,2,8,4096]{3,2,1,0:T(8,128)(2,1)}), bf16[16,2,8,4096]{3,2,1,0:T(8,128)(2,1)}, u32[]{:S(2)}, u32[]{:S(2)}) async-start(bf16[16,2,8,4096]{3,2,1,0:T(8,128)(2,1)} %bitcast.2), calls=%async_computation | async-start | bytes 4194304 | tf_op jit(solution)/shard_map/all_to_all | solution.py:432
  29.5 8.0 %copy-start.18 = (f32[40]{0:T(128)S(1)}, f32[40]{0:T(128)}, u32[]{:S(2)}) copy-start(f32[40]{0:T(128)} %param.19) | copy-start | bytes 484
  29.6 8.0 %copy-start.16 = (f32[40]{0:T(128)S(1)}, f32[40]{0:T(128)}, u32[]{:S(2)}) copy-start(f32[40]{0:T(128)} %param.21) | copy-start | bytes 484
  29.6 8.0 %copy-start.17 = (f32[40]{0:T(128)S(1)}, f32[40]{0:T(128)}, u32[]{:S(2)}) copy-start(f32[40]{0:T(128)} %param.20) | copy-start | bytes 484
  50.9 2.2 copy-start.5
  59.1 98.6 %copy-start.2 = (f32[64,128,128]{2,1,0:T(8,128)}, f32[64,128,128]{2,1,0:T(8,128)S(1)}, u32[]{:S(2)}) copy-start(f32[64,128,128]{2,1,0:T(8,128)S(1)} %get-tuple-element.72.d_ref.refs_8_) | copy-start | bytes 12582916
  59.1 15.8 %copy-start.11 = (f32[8]{0:T(128)S(1)}, f32[8]{0:T(128)}, u32[]{:S(2)}) copy-start(f32[8]{0:T(128)} %coef_ref.7) | copy-start | bytes 100
  59.1 5.7 %collective-permute-start = (bf16[64,16,128]{2,1,0:T(8,128)(2,1)S(1)}, bf16[64,16,128]{2,1,0:T(8,128)(2,1)S(1)}, u32[]{:S(2)}, u32[]{:S(2)}) collective-permute-start(bf16[64,16,128]{2,1,0:T(8,128)(2,1)S(1)} %get-tuple-element.58), channel_id=1, source_target_pairs={{0,1},{1,2},{2,3},{4,5},{5,6},{6,7},{8,9},{9,10},{10,11},{12,13},{... | collective-permute-start | bytes 786440 | tf_op jit(solution)/shard_map/ppermute | solution.py:442
  61.5 7.1 %collective-permute-start.1 = (bf16[64,16,128]{2,1,0:T(8,128)(2,1)S(1)}, bf16[64,16,128]{2,1,0:T(8,128)(2,1)S(1)}, u32[]{:S(2)}, u32[]{:S(2)}) collective-permute-start(bf16[64,16,128]{2,1,0:T(8,128)(2,1)S(1)} %get-tuple-element.59), channel_id=1, source_target_pairs={{1,0},{2,1},{3,2},{5,4},{6,5},{7,6},{9,8},{10,9},{11,10},{13,12},{... | collective-permute-start | bytes 786440 | tf_op jit(solution)/shard_map/ppermute | solution.py:442
  68.7 12.0 %collective-permute-start.2 = (bf16[12,160,128]{2,1,0:T(8,128)(2,1)S(1)}, bf16[12,160,128]{2,1,0:T(8,128)(2,1)S(1)}, u32[]{:S(2)}, u32[]{:S(2)}) collective-permute-start(bf16[12,160,128]{2,1,0:T(8,128)(2,1)S(1)} %get-tuple-element.60), channel_id=1, source_target_pairs={{0,4},{1,5},{2,6},{3,7},{4,8},{5,9},{6,10},{7,11},{8,12},{9,13},{1... | collective-permute-start | bytes 1474568 | tf_op jit(solution)/shard_map/ppermute | solution.py:442
  73.1 11.5 %collective-permute-start.3 = (bf16[12,160,128]{2,1,0:T(8,128)(2,1)S(1)}, bf16[12,160,128]{2,1,0:T(8,128)(2,1)S(1)}, u32[]{:S(2)}, u32[]{:S(2)}) collective-permute-start(bf16[12,160,128]{2,1,0:T(8,128)(2,1)S(1)} %get-tuple-element.61), channel_id=1, source_target_pairs={{4,0},{5,1},{6,2},{7,3},{8,4},{9,5},{10,6},{11,7},{12,8},{13,9},{1... | collective-permute-start | bytes 1474568 | tf_op jit(solution)/shard_map/ppermute | solution.py:442
  129.4 4.7 %collective-permute-start.4 = (f32[4,64,1152]{2,1,0:T(8,128)S(1)}, f32[4,64,1152]{2,1,0:T(8,128)S(1)}, u32[]{:S(2)}, u32[]{:S(2)}) collective-permute-start(f32[4,64,1152]{2,1,0:T(8,128)S(1)} %get-tuple-element.75), channel_id=1, source_target_pairs={{0,16},{16,0},{32,48},{48,32},{64,80},{80,64},{96,112},{112,96},{1... | collective-permute-start | bytes 3538952 | tf_op jit(solution)/shard_map/ppermute | solution.py:450
  134.7 6.7 %collective-permute-start.5 = (bf16[64,1280]{1,0:T(8,128)(2,1)S(1)}, bf16[64,1280]{1,0:T(8,128)(2,1)S(1)}, u32[]{:S(2)}, u32[]{:S(2)}) collective-permute-start(bf16[64,1280]{1,0:T(8,128)(2,1)S(1)} %get-tuple-element.77), channel_id=1, source_target_pairs={{0,32},{16,48},{32,64},{48,80},{64,96},{80,112},{96,0},{112,16},{1... | collective-permute-start | bytes 491528 | tf_op jit(solution)/shard_map/ppermute | solution.py:446
  135.1 6.3 %collective-permute-start.6 = (bf16[64,1280]{1,0:T(8,128)(2,1)S(1)}, bf16[64,1280]{1,0:T(8,128)(2,1)S(1)}, u32[]{:S(2)}, u32[]{:S(2)}) collective-permute-start(bf16[64,1280]{1,0:T(8,128)(2,1)S(1)} %get-tuple-element.78), channel_id=1, source_target_pairs={{0,96},{16,112},{32,0},{48,16},{64,32},{80,48},{96,64},{112,80},{1... | collective-permute-start | bytes 491528 | tf_op jit(solution)/shard_map/ppermute | solution.py:446
  137.5 6.4 %collective-permute-start.7 = (bf16[64,1280]{1,0:T(8,128)(2,1)S(1)}, bf16[64,1280]{1,0:T(8,128)(2,1)S(1)}, u32[]{:S(2)}, u32[]{:S(2)}) collective-permute-start(bf16[64,1280]{1,0:T(8,128)(2,1)S(1)} %get-tuple-element.79), channel_id=1, source_target_pairs={{0,64},{16,80},{32,96},{48,112},{64,0},{80,16},{96,32},{112,48},{1... | collective-permute-start | bytes 491528 | tf_op jit(solution)/shard_map/ppermute | solution.py:446
  144.6 6.1 %collective-permute-start.10 = (bf16[64,1024]{1,0:T(8,128)(2,1)S(1)}, bf16[64,1024]{1,0:T(8,128)(2,1)S(1)}, u32[]{:S(2)}, u32[]{:S(2)}) collective-permute-start(bf16[64,1024]{1,0:T(8,128)(2,1)S(1)} %update.2.refs_0_), channel_id=1, source_target_pairs={{0,64},{16,80},{32,96},{48,112},{64,0},{80,16},{96,32},{112,48},{1... | collective-permute-start | bytes 393224 | tf_op jit(solution)/shard_map/ppermute | solution.py:446
  146.2 8.1 %collective-permute-start.9 = (bf16[64,1024]{1,0:T(8,128)(2,1)S(1)}, bf16[64,1024]{1,0:T(8,128)(2,1)S(1)}, u32[]{:S(2)}, u32[]{:S(2)}) collective-permute-start(bf16[64,1024]{1,0:T(8,128)(2,1)S(1)} %update.2.refs_0_), channel_id=1, source_target_pairs={{0,96},{16,112},{32,0},{48,16},{64,32},{80,48},{96,64},{112,80},{1... | collective-permute-start | bytes 393224 | tf_op jit(solution)/shard_map/ppermute | solution.py:446
  148.6 6.4 %collective-permute-start.8 = (bf16[64,1024]{1,0:T(8,128)(2,1)S(1)}, bf16[64,1024]{1,0:T(8,128)(2,1)S(1)}, u32[]{:S(2)}, u32[]{:S(2)}) collective-permute-start(bf16[64,1024]{1,0:T(8,128)(2,1)S(1)} %update.2.refs_0_), channel_id=1, source_target_pairs={{0,32},{16,48},{32,64},{48,80},{64,96},{80,112},{96,0},{112,16},{1... | collective-permute-start | bytes 393224 | tf_op jit(solution)/shard_map/ppermute | solution.py:446
  148.6 8.0 %collective-permute-start.11 = (bf16[64,1024]{1,0:T(8,128)(2,1)S(1)}, bf16[64,1024]{1,0:T(8,128)(2,1)S(1)}, u32[]{:S(2)}, u32[]{:S(2)}) collective-permute-start(bf16[64,1024]{1,0:T(8,128)(2,1)S(1)} %update.2.refs_0_), channel_id=1, source_target_pairs={{0,16},{16,0},{32,48},{48,32},{64,80},{80,64},{96,112},{112,96},{1... | collective-permute-start | bytes 393224 | tf_op jit(solution)/shard_map/ppermute | solution.py:450
  150.7 6.0 %collective-permute-start.14 = (bf16[64,1024]{1,0:T(8,128)(2,1)S(1)}, bf16[64,1024]{1,0:T(8,128)(2,1)S(1)}, u32[]{:S(2)}, u32[]{:S(2)}) collective-permute-start(bf16[64,1024]{1,0:T(8,128)(2,1)S(1)} %collective-permute-done.10.refs_3_), channel_id=1, source_target_pairs={{0,16},{16,0},{32,48},{48,32},{64,80},{80,64},{96,112},{112,96},{1... | collective-permute-start | bytes 393224 | tf_op jit(solution)/shard_map/ppermute | solution.py:450
  154.3 2.3 collective-permute-start.13
  155.0 2.6 collective-permute-start.12
  164.1 18.5 %copy-start.7 = (bf16[8,1024,128]{2,1,0:T(8,128)(2,1)}, bf16[8,1024,128]{2,1,0:T(8,128)(2,1)S(1)}, u32[]{:S(2)}) copy-start(bf16[8,1024,128]{2,1,0:T(8,128)(2,1)S(1)} %get-tuple-element.101.ft_ref) | copy-start | bytes 6291460
  164.1 7.4 %collective-permute-start.15 = (bf16[64,16,128]{2,1,0:T(8,128)(2,1)S(1)}, bf16[64,16,128]{2,1,0:T(8,128)(2,1)S(1)}, u32[]{:S(2)}, u32[]{:S(2)}) collective-permute-start(bf16[64,16,128]{2,1,0:T(8,128)(2,1)S(1)} %get-tuple-element.82), channel_id=1, source_target_pairs={{0,1},{1,2},{2,3},{4,5},{5,6},{6,7},{8,9},{9,10},{10,11},{12,13},{... | collective-permute-start | bytes 786440 | tf_op jit(solution)/shard_map/ppermute | solution.py:442
  166.3 9.1 %collective-permute-start.16 = (bf16[64,16,128]{2,1,0:T(8,128)(2,1)S(1)}, bf16[64,16,128]{2,1,0:T(8,128)(2,1)S(1)}, u32[]{:S(2)}, u32[]{:S(2)}) collective-permute-start(bf16[64,16,128]{2,1,0:T(8,128)(2,1)S(1)} %get-tuple-element.83), channel_id=1, source_target_pairs={{1,0},{2,1},{3,2},{5,4},{6,5},{7,6},{9,8},{10,9},{11,10},{13,12},{... | collective-permute-start | bytes 786440 | tf_op jit(solution)/shard_map/ppermute | solution.py:442
  175.4 11.0 %collective-permute-start.17 = (bf16[12,160,128]{2,1,0:T(8,128)(2,1)S(1)}, bf16[12,160,128]{2,1,0:T(8,128)(2,1)S(1)}, u32[]{:S(2)}, u32[]{:S(2)}) collective-permute-start(bf16[12,160,128]{2,1,0:T(8,128)(2,1)S(1)} %get-tuple-element.84), channel_id=1, source_target_pairs={{0,4},{1,5},{2,6},{3,7},{4,8},{5,9},{6,10},{7,11},{8,12},{9,13},{1... | collective-permute-start | bytes 1474568 | tf_op jit(solution)/shard_map/ppermute | solution.py:442
  177.4 12.9 %collective-permute-start.18 = (bf16[12,160,128]{2,1,0:T(8,128)(2,1)S(1)}, bf16[12,160,128]{2,1,0:T(8,128)(2,1)S(1)}, u32[]{:S(2)}, u32[]{:S(2)}) collective-permute-start(bf16[12,160,128]{2,1,0:T(8,128)(2,1)S(1)} %get-tuple-element.85), channel_id=1, source_target_pairs={{4,0},{5,1},{6,2},{7,3},{8,4},{9,5},{10,6},{11,7},{12,8},{13,9},{1... | collective-permute-start | bytes 1474568 | tf_op jit(solution)/shard_map/ppermute | solution.py:442
  193.8 12.8 %all-to-all-start.5 = ((f32[16,48,128]{2,1,0:T(8,128)}), f32[16,48,128]{2,1,0:T(8,128)}, u32[]{:S(2)}, u32[]{:S(2)}) async-start(f32[16,48,128]{2,1,0:T(8,128)} %copy-done.9), calls=%async_computation.5 | async-start | bytes 786432 | tf_op jit(solution)/shard_map/all_to_all | solution.py:432
  230.7 44.1 %all-to-all-start.8 = ((bf16[16,2,8,4096]{3,2,1,0:T(8,128)(2,1)}), bf16[16,2,8,4096]{3,2,1,0:T(8,128)(2,1)}, u32[]{:S(2)}, u32[]{:S(2)}) async-start(bf16[16,2,8,4096]{3,2,1,0:T(8,128)(2,1)} %copy-done.6), calls=%async_computation.8 | async-start | bytes 4194304 | tf_op jit(solution)/shard_map/all_to_all | solution.py:432
  235.2 2.2 copy-start.3
  243.5 4.6 %collective-permute-start.19 = (f32[4,64,1152]{2,1,0:T(8,128)S(1)}, f32[4,64,1152]{2,1,0:T(8,128)S(1)}, u32[]{:S(2)}, u32[]{:S(2)}) collective-permute-start(f32[4,64,1152]{2,1,0:T(8,128)S(1)} %get-tuple-element.103), channel_id=1, source_target_pairs={{0,16},{16,0},{32,48},{48,32},{64,80},{80,64},{96,112},{112,96},{1... | collective-permute-start | bytes 3538952 | tf_op jit(solution)/shard_map/ppermute | solution.py:450
  248.7 6.8 %collective-permute-start.20 = (bf16[64,1280]{1,0:T(8,128)(2,1)S(1)}, bf16[64,1280]{1,0:T(8,128)(2,1)S(1)}, u32[]{:S(2)}, u32[]{:S(2)}) collective-permute-start(bf16[64,1280]{1,0:T(8,128)(2,1)S(1)} %get-tuple-element.105), channel_id=1, source_target_pairs={{0,32},{16,48},{32,64},{48,80},{64,96},{80,112},{96,0},{112,16},{1... | collective-permute-start | bytes 491528 | tf_op jit(solution)/shard_map/ppermute | solution.py:446
  249.1 6.4 %collective-permute-start.21 = (bf16[64,1280]{1,0:T(8,128)(2,1)S(1)}, bf16[64,1280]{1,0:T(8,128)(2,1)S(1)}, u32[]{:S(2)}, u32[]{:S(2)}) collective-permute-start(bf16[64,1280]{1,0:T(8,128)(2,1)S(1)} %get-tuple-element.106), channel_id=1, source_target_pairs={{0,96},{16,112},{32,0},{48,16},{64,32},{80,48},{96,64},{112,80},{1... | collective-permute-start | bytes 491528 | tf_op jit(solution)/shard_map/ppermute | solution.py:446
  251.5 6.4 %collective-permute-start.22 = (bf16[64,1280]{1,0:T(8,128)(2,1)S(1)}, bf16[64,1280]{1,0:T(8,128)(2,1)S(1)}, u32[]{:S(2)}, u32[]{:S(2)}) collective-permute-start(bf16[64,1280]{1,0:T(8,128)(2,1)S(1)} %get-tuple-element.107), channel_id=1, source_target_pairs={{0,64},{16,80},{32,96},{48,112},{64,0},{80,16},{96,32},{112,48},{1... | collective-permute-start | bytes 491528 | tf_op jit(solution)/shard_map/ppermute | solution.py:446
  258.6 6.1 %collective-permute-start.25 = (bf16[64,1024]{1,0:T(8,128)(2,1)S(1)}, bf16[64,1024]{1,0:T(8,128)(2,1)S(1)}, u32[]{:S(2)}, u32[]{:S(2)}) collective-permute-start(bf16[64,1024]{1,0:T(8,128)(2,1)S(1)} %update.3.refs_0_), channel_id=1, source_target_pairs={{0,64},{16,80},{32,96},{48,112},{64,0},{80,16},{96,32},{112,48},{1... | collective-permute-start | bytes 393224 | tf_op jit(solution)/shard_map/ppermute | solution.py:446
  260.3 8.1 %collective-permute-start.24 = (bf16[64,1024]{1,0:T(8,128)(2,1)S(1)}, bf16[64,1024]{1,0:T(8,128)(2,1)S(1)}, u32[]{:S(2)}, u32[]{:S(2)}) collective-permute-start(bf16[64,1024]{1,0:T(8,128)(2,1)S(1)} %update.3.refs_0_), channel_id=1, source_target_pairs={{0,96},{16,112},{32,0},{48,16},{64,32},{80,48},{96,64},{112,80},{1... | collective-permute-start | bytes 393224 | tf_op jit(solution)/shard_map/ppermute | solution.py:446
  262.7 6.3 %collective-permute-start.23 = (bf16[64,1024]{1,0:T(8,128)(2,1)S(1)}, bf16[64,1024]{1,0:T(8,128)(2,1)S(1)}, u32[]{:S(2)}, u32[]{:S(2)}) collective-permute-start(bf16[64,1024]{1,0:T(8,128)(2,1)S(1)} %update.3.refs_0_), channel_id=1, source_target_pairs={{0,32},{16,48},{32,64},{48,80},{64,96},{80,112},{96,0},{112,16},{1... | collective-permute-start | bytes 393224 | tf_op jit(solution)/shard_map/ppermute | solution.py:446
  262.7 8.6 %collective-permute-start.26 = (bf16[64,1024]{1,0:T(8,128)(2,1)S(1)}, bf16[64,1024]{1,0:T(8,128)(2,1)S(1)}, u32[]{:S(2)}, u32[]{:S(2)}) collective-permute-start(bf16[64,1024]{1,0:T(8,128)(2,1)S(1)} %update.3.refs_0_), channel_id=1, source_target_pairs={{0,16},{16,0},{32,48},{48,32},{64,80},{80,64},{96,112},{112,96},{1... | collective-permute-start | bytes 393224 | tf_op jit(solution)/shard_map/ppermute | solution.py:450
  264.7 6.6 %collective-permute-start.29 = (bf16[64,1024]{1,0:T(8,128)(2,1)S(1)}, bf16[64,1024]{1,0:T(8,128)(2,1)S(1)}, u32[]{:S(2)}, u32[]{:S(2)}) collective-permute-start(bf16[64,1024]{1,0:T(8,128)(2,1)S(1)} %collective-permute-done.25.refs_3_), channel_id=1, source_target_pairs={{0,16},{16,0},{32,48},{48,32},{64,80},{80,64},{96,112},{112,96},{1... | collective-permute-start | bytes 393224 | tf_op jit(solution)/shard_map/ppermute | solution.py:450
  268.5 2.9 %collective-permute-start.28 = (bf16[64,1024]{1,0:T(8,128)(2,1)S(1)}, bf16[64,1024]{1,0:T(8,128)(2,1)S(1)}, u32[]{:S(2)}, u32[]{:S(2)}) collective-permute-start(bf16[64,1024]{1,0:T(8,128)(2,1)S(1)} %collective-permute-done.24.refs_2_), channel_id=1, source_target_pairs={{0,16},{16,0},{32,48},{48,32},{64,80},{80,64},{96,112},{112,96},{1... | collective-permute-start | bytes 393224 | tf_op jit(solution)/shard_map/ppermute | solution.py:450
  269.1 2.7 collective-permute-start.27
  274.8 4.1 %copy-start.1 = (f32[32,4096]{1,0:T(8,128)S(1)}, f32[32,4096]{1,0:T(8,128)}, u32[]{:S(2)}) copy-start(f32[32,4096]{1,0:T(8,128)} %param.12) | copy-start | bytes 1572868
  (4 other events, 5.7 us)

commit v3 on v2

--- a/solution.py
+++ b/solution.py
@@ -52,20 +52,40 @@
     return lax.broadcasted_iota(jnp.int32, shape, len(shape) - 2)
 
 
-def call(body, outs, args, smem=0, scratch=(), name=None, room=6, aliases=None):
-    spaces = [pl.BlockSpec(memory_space=pltpu.SMEM)] * smem
-    spaces += [pl.BlockSpec(memory_space=pltpu.VMEM)] * (len(args) - smem)
-    held = [pltpu.with_memory_space_constraint(a, pltpu.VMEM) for a in args[smem:]]
+def call(body, outs, args, smem=0, scratch=(), name=None, room=6, aliases=None, away=(), space=pltpu.VMEM):
+    spaces, held = [], []
+    for k, arg in enumerate(args):
+        if k < smem:
+            spaces.append(pl.BlockSpec(memory_space=pltpu.SMEM))
+        elif k in away:
+            spaces.append(pl.BlockSpec(memory_space=pl.ANY))
+            arg = pltpu.with_memory_space_constraint(arg, pltpu.HBM)
+        else:
+            spaces.append(pl.BlockSpec(memory_space=pltpu.VMEM))
+            arg = pltpu.with_memory_space_constraint(arg, pltpu.VMEM)
+        held.append(arg)
     return pl.pallas_call(
         body,
-        out_shape=[pltpu.VMEM(s, d) for s, d in outs],
+        out_shape=[space(s, d) for s, d in outs],
         in_specs=spaces,
         out_specs=[pl.BlockSpec(memory_space=pltpu.VMEM)] * len(outs),
         scratch_shapes=list(scratch),
         input_output_aliases=aliases or {},
         compiler_params=pltpu.CompilerParams(vmem_limit_bytes=room << 20),
         name=name,
-    )(*args[:smem], *held)
+    )(*held)
+
+
+def fetches(sources, targets, sems, count):
+    copies = []
+    for k, (source, target) in enumerate(zip(sources, targets)):
+        size = source.shape[0] // count
+        copies.append(
+            lambda j, k=k, source=source, target=target, size=size: pltpu.make_async_copy(
+                source.at[pl.ds(j * size, size)], target.at[pl.ds(j * size, size)], sems.at[k, j]
+            )
+        )
+    return copies
 
 
 def column(line, rows):
@@ -74,11 +94,11 @@
     return jnp.sum(spread, axis=1, keepdims=True)
 
 
-def picked(g_ref, pick_ref):
-    keys = g_ref.shape[0] * g_ref.shape[1]
+def picked(gathered, pick_ref):
+    keys = gathered.shape[0]
     wanted = column(pick_ref[0:1], WIDE).astype(jnp.int32)
     chosen = (wanted == lane((WIDE, keys))).astype(F32).astype(BF16)
-    return nn(chosen, g_ref[...].reshape(keys, WIDE)).astype(BF16)
+    return nn(chosen, gathered).astype(BF16)
 
 
 def doubled(block):
@@ -159,8 +179,63 @@
     out_ref[...] = jnp.broadcast_to(jnp.concatenate([upper, lower], axis=0), (WIDE, WIDE))
 
 
-def collect_body(g_ref, lines_ref, out_ref):
-    out_ref[...] = picked(g_ref, lines_ref)
+def pack_body(movie_ref, traces_ref, out_ref):
+    step = pl.program_id(0)
+
+    @pl.when(step < 8)
+    def _():
+        for k in range(2):
+            part = movie_ref[:, :, k * 256 : (k + 1) * 256].astype(F32)
+            part = jnp.swapaxes(part, 0, 1).reshape(out_ref.shape[0], 2, 8, 256)
+            for t in range(2):
+                out_ref[:, 2 * k + t] = part[:, t].astype(BF16)
+
+    @pl.when(step == 8)
+    def _():
+        padded = jnp.concatenate([traces_ref[...], jnp.zeros((NPAD - NEUR, WIDE), F32)], axis=0)
+        for g in range(3):
+            both = [padded[g * 16 + h * 8 : g * 16 + h * 8 + 8] for h in range(2)]
+            line = jnp.concatenate(both, axis=1).astype(BF16)
+            for d in range(out_ref.shape[0]):
+                out_ref[d, g] = line
+        for d in range(out_ref.shape[0]):
+            out_ref[d, 3] = jnp.zeros((8, 256), BF16)
+
+
+def pack(movie, traces, tiles):
+    last = movie.shape[2] // 512
+    return pl.pallas_call(
+        pack_body,
+        grid=(last + 1,),
+        out_shape=jax.ShapeDtypeStruct((tiles, 4 * (last + 1), 8, 256), BF16),
+        in_specs=[
+            pl.BlockSpec((8, 2 * tiles, 512), lambda j: (0, 0, jnp.minimum(j, last - 1))),
+            pl.BlockSpec((NEUR, WIDE), lambda j: (0, 0)),
+        ],
+        out_specs=pl.BlockSpec((tiles, 4, 8, 256), lambda j: (0, j, 0, 0)),
+        compiler_params=pltpu.CompilerParams(vmem_limit_bytes=8 << 20),
+        name="pack",
+    )(pltpu.with_memory_space_constraint(movie, pltpu.HBM), traces)
+
+
+def unpack_body(in_ref, out_ref):
+    for k in range(2):
+        part = in_ref[:, 2 * k : 2 * k + 2].astype(F32)
+        part = jnp.swapaxes(part.reshape(-1, 8, 256), 0, 1)
+        out_ref[:, :, k * 256 : (k + 1) * 256] = part.astype(BF16)
+
+
+def unpack(chunks):
+    tiles, count = chunks.shape[:2]
+    return pl.pallas_call(
+        unpack_body,
+        grid=(count // 4,),
+        out_shape=jax.ShapeDtypeStruct((8, 2 * tiles, 128 * count), BF16),
+        in_specs=[pl.BlockSpec((tiles, 4, 8, 256), lambda j: (0, j, 0, 0))],
+        out_specs=pl.BlockSpec((8, 2 * tiles, 512), lambda j: (0, 0, j)),
+        compiler_params=pltpu.CompilerParams(vmem_limit_bytes=8 << 20),
+        name="unpack",
+    )(pltpu.with_memory_space_constraint(chunks, pltpu.HBM))
 
 
 def sides(left_ref, west, east):
@@ -168,15 +243,25 @@
     east[...] = left_ref[:, WIDE - STRIP :]
 
 
-def first_left_body(x_ref, base_ref, ft_ref, s_ref, d_ref, resid_ref, left_ref, west, east):
+def first_left_body(
+    x_any, base_any, ft_ref, lines_ref, d_ref, resid_ref, left_ref, west, east,
+    x_ref, base_ref, x_sem, sems,
+):
+    movie = pltpu.make_async_copy(x_any, x_ref, x_sem)
+    movie.start()
+    (base,) = fetches((base_any,), (base_ref,), sems, 4)
+    for j in range(4):
+        base(j).start()
     unit = eye(256)
-    slots = s_ref[...]
+    movie.wait()
+    first = x_ref[:, 32:35].astype(F32)
+    first = jnp.stack([first[..., :WIDE], first[..., WIDE:]], axis=2)
+    slots = picked(first.reshape(-1, WIDE).astype(BF16), lines_ref)
 
     def step(j, carry):
         halves = []
         for t in range(2):
-            part = x_ref[:, t, :, pl.ds(pl.multiple_of(j * 256, 256), 256)].astype(F32)
-            part = part.reshape(WIDE, 256).astype(BF16)
+            part = x_ref[:, 2 * j + t].astype(F32).reshape(WIDE, 256).astype(BF16)
             halves.append(nt(unit, part).reshape(4, SIDE, WIDE))
         rows = pl.ds(j * 4, 4)
         clean = jnp.concatenate(halves, axis=1) - base_ref[rows]
@@ -187,7 +272,9 @@
         left_ref[rows] = resid.astype(BF16)
         return carry
 
-    lax.fori_loop(0, 16, step, 0)
+    for quarter in range(4):
+        base(quarter).wait()
+        lax.fori_loop(quarter * 4, quarter * 4 + 4, step, 0)
     sides(left_ref, west, east)
 
 
@@ -317,12 +404,14 @@
         ends.append(jnp.sum(jnp.where(diagonal, at_end, 0.0), axis=0, keepdims=True))
     ends.append(jnp.zeros((6, WIDE), F32))
     block = jnp.concatenate(ends, axis=0)
-    for k in range(out_ref.shape[0]):
-        out_ref[k] = block
-
-
-def entering_body(info_ref, ends_ref, lines_ref, a_ref, b_ref, out_ref, copies_ref):
+    out_ref[...] = block
+
+
+def entering_body(info_ref, lines_ref, a_ref, b_ref, *refs):
+    ends, (out_ref, copies_ref, ends_ref) = refs[:8], refs[8:]
     here = info_ref[0]
+    for end, j in zip(ends, owners(info_ref)):
+        ends_ref[j] = end[...]
     rates = lines_ref[1:3]
     for _ in range(7):
         rates = rates * rates
@@ -349,8 +438,26 @@
         copies_ref[k] = padded
 
 
-def numer_body(info_ref, g_ref, lines_ref, d_ref, drop_ref, ft_ref, s_ref, keep_ref, send_ref):
-    slots = picked(g_ref, lines_ref)
+def numer_away_body(info_ref, g_ref, lines_ref, d_any, drop_any, ft_any, *refs):
+    outs, (d_ref, drop_ref, ft_ref, sems) = refs[:3], refs[3:]
+    copies = fetches((d_any, drop_any, ft_any), (d_ref, drop_ref, ft_ref), sems, 8)
+    core = info_ref[0] % 2
+    for k in range(8):
+        j = 2 * (k % 4) + (1 - core if k < 4 else core)
+        for copy in copies:
+            copy(j).start()
+
+    def ready(j):
+        for copy in copies:
+            copy(j).wait()
+
+    numer_body(info_ref, g_ref, lines_ref, d_ref, drop_ref, ft_ref, *outs, ready=ready)
+
+
+def numer_body(
+    info_ref, g_ref, lines_ref, d_ref, drop_ref, ft_ref, s_ref, keep_ref, send_ref, ready=None
+):
+    slots = picked(g_ref[...].reshape(-1, WIDE), lines_ref)
     s_ref[...] = slots
     wide = slots.astype(F32)
     sums = jnp.concatenate(
@@ -369,6 +476,8 @@
 
         def step(x, carry):
             j = 2 * x + side
+            if ready is not None:
+                ready(j)
             rebuilt = nn(ft_ref[j], slots)
             rows = pl.ds(j * 8, 8)
             clean = d_ref[rows] - drop_ref[rows].astype(F32)
@@ -421,8 +530,7 @@
     def step(j, carry):
         for t in range(2):
             part = drop_ref[pl.ds(j * 4, 4), t * SIDE : (t + 1) * SIDE, :].reshape(256, WIDE)
-            turned = nt(unit, part).reshape(16, 8, 256)
-            out_ref[:, t, :, pl.ds(pl.multiple_of(j * 256, 256), 256)] = turned.astype(BF16)
+            out_ref[:, 2 * j + t] = nt(unit, part).reshape(-1, 8, 256).astype(BF16)
         return carry
 
     lax.fori_loop(0, 16, step, 0)
@@ -448,6 +556,11 @@
 
 def other_core(piece):
     return lax.ppermute(piece, "tm", [(k, k ^ 1) for k in range(8)])
+
+
+def everyone(piece):
+    pieces = [piece] + [along(piece, away) for away in (1, -1, 2)]
+    return pieces + [other_core(p) for p in pieces]
 
 
 def body(
@@ -472,12 +585,7 @@
     turned_shape = (8, 8 * WIDE, WIDE)
     shape_block = (SLOTS, 8 * WIDE)
 
-    ready = movie_frames.reshape(frames_dev, tiles, 2, pixels).transpose(1, 2, 0, 3)
-    local_movie = swapped(ready, "tile")
-
-    ready, traces_later = lax.optimization_barrier((ready, traces))
-    padded = jnp.pad(traces_later, ((0, NPAD - NEUR), (0, 0))).astype(BF16)
-    gathered = swapped(jnp.broadcast_to(padded, (tiles, NPAD, WIDE)), "tile")
+    local_movie = swapped(pack(movie_frames, traces, tiles), "tile")
 
     base = lax.dynamic_slice_in_dim(baseline, here * 2, 2, 0).reshape(2, 1, pixels)
     occupied = jnp.arange(SLOTS, dtype=jnp.int32)[None, :] < counts[:, None]
@@ -489,7 +597,9 @@
     lines = jnp.concatenate(lines + [jnp.zeros((4, WIDE), F32)])
     info = jnp.concatenate([block.reshape(1), counts, offsets.reshape(-1)])
 
-    (base_cols,) = call(baseline_body, [(picture, F32)], (base,), name="base")
+    (base_cols,) = call(
+        baseline_body, [(picture, F32)], (base,), name="base", space=pltpu.HBM
+    )
     (shapes,) = call(
         merge_body,
         [((8, SLOTS, 8 * WIDE), BF16)],
@@ -498,7 +608,6 @@
         name="merge",
     )
     (turned,) = call(expand_body, [(turned_shape, BF16)], (shapes,), name="expand")
-    (slots,) = call(collect_body, [((WIDE, WIDE), BF16)], (gathered, lines), name="collect")
     side_shapes = [((SIDE, STRIP, WIDE), BF16)] * 2
     shelf_shapes = [((RAD, WIDE + 2 * STRIP, WIDE), BF16)] * 2
     pad_shape = (SIDE + 2 * RAD, WIDE + 2 * STRIP, WIDE)
@@ -508,8 +617,16 @@
             clean, resid, left, west, east = call(
                 first_left_body,
                 [(picture, F32), (picture, F32), (picture, BF16)] + side_shapes,
-                (local_movie, base_cols, turned, slots),
+                (local_movie, base_cols, turned, lines),
                 name="left0",
+                room=16,
+                away=(0, 1),
+                scratch=[
+                    pltpu.VMEM(local_movie.shape, BF16),
+                    pltpu.VMEM(picture, F32),
+                    pltpu.SemaphoreType.DMA,
+                    pltpu.SemaphoreType.DMA((1, 4)),
+                ],
             )
         else:
             shapes, turned, resid, left, west, east = call(
@@ -541,33 +658,49 @@
             aliases={9: 0, 10: 1, 11: 2},
         )
         arrived = swapped(terms, "tile")
-        if iteration == ITERS - 1:
-            (by_frame,) = call(
-                frames_body, [((tiles, 2, frames_dev, pixels), BF16)], (drop,), name="turn"
-            )
-            by_frame, arrived = lax.optimization_barrier((by_frame, arrived))
-            by_frame = swapped(by_frame, "tile")
         a, b, ends = call(
             filter_body,
-            [((NEUR, WIDE), F32), ((NEUR, WIDE), F32), ((frames, 8, WIDE), F32)],
+            [((NEUR, WIDE), F32), ((NEUR, WIDE), F32), ((8, WIDE), F32)],
             (arrived, traces, lines),
             name="filter",
         )
-        ends = swapped(ends, "tm")
+        if iteration == ITERS - 1:
+            drop, ends = lax.optimization_barrier((drop, ends))
+            (by_frame,) = call(
+                frames_body,
+                [((tiles, 32, frames_dev, 256), BF16)],
+                (drop,),
+                name="turn",
+                space=pltpu.HBM,
+            )
+        ends = everyone(ends)
         traces, copies = call(
             entering_body,
             [((NEUR, WIDE), F32), ((tiles, NPAD, WIDE), BF16)],
-            (info, ends, lines, a, b),
+            (info, lines, a, b, *ends),
             smem=1,
             name="entering",
+            scratch=[pltpu.VMEM((frames, 8, WIDE), F32)],
         )
         gathered = swapped(copies, "tile")
+        if iteration == ITERS - 1:
+            by_frame, gathered = lax.optimization_barrier((by_frame, gathered))
+            by_frame = swapped(by_frame, "tile")
+        last = iteration == ITERS - 1
         slots, keep, send = call(
-            numer_body,
+            numer_away_body if last else numer_body,
             [((WIDE, WIDE), BF16), ((4, SLOTS, 9 * WIDE), F32), ((4, SLOTS, 9 * WIDE), F32)],
             (info, gathered, lines, clean, drop, turned),
             smem=1,
             name="numer",
+            room=16 if last else 6,
+            away=(3, 4, 5) if last else (),
+            scratch=[
+                pltpu.VMEM(picture, F32),
+                pltpu.VMEM(picture, BF16),
+                pltpu.VMEM(turned_shape, BF16),
+                pltpu.SemaphoreType.DMA((3, 8)),
+            ] if last else [],
         )
         own, *outward = call(
             fold_body,
@@ -580,9 +713,9 @@
         (fresh,) = call(
             update_body, [(shape_block, BF16)], (info, own, *inward, shapes), smem=1, name="update"
         )
-        blocks = [fresh] + [along(fresh, away) for away in (1, -1, 2)]
-        blocks = blocks + [other_core(piece) for piece in blocks]
-    backdrop = by_frame.transpose(2, 0, 1, 3).reshape(movie_frames.shape)
+        blocks = everyone(fresh)
+    backdrop = unpack(by_frame)
+    backdrop, blocks = lax.optimization_barrier((backdrop, blocks))
     (out_shapes,) = call(
         split_body, [((2, SLOTS, pixels), BF16)], (info, *blocks), smem=1, name="split"
     )

time: 280 us -> 274 us (0.979)
  blocking collectives: 73.6 us -> 35.8 us
  starting transfers between devices: 63.7 us -> 90 us
  Pallas kernels: 55.1 us -> 72.5 us
  local copies, waits for them, and re-layouts: 22 us -> 5.1 us
  waiting for transfers between devices: 63.2 us -> 68.9 us
    all_to_all x6 -> x3, blocking collectives: 73.6 us -> 35.8 us  [swapped(): return lax.all_to_all(x, axis, split_axis=0, concat_axis=0, tiled=True)]
    ppermute x10 -> x18, starting transfers between devices: 20.3 us -> 38.9 us  [other_core(): return lax.ppermute(piece, 'tm', [(k, k ^ 1) for k in range(8)])]
    pallas_call x26 -> x27, Pallas kernels: 55.1 us -> 72.5 us  [the longest x25 60.2 us: call(): pl.pallas_call(body, out_shape=[space(s, d) for s, d in outs], in_specs=s...]
    unnamed x44 -> x36, local copies, waits for them, and re-layouts: 21.7 us -> 4.86 us
    ppermute x12 -> x18, starting transfers between devices: 13.7 us -> 20.9 us  [along(): lax.ppermute(piece, 'tm', [(k, (k + 2 * away) % 8) for k in range(8)])]
    all_to_all x3, waiting for transfers between devices: 16.7 us -> 21.8 us  [swapped(): return lax.all_to_all(x, axis, split_axis=0, concat_axis=0, tiled=True)]
    all_to_all x3, starting transfers between devices: 13.8 us -> 16.8 us  [swapped(): return lax.all_to_all(x, axis, split_axis=0, concat_axis=0, tiled=True)]
    ppermute x10 -> x18, waiting for transfers between devices: 6.31 us -> 7.58 us  [other_core(): return lax.ppermute(piece, 'tm', [(k, k ^ 1) for k in range(8)])]
  transfers between devices with their start and end apart: 33 -> 47, of which waited for: 18 -> 20; matrix products, arithmetic and copies ran while one was open for 1% -> 1% of each run, Pallas kernels for 10% -> 14%
where the time goes in v3:
time: 274 us
  starting transfers between devices  90 us (33%)
  Pallas kernels  72.5 us (26%)
  waiting for transfers between devices  68.9 us (25%)
  blocking collectives  35.8 us (13%)
  local copies, waits for them, and re-layouts  5.1 us (2%)
    pallas_call x25, Pallas kernels, call(): pl.pallas_call(body, out_shape=[space(s, d) for s, d in outs], in_specs=s...  60.2 us
    ppermute x18, starting transfers between devices, other_core(): return lax.ppermute(piece, 'tm', [(k, k ^ 1) for k in range(8)])  38.9 us
    all_to_all x3, blocking collectives, swapped(): return lax.all_to_all(x, axis, split_axis=0, concat_axis=0, tiled=True)  35.8 us
    ppermute x8, waiting for transfers between devices, moved(): return lax.ppermute(piece, 'tile', pairs)  26.6 us
    all_to_all x3, waiting for transfers between devices, swapped(): return lax.all_to_all(x, axis, split_axis=0, concat_axis=0, tiled=True)  21.8 us
    ppermute x18, starting transfers between devices, along(): lax.ppermute(piece, 'tm', [(k, (k + 2 * away) % 8) for k in range(8)])  20.9 us
    all_to_all x3, starting transfers between devices, swapped(): return lax.all_to_all(x, axis, split_axis=0, concat_axis=0, tiled=True)  16.8 us
    ppermute x8, starting transfers between devices, moved(): return lax.ppermute(piece, 'tile', pairs)  13.4 us
  transfers between devices with their start and end apart: 47, of which 20 were waited for; matrix products, arithmetic and copies ran while one was open for 1% of the time, Pallas kernels for 14%

profile of v3, /device:TPU:1, one launch (start us, length us, event | category | flops | bytes accessed | tf_op | source)
XLA Modules:
  0.0 273.6 jit_solution(4465132858286133930)
XLA Ops:
  1.4 6.2 %pack.1 = bf16[16,36,8,256]{3,2,1,0:T(8,128)(2,1)} custom-call(bf16[8,32,4096]{2,1,0:T(8,128)(2,1)} %movie_ref.1, f32[40,128]{1,0:T(8,128)S(1)} %copy-done.6), custom_call_target="tpu_custom_call" | custom-call | tf_op jit(solution)/shard_map/pack/pallas_call | solution.py:207
  7.7 8.8 %all-to-all-start = ((bf16[16,36,8,256]{3,2,1,0:T(8,128)(2,1)}), bf16[16,36,8,256]{3,2,1,0:T(8,128)(2,1)}, u32[]{:S(2)}, u32[]{:S(2)}) async-start(bf16[16,36,8,256]{3,2,1,0:T(8,128)(2,1)} %pack.1), calls=%async_computation | async-start | bytes 4718592 | tf_op jit(solution)/shard_map/all_to_all | solution.py:540
  18.6 2.4 expand.1.ft_ref
  21.0 7.9 %base.1.base_any = f32[64,128,128]{2,1,0:T(8,128)} custom-call(f32[2,1,4096]{2,1,0:T(1,128)S(1)} %reshape.44.base_ref), custom_call_target="tpu_custom_call" | custom-call | tf_op jit(solution)/shard_map/base/pallas_call | solution.py:67
  29.1 19.3 %all-to-all-done.x_any = bf16[16,36,8,256]{3,2,1,0:T(8,128)(2,1)} async-done(((bf16[16,36,8,256]{3,2,1,0:T(8,128)(2,1)}), bf16[16,36,8,256]{3,2,1,0:T(8,128)(2,1)}, u32[]{:S(2)}, u32[]{:S(2)}) %all-to-all-start) | async-done | bytes 2359328 | tf_op jit(solution)/shard_map/all_to_all | solution.py:540
  48.3 7.3 %left0.1 = (f32[64,128,128]{2,1,0:T(8,128)S(1)}, f32[64,128,128]{2,1,0:T(8,128)S(1)}, bf16[64,128,128]{2,1,0:T(8,128)(2,1)S(1)}, bf16[64,16,128]{2,1,0:T(8,128)(2,1)S(1)}, bf16[64,16,128]{2,1,0:T(8,128)(2,1)S(1)}) custom-call(bf16[16,36,8,256]{3,2,1,0:T(8,128)(2,1)} %all-to-all-done.x_any, f32[64,128,128]{2,1,0:T(8,128)} %base.1.base_any, ...), custom_call_target="tpu_custom_call" | custom-call | tf_op jit(solution)/shard_map/left0/pallas_call | solution.py:67
  55.6 2.3 collective-permute-start
  61.3 3.8 %collective-permute-done.1.east = bf16[64,16,128]{2,1,0:T(8,128)(2,1)S(1)} collective-permute-done((bf16[64,16,128]{2,1,0:T(8,128)(2,1)S(1)}, bf16[64,16,128]{2,1,0:T(8,128)(2,1)S(1)}, u32[]{:S(2)}, u32[]{:S(2)}) %collective-permute-start.1) | collective-permute-done | bytes 262176 | tf_op jit(solution)/shard_map/ppermute | solution.py:550
  69.0 3.6 %inner.2 = (f32[88,160,128]{2,1,0:T(8,128)S(1)}, bf16[64,128,128]{2,1,0:T(8,128)(2,1)S(1)}, bf16[64,128,128]{2,1,0:T(8,128)(2,1)S(1)}, f32[128,128]{1,0:T(8,128)S(1)}) custom-call(s32[19]{0:T(128)S(1)} %pad_add_fusion.info_ref, f32[8]{0:T(128)S(1)} %copy-done.8, bf16[64,128,128]{2,1,0:T(8,128)(2,1)S(1)} %get-tuple-element.66.left_ref, ...), custom_call_target="tpu_custom_call" | custom-call | tf_op jit(solution)/shard_map/inner/pallas_call | solution.py:67
  74.2 3.9 %collective-permute-done.3.bottom = bf16[12,160,128]{2,1,0:T(8,128)(2,1)S(1)} collective-permute-done((bf16[12,160,128]{2,1,0:T(8,128)(2,1)S(1)}, bf16[12,160,128]{2,1,0:T(8,128)(2,1)S(1)}, u32[]{:S(2)}, u32[]{:S(2)}) %collective-permute-start.3) | collective-permute-done | bytes 491552 | tf_op jit(solution)/shard_map/ppermute | solution.py:550
  78.1 2.9 %outer.2 = (f32[88,160,128]{2,1,0:T(8,128)S(1)}, bf16[64,128,128]{2,1,0:T(8,128)(2,1)S(1)}, bf16[64,128,128]{2,1,0:T(8,128)(2,1)S(1)}, f32[16,48,128]{2,1,0:T(8,128)S(1)}) custom-call(s32[19]{0:T(128)S(1)} %pad_add_fusion.info_ref, f32[8]{0:T(128)S(1)} %copy-done.8, ...), custom_call_target="tpu_custom_call", output_to_operand_aliasing={{0}: (9, {}), {1}: (10, {}), {2}: (11, {})} | custom-call | tf_op jit(solution)/shard_map/outer/pallas_call | solution.py:67
  81.0 13.0 %all_to_all.30.sum_ref = f32[16,48,128]{2,1,0:T(8,128)S(1)} all-to-all(f32[16,48,128]{2,1,0:T(8,128)S(1)} %get-tuple-element.76), channel_id=1, replica_groups=mesh['tm'=8,'tile'=16] {'tile'}, dimensions={0} | all-to-all | bytes 786432 | tf_op jit(solution)/shard_map/all_to_all | solution.py:540
  94.7 2.8 %collective-permute-start.6 = (f32[8,128]{1,0:T(8,128)S(1)}, f32[8,128]{1,0:T(8,128)S(1)}, u32[]{:S(2)}, u32[]{:S(2)}) collective-permute-start(f32[8,128]{1,0:T(8,128)S(1)} %get-tuple-element.79.refs_0_), channel_id=1, source_target_pairs={{0,64},{16,80},{32,96},{48,112},{64,0},{80,16},{96,32},{112,48},{1... | collective-permute-start | bytes 12296 | tf_op jit(solution)/shard_map/ppermute | solution.py:554
  99.0 6.1 %collective-permute-start.7 = (f32[8,128]{1,0:T(8,128)S(1)}, f32[8,128]{1,0:T(8,128)S(1)}, u32[]{:S(2)}, u32[]{:S(2)}) collective-permute-start(f32[8,128]{1,0:T(8,128)S(1)} %get-tuple-element.79.refs_0_), channel_id=1, source_target_pairs={{0,16},{16,0},{32,48},{48,32},{64,80},{80,64},{96,112},{112,96},{1... | collective-permute-start | bytes 12296 | tf_op jit(solution)/shard_map/ppermute | solution.py:558
  106.7 2.3 collective-permute-start.8
  110.6 10.3 %all_to_all.31.g_ref = bf16[16,48,128]{2,1,0:T(8,128)(2,1)S(1)} all-to-all(bf16[16,48,128]{2,1,0:T(8,128)(2,1)S(1)} %get-tuple-element.80), channel_id=1, replica_groups=mesh['tm'=8,'tile'=16] {'tile'}, dimensions={0} | all-to-all | bytes 393216 | tf_op jit(solution)/shard_map/all_to_all | solution.py:540
  120.8 4.3 %numer.2 = (bf16[128,128]{1,0:T(8,128)(2,1)S(1)}, f32[4,64,1152]{2,1,0:T(8,128)S(1)}, f32[4,64,1152]{2,1,0:T(8,128)S(1)}) custom-call(s32[19]{0:T(128)S(1)} %pad_add_fusion.info_ref, bf16[16,48,128]{2,1,0:T(8,128)(2,1)S(1)} %all_to_all.31.g_ref, f32[8,128]{1,0:T(8,128)S(1)} %concatenate.7.lines_ref, ...), custom_call_target="tpu_custom_call" | custom-call | tf_op jit(solution)/shard_map/numer/pallas_call | solution.py:67
  127.0 2.5 collective-permute-done.11.got_ref
  130.3 2.7 collective-permute-start.13
  132.9 3.9 %collective-permute-done.12.one = bf16[64,1280]{1,0:T(8,128)(2,1)S(1)} collective-permute-done((bf16[64,1280]{1,0:T(8,128)(2,1)S(1)}, bf16[64,1280]{1,0:T(8,128)(2,1)S(1)}, u32[]{:S(2)}, u32[]{:S(2)}) %collective-permute-start.12) | collective-permute-done | bytes 163872 | tf_op jit(solution)/shard_map/ppermute | solution.py:554
  136.9 2.5 collective-permute-done.14.far
  141.7 2.4 collective-permute-start.16
  144.1 2.1 collective-permute-start.18
  146.2 4.0 %collective-permute-start.21 = (bf16[64,1024]{1,0:T(8,128)(2,1)S(1)}, bf16[64,1024]{1,0:T(8,128)(2,1)S(1)}, u32[]{:S(2)}, u32[]{:S(2)}) collective-permute-start(bf16[64,1024]{1,0:T(8,128)(2,1)S(1)} %collective-permute-done.17.refs_3_), channel_id=1, source_target_pairs={{0,16},{16,0},{32,48},{48,32},{64,80},{80,64},{96,112},{112,96},{1... | collective-permute-start | bytes 393224 | tf_op jit(solution)/shard_map/ppermute | solution.py:558
  153.1 6.5 %left1.1 = (bf16[8,64,1024]{2,1,0:T(8,128)(2,1)S(1)}, bf16[8,1024,128]{2,1,0:T(8,128)(2,1)S(1)}, f32[64,128,128]{2,1,0:T(8,128)S(1)}, bf16[64,128,128]{2,1,0:T(8...) custom-call(s32[19]{0:T(128)S(1)} %pad_add_fusion.info_ref, ...), custom_call_target="tpu_custom_call" | custom-call | tf_op jit(solution)/shard_map/left1/pallas_call | solution.py:67
  159.6 2.2 collective-permute-start.22
  163.1 4.0 %collective-permute-done.22.west = bf16[64,16,128]{2,1,0:T(8,128)(2,1)S(1)} collective-permute-done((bf16[64,16,128]{2,1,0:T(8,128)(2,1)S(1)}, bf16[64,16,128]{2,1,0:T(8,128)(2,1)S(1)}, u32[]{:S(2)}, u32[]{:S(2)}) %collective-permute-start.22) | collective-permute-done | bytes 262176 | tf_op jit(solution)/shard_map/ppermute | solution.py:550
  167.1 3.8 %collective-permute-done.23.east = bf16[64,16,128]{2,1,0:T(8,128)(2,1)S(1)} collective-permute-done((bf16[64,16,128]{2,1,0:T(8,128)(2,1)S(1)}, bf16[64,16,128]{2,1,0:T(8,128)(2,1)S(1)}, u32[]{:S(2)}, u32[]{:S(2)}) %collective-permute-start.23) | collective-permute-done | bytes 262176 | tf_op jit(solution)/shard_map/ppermute | solution.py:550
  174.6 3.6 %inner.3 = (f32[88,160,128]{2,1,0:T(8,128)S(1)}, bf16[64,128,128]{2,1,0:T(8,128)(2,1)S(1)}, bf16[64,128,128]{2,1,0:T(8,128)(2,1)S(1)}, f32[128,128]{1,0:T(8,128)S(1)}) custom-call(s32[19]{0:T(128)S(1)} %pad_add_fusion.info_ref, f32[8]{0:T(128)S(1)} %copy-done.8, bf16[64,128,128]{2,1,0:T(8,128)(2,1)S(1)} %get-tuple-element.90.left_ref, ...), custom_call_target="tpu_custom_call" | custom-call | tf_op jit(solution)/shard_map/inner/pallas_call | solution.py:67
  178.2 3.6 %collective-permute-done.24.top = bf16[12,160,128]{2,1,0:T(8,128)(2,1)S(1)} collective-permute-done((bf16[12,160,128]{2,1,0:T(8,128)(2,1)S(1)}, bf16[12,160,128]{2,1,0:T(8,128)(2,1)S(1)}, u32[]{:S(2)}, u32[]{:S(2)}) %collective-permute-start.24) | collective-permute-done | bytes 491552 | tf_op jit(solution)/shard_map/ppermute | solution.py:550
  181.8 3.9 %collective-permute-done.25.bottom = bf16[12,160,128]{2,1,0:T(8,128)(2,1)S(1)} collective-permute-done((bf16[12,160,128]{2,1,0:T(8,128)(2,1)S(1)}, bf16[12,160,128]{2,1,0:T(8,128)(2,1)S(1)}, u32[]{:S(2)}, u32[]{:S(2)}) %collective-permute-start.25) | collective-permute-done | bytes 491552 | tf_op jit(solution)/shard_map/ppermute | solution.py:550
  185.6 2.9 %outer.3 = (f32[88,160,128]{2,1,0:T(8,128)S(1)}, bf16[64,128,128]{2,1,0:T(8,128)(2,1)S(1)}, bf16[64,128,128]{2,1,0:T(8,128)(2,1)S(1)}, f32[16,48,128]{2,1,0:T(8,128)S(1)}) custom-call(s32[19]{0:T(128)S(1)} %pad_add_fusion.info_ref, f32[8]{0:T(128)S(1)} %copy-done.8, ...), custom_call_target="tpu_custom_call", output_to_operand_aliasing={{0}: (9, {}), {1}: (10, {}), {2}: (11, {})} | custom-call | tf_op jit(solution)/shard_map/outer/pallas_call | solution.py:67
  188.6 12.5 %all_to_all.32.sum_ref = f32[16,48,128]{2,1,0:T(8,128)S(1)} all-to-all(f32[16,48,128]{2,1,0:T(8,128)S(1)} %get-tuple-element.101), channel_id=1, replica_groups=mesh['tm'=8,'tile'=16] {'tile'}, dimensions={0} | all-to-all | bytes 786432 | tf_op jit(solution)/shard_map/all_to_all | solution.py:540
  202.7 2.1 collective-permute-start.27
  204.8 4.4 %collective-permute-start.29 = (f32[8,128]{1,0:T(8,128)S(1)}, f32[8,128]{1,0:T(8,128)S(1)}, u32[]{:S(2)}, u32[]{:S(2)}) collective-permute-start(f32[8,128]{1,0:T(8,128)S(1)} %get-tuple-element.107.refs_0_), channel_id=1, source_target_pairs={{0,16},{16,0},{32,48},{48,32},{64,80},{80,64},{96,112},{112,96},{1... | collective-permute-start | bytes 12296 | tf_op jit(solution)/shard_map/ppermute | solution.py:558
  211.0 3.0 %collective-permute-start.30 = (f32[8,128]{1,0:T(8,128)S(1)}, f32[8,128]{1,0:T(8,128)S(1)}, u32[]{:S(2)}, u32[]{:S(2)}) collective-permute-start(f32[8,128]{1,0:T(8,128)S(1)} %collective-permute-done.26.refs_1_), channel_id=1, source_target_pairs={{0,16},{16,0},{32,48},{48,32},{64,80},{80,64},{96,112},{112,96},{1... | collective-permute-start | bytes 12296 | tf_op jit(solution)/shard_map/ppermute | solution.py:558
  216.2 3.5 %all-to-all-start.4 = ((bf16[16,48,128]{2,1,0:T(8,128)(2,1)}), bf16[16,48,128]{2,1,0:T(8,128)(2,1)S(1)}, u32[]{:S(2)}, u32[]{:S(2)}) async-start(bf16[16,48,128]{2,1,0:T(8,128)(2,1)} %copy-done.5), calls=%async_computation.4 | async-start | bytes 393216 | tf_op jit(solution)/shard_map/all_to_all | solution.py:540
  219.8 4.4 %turn.1 = bf16[16,32,8,256]{3,2,1,0:T(8,128)(2,1)} custom-call(bf16[64,128,128]{2,1,0:T(8,128)(2,1)S(1)} %get-tuple-element.109.drop_ref.drop_any), custom_call_target="tpu_custom_call" | custom-call | tf_op jit(solution)/shard_map/turn/pallas_call | solution.py:67
  224.2 2.5 all-to-all-done.4.g_ref
  226.7 4.5 %all-to-all-start.5 = ((bf16[16,32,8,256]{3,2,1,0:T(8,128)(2,1)}), bf16[16,32,8,256]{3,2,1,0:T(8,128)(2,1)}, u32[]{:S(2)}, u32[]{:S(2)}) async-start(bf16[16,32,8,256]{3,2,1,0:T(8,128)(2,1)} %turn.1), calls=%async_computation.5 | async-start | bytes 4194304 | tf_op jit(solution)/shard_map/all_to_all | solution.py:540
  231.2 5.7 %numer.3 = (bf16[128,128]{1,0:T(8,128)(2,1)}, f32[4,64,1152]{2,1,0:T(8,128)S(1)}, f32[4,64,1152]{2,1,0:T(8,128)S(1)}) custom-call(s32[19]{0:T(128)S(1)} %pad_add_fusion.info_ref, bf16[16,48,128]{2,1,0:T(8,128)(2,1)S(1)} %all-to-all-done.4.g_ref, f32[8,128]{1,0:T(8,128)S(1)} %concatenate.7.lines_ref, f32[64,128,128]{2,1,0:T(8,128)} %copy-done.2, ...), custom_call_target="tpu_custom_call" | custom-call | tf_op jit(solution)/shard_map/numer/pallas_call | solution.py:67
  238.8 2.5 collective-permute-done.33.got_ref
  242.0 2.7 collective-permute-start.35
  244.7 4.0 %collective-permute-done.34.one = bf16[64,1280]{1,0:T(8,128)(2,1)S(1)} collective-permute-done((bf16[64,1280]{1,0:T(8,128)(2,1)S(1)}, bf16[64,1280]{1,0:T(8,128)(2,1)S(1)}, u32[]{:S(2)}, u32[]{:S(2)}) %collective-permute-start.34) | collective-permute-done | bytes 163872 | tf_op jit(solution)/shard_map/ppermute | solution.py:554
  248.7 2.5 collective-permute-done.36.far
  253.4 2.5 collective-permute-start.38
  257.9 3.9 %collective-permute-start.43 = (bf16[64,1024]{1,0:T(8,128)(2,1)S(1)}, bf16[64,1024]{1,0:T(8,128)(2,1)S(1)}, u32[]{:S(2)}, u32[]{:S(2)}) collective-permute-start(bf16[64,1024]{1,0:T(8,128)(2,1)S(1)} %collective-permute-done.39.refs_3_), channel_id=1, source_target_pairs={{0,16},{16,0},{32,48},{48,32},{64,80},{80,64},{96,112},{112,96},{1... | collective-permute-start | bytes 393224 | tf_op jit(solution)/shard_map/ppermute | solution.py:558
  264.4 6.1 %unpack.1 = bf16[8,32,4096]{2,1,0:T(8,128)(2,1)} custom-call(bf16[16,32,8,256]{3,2,1,0:T(8,128)(2,1)} %all-to-all-done.5.in_ref), custom_call_target="tpu_custom_call" | custom-call | tf_op jit(solution)/shard_map/unpack/pallas_call | solution.py:230
  (122 shorter events, 48.0 us)
Async XLA Ops:
  7.7 40.7 %all-to-all-start = ((bf16[16,36,8,256]{3,2,1,0:T(8,128)(2,1)}), bf16[16,36,8,256]{3,2,1,0:T(8,128)(2,1)}, u32[]{:S(2)}, u32[]{:S(2)}) async-start(bf16[16,36,8,256]{3,2,1,0:T(8,128)(2,1)} %pack.1), calls=%async_computation | async-start | bytes 4718592 | tf_op jit(solution)/shard_map/all_to_all | solution.py:540
  55.6 97.4 %copy-start.2 = (f32[64,128,128]{2,1,0:T(8,128)}, f32[64,128,128]{2,1,0:T(8,128)S(1)}, u32[]{:S(2)}) copy-start(f32[64,128,128]{2,1,0:T(8,128)S(1)} %get-tuple-element.81.d_ref.refs_8_.d_any) | copy-start | bytes 12582916
  55.6 5.6 %collective-permute-start = (bf16[64,16,128]{2,1,0:T(8,128)(2,1)S(1)}, bf16[64,16,128]{2,1,0:T(8,128)(2,1)S(1)}, u32[]{:S(2)}, u32[]{:S(2)}) collective-permute-start(bf16[64,16,128]{2,1,0:T(8,128)(2,1)S(1)} %get-tuple-element.67), channel_id=1, source_target_pairs={{0,1},{1,2},{2,3},{4,5},{5,6},{6,7},{8,9},{9,10},{10,11},{12,13},{... | collective-permute-start | bytes 786440 | tf_op jit(solution)/shard_map/ppermute | solution.py:550
  58.0 7.1 %collective-permute-start.1 = (bf16[64,16,128]{2,1,0:T(8,128)(2,1)S(1)}, bf16[64,16,128]{2,1,0:T(8,128)(2,1)S(1)}, u32[]{:S(2)}, u32[]{:S(2)}) collective-permute-start(bf16[64,16,128]{2,1,0:T(8,128)(2,1)S(1)} %get-tuple-element.68), channel_id=1, source_target_pairs={{1,0},{2,1},{3,2},{5,4},{6,5},{7,6},{9,8},{10,9},{11,10},{13,12},{... | collective-permute-start | bytes 786440 | tf_op jit(solution)/shard_map/ppermute | solution.py:550
  65.2 9.0 %collective-permute-start.2 = (bf16[12,160,128]{2,1,0:T(8,128)(2,1)S(1)}, bf16[12,160,128]{2,1,0:T(8,128)(2,1)S(1)}, u32[]{:S(2)}, u32[]{:S(2)}) collective-permute-start(bf16[12,160,128]{2,1,0:T(8,128)(2,1)S(1)} %get-tuple-element.69), channel_id=1, source_target_pairs={{0,4},{1,5},{2,6},{3,7},{4,8},{5,9},{6,10},{7,11},{8,12},{9,13},{1... | collective-permute-start | bytes 1474568 | tf_op jit(solution)/shard_map/ppermute | solution.py:550
  67.1 11.0 %collective-permute-start.3 = (bf16[12,160,128]{2,1,0:T(8,128)(2,1)S(1)}, bf16[12,160,128]{2,1,0:T(8,128)(2,1)S(1)}, u32[]{:S(2)}, u32[]{:S(2)}) collective-permute-start(bf16[12,160,128]{2,1,0:T(8,128)(2,1)S(1)} %get-tuple-element.70), channel_id=1, source_target_pairs={{4,0},{5,1},{6,2},{7,3},{8,4},{9,5},{10,6},{11,7},{12,8},{13,9},{1... | collective-permute-start | bytes 1474568 | tf_op jit(solution)/shard_map/ppermute | solution.py:550
  94.7 10.4 %collective-permute-start.6 = (f32[8,128]{1,0:T(8,128)S(1)}, f32[8,128]{1,0:T(8,128)S(1)}, u32[]{:S(2)}, u32[]{:S(2)}) collective-permute-start(f32[8,128]{1,0:T(8,128)S(1)} %get-tuple-element.79.refs_0_), channel_id=1, source_target_pairs={{0,64},{16,80},{32,96},{48,112},{64,0},{80,16},{96,32},{112,48},{1... | collective-permute-start | bytes 12296 | tf_op jit(solution)/shard_map/ppermute | solution.py:554
  97.5 7.7 %collective-permute-start.5 = (f32[8,128]{1,0:T(8,128)S(1)}, f32[8,128]{1,0:T(8,128)S(1)}, u32[]{:S(2)}, u32[]{:S(2)}) collective-permute-start(f32[8,128]{1,0:T(8,128)S(1)} %get-tuple-element.79.refs_0_), channel_id=1, source_target_pairs={{0,96},{16,112},{32,0},{48,16},{64,32},{80,48},{96,64},{112,80},{1... | collective-permute-start | bytes 12296 | tf_op jit(solution)/shard_map/ppermute | solution.py:554
  98.4 8.3 %collective-permute-start.4 = (f32[8,128]{1,0:T(8,128)S(1)}, f32[8,128]{1,0:T(8,128)S(1)}, u32[]{:S(2)}, u32[]{:S(2)}) collective-permute-start(f32[8,128]{1,0:T(8,128)S(1)} %get-tuple-element.79.refs_0_), channel_id=1, source_target_pairs={{0,32},{16,48},{32,64},{48,80},{64,96},{80,112},{96,0},{112,16},{1... | collective-permute-start | bytes 12296 | tf_op jit(solution)/shard_map/ppermute | solution.py:554
  99.0 10.1 %collective-permute-start.7 = (f32[8,128]{1,0:T(8,128)S(1)}, f32[8,128]{1,0:T(8,128)S(1)}, u32[]{:S(2)}, u32[]{:S(2)}) collective-permute-start(f32[8,128]{1,0:T(8,128)S(1)} %get-tuple-element.79.refs_0_), channel_id=1, source_target_pairs={{0,16},{16,0},{32,48},{48,32},{64,80},{80,64},{96,112},{112,96},{1... | collective-permute-start | bytes 12296 | tf_op jit(solution)/shard_map/ppermute | solution.py:558
  105.1 3.9 %collective-permute-start.10 = (f32[8,128]{1,0:T(8,128)S(1)}, f32[8,128]{1,0:T(8,128)S(1)}, u32[]{:S(2)}, u32[]{:S(2)}) collective-permute-start(f32[8,128]{1,0:T(8,128)S(1)} %collective-permute-done.6.refs_3_), channel_id=1, source_target_pairs={{0,16},{16,0},{32,48},{48,32},{64,80},{80,64},{96,112},{112,96},{1... | collective-permute-start | bytes 12296 | tf_op jit(solution)/shard_map/ppermute | solution.py:558
  105.2 3.9 %collective-permute-start.9 = (f32[8,128]{1,0:T(8,128)S(1)}, f32[8,128]{1,0:T(8,128)S(1)}, u32[]{:S(2)}, u32[]{:S(2)}) collective-permute-start(f32[8,128]{1,0:T(8,128)S(1)} %collective-permute-done.5.refs_2_), channel_id=1, source_target_pairs={{0,16},{16,0},{32,48},{48,32},{64,80},{80,64},{96,112},{112,96},{1... | collective-permute-start | bytes 12296 | tf_op jit(solution)/shard_map/ppermute | solution.py:558
  106.7 3.2 %collective-permute-start.8 = (f32[8,128]{1,0:T(8,128)S(1)}, f32[8,128]{1,0:T(8,128)S(1)}, u32[]{:S(2)}, u32[]{:S(2)}) collective-permute-start(f32[8,128]{1,0:T(8,128)S(1)} %collective-permute-done.4.refs_1_), channel_id=1, source_target_pairs={{0,16},{16,0},{32,48},{48,32},{64,80},{80,64},{96,112},{112,96},{1... | collective-permute-start | bytes 12296 | tf_op jit(solution)/shard_map/ppermute | solution.py:558
  125.2 4.4 %collective-permute-start.11 = (f32[4,64,1152]{2,1,0:T(8,128)S(1)}, f32[4,64,1152]{2,1,0:T(8,128)S(1)}, u32[]{:S(2)}, u32[]{:S(2)}) collective-permute-start(f32[4,64,1152]{2,1,0:T(8,128)S(1)} %get-tuple-element.84), channel_id=1, source_target_pairs={{0,16},{16,0},{32,48},{48,32},{64,80},{80,64},{96,112},{112,96},{1... | collective-permute-start | bytes 3538952 | tf_op jit(solution)/shard_map/ppermute | solution.py:558
  130.2 6.7 %collective-permute-start.12 = (bf16[64,1280]{1,0:T(8,128)(2,1)S(1)}, bf16[64,1280]{1,0:T(8,128)(2,1)S(1)}, u32[]{:S(2)}, u32[]{:S(2)}) collective-permute-start(bf16[64,1280]{1,0:T(8,128)(2,1)S(1)} %get-tuple-element.86), channel_id=1, source_target_pairs={{0,32},{16,48},{32,64},{48,80},{64,96},{80,112},{96,0},{112,16},{1... | collective-permute-start | bytes 491528 | tf_op jit(solution)/shard_map/ppermute | solution.py:554
  130.3 6.6 %collective-permute-start.13 = (bf16[64,1280]{1,0:T(8,128)(2,1)S(1)}, bf16[64,1280]{1,0:T(8,128)(2,1)S(1)}, u32[]{:S(2)}, u32[]{:S(2)}) collective-permute-start(bf16[64,1280]{1,0:T(8,128)(2,1)S(1)} %get-tuple-element.87), channel_id=1, source_target_pairs={{0,96},{16,112},{32,0},{48,16},{64,32},{80,48},{96,64},{112,80},{1... | collective-permute-start | bytes 491528 | tf_op jit(solution)/shard_map/ppermute | solution.py:554
  132.9 6.4 %collective-permute-start.14 = (bf16[64,1280]{1,0:T(8,128)(2,1)S(1)}, bf16[64,1280]{1,0:T(8,128)(2,1)S(1)}, u32[]{:S(2)}, u32[]{:S(2)}) collective-permute-start(bf16[64,1280]{1,0:T(8,128)(2,1)S(1)} %get-tuple-element.88), channel_id=1, source_target_pairs={{0,64},{16,80},{32,96},{48,112},{64,0},{80,16},{96,32},{112,48},{1... | collective-permute-start | bytes 491528 | tf_op jit(solution)/shard_map/ppermute | solution.py:554
  140.0 6.1 %collective-permute-start.17 = (bf16[64,1024]{1,0:T(8,128)(2,1)S(1)}, bf16[64,1024]{1,0:T(8,128)(2,1)S(1)}, u32[]{:S(2)}, u32[]{:S(2)}) collective-permute-start(bf16[64,1024]{1,0:T(8,128)(2,1)S(1)} %update.2.refs_0_), channel_id=1, source_target_pairs={{0,64},{16,80},{32,96},{48,112},{64,0},{80,16},{96,32},{112,48},{1... | collective-permute-start | bytes 393224 | tf_op jit(solution)/shard_map/ppermute | solution.py:554
  141.7 8.4 %collective-permute-start.16 = (bf16[64,1024]{1,0:T(8,128)(2,1)S(1)}, bf16[64,1024]{1,0:T(8,128)(2,1)S(1)}, u32[]{:S(2)}, u32[]{:S(2)}) collective-permute-start(bf16[64,1024]{1,0:T(8,128)(2,1)S(1)} %update.2.refs_0_), channel_id=1, source_target_pairs={{0,96},{16,112},{32,0},{48,16},{64,32},{80,48},{96,64},{112,80},{1... | collective-permute-start | bytes 393224 | tf_op jit(solution)/shard_map/ppermute | solution.py:554
  144.1 7.3 %collective-permute-start.15 = (bf16[64,1024]{1,0:T(8,128)(2,1)S(1)}, bf16[64,1024]{1,0:T(8,128)(2,1)S(1)}, u32[]{:S(2)}, u32[]{:S(2)}) collective-permute-start(bf16[64,1024]{1,0:T(8,128)(2,1)S(1)} %update.2.refs_0_), channel_id=1, source_target_pairs={{0,32},{16,48},{32,64},{48,80},{64,96},{80,112},{96,0},{112,16},{1... | collective-permute-start | bytes 393224 | tf_op jit(solution)/shard_map/ppermute | solution.py:554
  144.1 8.0 %collective-permute-start.18 = (bf16[64,1024]{1,0:T(8,128)(2,1)S(1)}, bf16[64,1024]{1,0:T(8,128)(2,1)S(1)}, u32[]{:S(2)}, u32[]{:S(2)}) collective-permute-start(bf16[64,1024]{1,0:T(8,128)(2,1)S(1)} %update.2.refs_0_), channel_id=1, source_target_pairs={{0,16},{16,0},{32,48},{48,32},{64,80},{80,64},{96,112},{112,96},{1... | collective-permute-start | bytes 393224 | tf_op jit(solution)/shard_map/ppermute | solution.py:558
  146.2 5.9 %collective-permute-start.21 = (bf16[64,1024]{1,0:T(8,128)(2,1)S(1)}, bf16[64,1024]{1,0:T(8,128)(2,1)S(1)}, u32[]{:S(2)}, u32[]{:S(2)}) collective-permute-start(bf16[64,1024]{1,0:T(8,128)(2,1)S(1)} %collective-permute-done.17.refs_3_), channel_id=1, source_target_pairs={{0,16},{16,0},{32,48},{48,32},{64,80},{80,64},{96,112},{112,96},{1... | collective-permute-start | bytes 393224 | tf_op jit(solution)/shard_map/ppermute | solution.py:558
  150.1 2.2 collective-permute-start.20
  151.3 1.7 collective-permute-start.19
  159.6 7.5 %collective-permute-start.22 = (bf16[64,16,128]{2,1,0:T(8,128)(2,1)S(1)}, bf16[64,16,128]{2,1,0:T(8,128)(2,1)S(1)}, u32[]{:S(2)}, u32[]{:S(2)}) collective-permute-start(bf16[64,16,128]{2,1,0:T(8,128)(2,1)S(1)} %get-tuple-element.91), channel_id=1, source_target_pairs={{0,1},{1,2},{2,3},{4,5},{5,6},{6,7},{8,9},{9,10},{10,11},{12,13},{... | collective-permute-start | bytes 786440 | tf_op jit(solution)/shard_map/ppermute | solution.py:550
  161.8 9.1 %collective-permute-start.23 = (bf16[64,16,128]{2,1,0:T(8,128)(2,1)S(1)}, bf16[64,16,128]{2,1,0:T(8,128)(2,1)S(1)}, u32[]{:S(2)}, u32[]{:S(2)}) collective-permute-start(bf16[64,16,128]{2,1,0:T(8,128)(2,1)S(1)} %get-tuple-element.92), channel_id=1, source_target_pairs={{1,0},{2,1},{3,2},{5,4},{6,5},{7,6},{9,8},{10,9},{11,10},{13,12},{... | collective-permute-start | bytes 786440 | tf_op jit(solution)/shard_map/ppermute | solution.py:550
  171.0 10.8 %collective-permute-start.24 = (bf16[12,160,128]{2,1,0:T(8,128)(2,1)S(1)}, bf16[12,160,128]{2,1,0:T(8,128)(2,1)S(1)}, u32[]{:S(2)}, u32[]{:S(2)}) collective-permute-start(bf16[12,160,128]{2,1,0:T(8,128)(2,1)S(1)} %get-tuple-element.93), channel_id=1, source_target_pairs={{0,4},{1,5},{2,6},{3,7},{4,8},{5,9},{6,10},{7,11},{8,12},{9,13},{1... | collective-permute-start | bytes 1474568 | tf_op jit(solution)/shard_map/ppermute | solution.py:550
  172.8 12.9 %collective-permute-start.25 = (bf16[12,160,128]{2,1,0:T(8,128)(2,1)S(1)}, bf16[12,160,128]{2,1,0:T(8,128)(2,1)S(1)}, u32[]{:S(2)}, u32[]{:S(2)}) collective-permute-start(bf16[12,160,128]{2,1,0:T(8,128)(2,1)S(1)} %get-tuple-element.94), channel_id=1, source_target_pairs={{4,0},{5,1},{6,2},{7,3},{8,4},{9,5},{10,6},{11,7},{12,8},{13,9},{1... | collective-permute-start | bytes 1474568 | tf_op jit(solution)/shard_map/ppermute | solution.py:550
  201.8 7.4 %collective-permute-start.28 = (f32[8,128]{1,0:T(8,128)S(1)}, f32[8,128]{1,0:T(8,128)S(1)}, u32[]{:S(2)}, u32[]{:S(2)}) collective-permute-start(f32[8,128]{1,0:T(8,128)S(1)} %get-tuple-element.107.refs_0_), channel_id=1, source_target_pairs={{0,64},{16,80},{32,96},{48,112},{64,0},{80,16},{96,32},{112,48},{1... | collective-permute-start | bytes 12296 | tf_op jit(solution)/shard_map/ppermute | solution.py:554
  202.7 8.3 %collective-permute-start.27 = (f32[8,128]{1,0:T(8,128)S(1)}, f32[8,128]{1,0:T(8,128)S(1)}, u32[]{:S(2)}, u32[]{:S(2)}) collective-permute-start(f32[8,128]{1,0:T(8,128)S(1)} %get-tuple-element.107.refs_0_), channel_id=1, source_target_pairs={{0,96},{16,112},{32,0},{48,16},{64,32},{80,48},{96,64},{112,80},{1... | collective-permute-start | bytes 12296 | tf_op jit(solution)/shard_map/ppermute | solution.py:554
  204.8 6.2 %collective-permute-start.26 = (f32[8,128]{1,0:T(8,128)S(1)}, f32[8,128]{1,0:T(8,128)S(1)}, u32[]{:S(2)}, u32[]{:S(2)}) collective-permute-start(f32[8,128]{1,0:T(8,128)S(1)} %get-tuple-element.107.refs_0_), channel_id=1, source_target_pairs={{0,32},{16,48},{32,64},{48,80},{64,96},{80,112},{96,0},{112,16},{1... | collective-permute-start | bytes 12296 | tf_op jit(solution)/shard_map/ppermute | solution.py:554
  204.8 9.2 %collective-permute-start.29 = (f32[8,128]{1,0:T(8,128)S(1)}, f32[8,128]{1,0:T(8,128)S(1)}, u32[]{:S(2)}, u32[]{:S(2)}) collective-permute-start(f32[8,128]{1,0:T(8,128)S(1)} %get-tuple-element.107.refs_0_), channel_id=1, source_target_pairs={{0,16},{16,0},{32,48},{48,32},{64,80},{80,64},{96,112},{112,96},{1... | collective-permute-start | bytes 12296 | tf_op jit(solution)/shard_map/ppermute | solution.py:558
  209.2 4.8 %collective-permute-start.32 = (f32[8,128]{1,0:T(8,128)S(1)}, f32[8,128]{1,0:T(8,128)S(1)}, u32[]{:S(2)}, u32[]{:S(2)}) collective-permute-start(f32[8,128]{1,0:T(8,128)S(1)} %collective-permute-done.28.refs_3_), channel_id=1, source_target_pairs={{0,16},{16,0},{32,48},{48,32},{64,80},{80,64},{96,112},{112,96},{1... | collective-permute-start | bytes 12296 | tf_op jit(solution)/shard_map/ppermute | solution.py:558
  211.0 3.0 %collective-permute-start.31 = (f32[8,128]{1,0:T(8,128)S(1)}, f32[8,128]{1,0:T(8,128)S(1)}, u32[]{:S(2)}, u32[]{:S(2)}) collective-permute-start(f32[8,128]{1,0:T(8,128)S(1)} %collective-permute-done.27.refs_2_), channel_id=1, source_target_pairs={{0,16},{16,0},{32,48},{48,32},{64,80},{80,64},{96,112},{112,96},{1... | collective-permute-start | bytes 12296 | tf_op jit(solution)/shard_map/ppermute | solution.py:558
  211.0 3.9 %collective-permute-start.30 = (f32[8,128]{1,0:T(8,128)S(1)}, f32[8,128]{1,0:T(8,128)S(1)}, u32[]{:S(2)}, u32[]{:S(2)}) collective-permute-start(f32[8,128]{1,0:T(8,128)S(1)} %collective-permute-done.26.refs_1_), channel_id=1, source_target_pairs={{0,16},{16,0},{32,48},{48,32},{64,80},{80,64},{96,112},{112,96},{1... | collective-permute-start | bytes 12296 | tf_op jit(solution)/shard_map/ppermute | solution.py:558
  216.2 10.5 %all-to-all-start.4 = ((bf16[16,48,128]{2,1,0:T(8,128)(2,1)}), bf16[16,48,128]{2,1,0:T(8,128)(2,1)S(1)}, u32[]{:S(2)}, u32[]{:S(2)}) async-start(bf16[16,48,128]{2,1,0:T(8,128)(2,1)} %copy-done.5), calls=%async_computation.4 | async-start | bytes 393216 | tf_op jit(solution)/shard_map/all_to_all | solution.py:540
  226.7 37.7 %all-to-all-start.5 = ((bf16[16,32,8,256]{3,2,1,0:T(8,128)(2,1)}), bf16[16,32,8,256]{3,2,1,0:T(8,128)(2,1)}, u32[]{:S(2)}, u32[]{:S(2)}) async-start(bf16[16,32,8,256]{3,2,1,0:T(8,128)(2,1)} %turn.1), calls=%async_computation.5 | async-start | bytes 4194304 | tf_op jit(solution)/shard_map/all_to_all | solution.py:540
  236.9 4.4 %collective-permute-start.33 = (f32[4,64,1152]{2,1,0:T(8,128)S(1)}, f32[4,64,1152]{2,1,0:T(8,128)S(1)}, u32[]{:S(2)}, u32[]{:S(2)}) collective-permute-start(f32[4,64,1152]{2,1,0:T(8,128)S(1)} %get-tuple-element.115), channel_id=1, source_target_pairs={{0,16},{16,0},{32,48},{48,32},{64,80},{80,64},{96,112},{112,96},{1... | collective-permute-start | bytes 3538952 | tf_op jit(solution)/shard_map/ppermute | solution.py:558
  241.9 6.8 %collective-permute-start.34 = (bf16[64,1280]{1,0:T(8,128)(2,1)S(1)}, bf16[64,1280]{1,0:T(8,128)(2,1)S(1)}, u32[]{:S(2)}, u32[]{:S(2)}) collective-permute-start(bf16[64,1280]{1,0:T(8,128)(2,1)S(1)} %get-tuple-element.117), channel_id=1, source_target_pairs={{0,32},{16,48},{32,64},{48,80},{64,96},{80,112},{96,0},{112,16},{1... | collective-permute-start | bytes 491528 | tf_op jit(solution)/shard_map/ppermute | solution.py:554
  242.0 6.7 %collective-permute-start.35 = (bf16[64,1280]{1,0:T(8,128)(2,1)S(1)}, bf16[64,1280]{1,0:T(8,128)(2,1)S(1)}, u32[]{:S(2)}, u32[]{:S(2)}) collective-permute-start(bf16[64,1280]{1,0:T(8,128)(2,1)S(1)} %get-tuple-element.118), channel_id=1, source_target_pairs={{0,96},{16,112},{32,0},{48,16},{64,32},{80,48},{96,64},{112,80},{1... | collective-permute-start | bytes 491528 | tf_op jit(solution)/shard_map/ppermute | solution.py:554
  244.7 6.5 %collective-permute-start.36 = (bf16[64,1280]{1,0:T(8,128)(2,1)S(1)}, bf16[64,1280]{1,0:T(8,128)(2,1)S(1)}, u32[]{:S(2)}, u32[]{:S(2)}) collective-permute-start(bf16[64,1280]{1,0:T(8,128)(2,1)S(1)} %get-tuple-element.119), channel_id=1, source_target_pairs={{0,64},{16,80},{32,96},{48,112},{64,0},{80,16},{96,32},{112,48},{1... | collective-permute-start | bytes 491528 | tf_op jit(solution)/shard_map/ppermute | solution.py:554
  251.9 6.0 %collective-permute-start.39 = (bf16[64,1024]{1,0:T(8,128)(2,1)S(1)}, bf16[64,1024]{1,0:T(8,128)(2,1)S(1)}, u32[]{:S(2)}, u32[]{:S(2)}) collective-permute-start(bf16[64,1024]{1,0:T(8,128)(2,1)S(1)} %update.3.refs_0_), channel_id=1, source_target_pairs={{0,64},{16,80},{32,96},{48,112},{64,0},{80,16},{96,32},{112,48},{1... | collective-permute-start | bytes 393224 | tf_op jit(solution)/shard_map/ppermute | solution.py:554
  253.4 8.3 %collective-permute-start.38 = (bf16[64,1024]{1,0:T(8,128)(2,1)S(1)}, bf16[64,1024]{1,0:T(8,128)(2,1)S(1)}, u32[]{:S(2)}, u32[]{:S(2)}) collective-permute-start(bf16[64,1024]{1,0:T(8,128)(2,1)S(1)} %update.3.refs_0_), channel_id=1, source_target_pairs={{0,96},{16,112},{32,0},{48,16},{64,32},{80,48},{96,64},{112,80},{1... | collective-permute-start | bytes 393224 | tf_op jit(solution)/shard_map/ppermute | solution.py:554
  255.9 7.3 %collective-permute-start.37 = (bf16[64,1024]{1,0:T(8,128)(2,1)S(1)}, bf16[64,1024]{1,0:T(8,128)(2,1)S(1)}, u32[]{:S(2)}, u32[]{:S(2)}) collective-permute-start(bf16[64,1024]{1,0:T(8,128)(2,1)S(1)} %update.3.refs_0_), channel_id=1, source_target_pairs={{0,32},{16,48},{32,64},{48,80},{64,96},{80,112},{96,0},{112,16},{1... | collective-permute-start | bytes 393224 | tf_op jit(solution)/shard_map/ppermute | solution.py:554
  256.0 14.6 %collective-permute-start.40 = (bf16[64,1024]{1,0:T(8,128)(2,1)S(1)}, bf16[64,1024]{1,0:T(8,128)(2,1)S(1)}, u32[]{:S(2)}, u32[]{:S(2)}) collective-permute-start(bf16[64,1024]{1,0:T(8,128)(2,1)S(1)} %update.3.refs_0_), channel_id=1, source_target_pairs={{0,16},{16,0},{32,48},{48,32},{64,80},{80,64},{96,112},{112,96},{1... | collective-permute-start | bytes 393224 | tf_op jit(solution)/shard_map/ppermute | solution.py:558
  257.9 12.6 %collective-permute-start.43 = (bf16[64,1024]{1,0:T(8,128)(2,1)S(1)}, bf16[64,1024]{1,0:T(8,128)(2,1)S(1)}, u32[]{:S(2)}, u32[]{:S(2)}) collective-permute-start(bf16[64,1024]{1,0:T(8,128)(2,1)S(1)} %collective-permute-done.39.refs_3_), channel_id=1, source_target_pairs={{0,16},{16,0},{32,48},{48,32},{64,80},{80,64},{96,112},{112,96},{1... | collective-permute-start | bytes 393224 | tf_op jit(solution)/shard_map/ppermute | solution.py:558
  261.8 8.8 %collective-permute-start.42 = (bf16[64,1024]{1,0:T(8,128)(2,1)S(1)}, bf16[64,1024]{1,0:T(8,128)(2,1)S(1)}, u32[]{:S(2)}, u32[]{:S(2)}) collective-permute-start(bf16[64,1024]{1,0:T(8,128)(2,1)S(1)} %collective-permute-done.38.refs_2_), channel_id=1, source_target_pairs={{0,16},{16,0},{32,48},{48,32},{64,80},{80,64},{96,112},{112,96},{1... | collective-permute-start | bytes 393224 | tf_op jit(solution)/shard_map/ppermute | solution.py:558
  263.2 7.3 %collective-permute-start.41 = (bf16[64,1024]{1,0:T(8,128)(2,1)S(1)}, bf16[64,1024]{1,0:T(8,128)(2,1)S(1)}, u32[]{:S(2)}, u32[]{:S(2)}) collective-permute-start(bf16[64,1024]{1,0:T(8,128)(2,1)S(1)} %collective-permute-done.37.refs_1_), channel_id=1, source_target_pairs={{0,16},{16,0},{32,48},{48,32},{64,80},{80,64},{96,112},{112,96},{1... | collective-permute-start | bytes 393224 | tf_op jit(solution)/shard_map/ppermute | solution.py:558
  (15 other events, 170.1 us)
